TPU v7x, 32 devices: a whole 2x2x4 slice. The times are simulated.
32 devices in a mesh: depth: 4 (over z), lat: 8 (over y, x, core).
Axes of the slice: x: 2, y: 2, z: 4, core: 2. Of those that a mesh axis runs over, the one named last changes fastest.
Arguments:
- down_real: float32 [16, 256, 256], P('depth', 'lat'), may hold values from -6 to 6
- down_imaginary: float32 [16, 256, 256], P('depth', 'lat'), may hold values from -6 to 6
- up_real: float32 [16, 256, 256], P('depth', 'lat'), may hold values from -6 to 6
- up_imaginary: float32 [16, 256, 256], P('depth', 'lat'), may hold values from -6 to 6
- slowness: float32 [16, 256, 256], P('depth', 'lat'), may hold values from 0.7 to 1.4
- ref_slow: float32 [16], P('depth'), may hold values from 0.8 to 1.2
- reflectivity: float32 [16, 256, 256], P('depth', 'lat'), may hold values from -0.3 to 0.3
- source_real: float32 [256, 256], P('lat'), may hold values from -6 to 6
- source_imaginary: float32 [256, 256], P('lat'), may hold values from -6 to 6
Outputs:
- next_down_real: float32 [16, 256, 256], P('depth', 'lat')
- next_down_imaginary: float32 [16, 256, 256], P('depth', 'lat')
- next_up_real: float32 [16, 256, 256], P('depth', 'lat')
- next_up_imaginary: float32 [16, 256, 256], P('depth', 'lat')
All inputs are finite; a program needn't handle non-finite values.
Results may differ from a plain program's by a relative error of at most 0.0003.
Values sent between devices are 32-bit elements; how exact they have to be, the bound alone decides.
No kernel may reach another device: no remote copies, remote signals or barrier semaphores. Data moves between devices by JAX's collectives and lax.ppermute only.
A program may use at most 64 MiB of HBM per device.

v0:
```python
import math

import jax
import jax.numpy as jnp
import numpy as np
from jax import lax
from jax.experimental import pallas as pl
from jax.experimental.pallas import tpu as pltpu
from jax.sharding import PartitionSpec as P


TICKS = 3

OMEGA = 2.5
DEPTH_STEP = 1.0


def passed_along(value, axis, steps):
    count = lax.axis_size(axis)
    initial, last = (max(0, -steps), min(count, count - steps))
    return lax.ppermute(value, axis, [(source, source + steps) for source in range(initial, last)])


def tables(count):
    index = jnp.arange(count, dtype=jnp.int32)
    phase = index[:, None] * index[None, :] % count
    angle = phase.astype(jnp.float32) * (2.0 * math.pi / count)
    return (jnp.cos(angle), jnp.sin(angle))


def wrapped_numbers(index, count):
    folded = jnp.where(index < count // 2, index, index - count)
    return folded.astype(jnp.float32) * (2.0 * math.pi / count)


def complex_product(form, real, imag, cosine, sine, inverse):
    real_cos = jnp.einsum(form, real, cosine, precision=lax.Precision.HIGHEST)
    real_sin = jnp.einsum(form, real, sine, precision=lax.Precision.HIGHEST)
    imag_cos = jnp.einsum(form, imag, cosine, precision=lax.Precision.HIGHEST)
    imag_sin = jnp.einsum(form, imag, sine, precision=lax.Precision.HIGHEST)
    if inverse:
        return (real_cos - imag_sin, imag_cos + real_sin)
    return (real_cos + imag_sin, imag_cos - real_sin)


def spectral(real, imag, mult_real, mult_imag, corr_real, corr_imag, all_tables, lat_count):
    cos_y, sin_y, cos_x, sin_x = all_tables
    planes = real.shape[0]
    rows_here = real.shape[1]
    width_y = real.shape[2]
    width_x = rows_here * lat_count
    cols_here = width_y // lat_count
    first_real, first_imag = complex_product("nxy,yk->xkn", real, imag, cos_y, sin_y, False)
    send_real = jnp.swapaxes(
        first_real.reshape(rows_here, lat_count, cols_here, planes), 0, 1
    ).reshape(lat_count, rows_here * cols_here * planes)
    send_imag = jnp.swapaxes(
        first_imag.reshape(rows_here, lat_count, cols_here, planes), 0, 1
    ).reshape(lat_count, rows_here * cols_here * planes)
    got_real, got_imag = (
        lax.all_to_all(send_real, "lat", split_axis=0, concat_axis=0, tiled=True),
        lax.all_to_all(send_imag, "lat", split_axis=0, concat_axis=0, tiled=True),
    )
    got_real = got_real.reshape(width_x, cols_here, planes)
    got_imag = got_imag.reshape(width_x, cols_here, planes)
    spec_real, spec_imag = complex_product("xqn,xp->nqp", got_real, got_imag, cos_x, sin_x, False)
    moved_real = spec_real * mult_real - spec_imag * mult_imag
    moved_imag = spec_real * mult_imag + spec_imag * mult_real
    back_real, back_imag = complex_product(
        "nqp,px->qxn", moved_real, moved_imag, cos_x, sin_x, True
    )
    back_real = jnp.swapaxes(
        (back_real / width_x).reshape(cols_here, lat_count, rows_here, planes), 0, 1
    ).reshape(lat_count, cols_here * rows_here * planes)
    back_imag = jnp.swapaxes(
        (back_imag / width_x).reshape(cols_here, lat_count, rows_here, planes), 0, 1
    ).reshape(lat_count, cols_here * rows_here * planes)
    ret_real, ret_imag = (
        lax.all_to_all(back_real, "lat", split_axis=0, concat_axis=0, tiled=True),
        lax.all_to_all(back_imag, "lat", split_axis=0, concat_axis=0, tiled=True),
    )
    ret_real = ret_real.reshape(width_y, rows_here, planes)
    ret_imag = ret_imag.reshape(width_y, rows_here, planes)
    plane_real, plane_imag = complex_product("kxn,ky->nxy", ret_real, ret_imag, cos_y, sin_y, True)
    plane_real = plane_real / width_y
    plane_imag = plane_imag / width_y
    final_real = plane_real * corr_real - plane_imag * corr_imag
    final_imag = plane_real * corr_imag + plane_imag * corr_real
    return (final_real, final_imag)


def media_factors(slow_planes, slow_refs, lat_count, lat_index):
    rows_here = slow_planes.shape[1]
    width_y = slow_planes.shape[2]
    width_x = rows_here * lat_count
    cols_here = width_y // lat_count
    wave_x = wrapped_numbers(jnp.arange(width_x, dtype=jnp.int32), width_x)
    wave_y = wrapped_numbers(
        lat_index * cols_here + jnp.arange(cols_here, dtype=jnp.int32), width_y
    )
    squared = wave_y[:, None] ** 2 + wave_x[None, :] ** 2
    argument = (OMEGA * slow_refs[:, None, None]) ** 2 - squared[None]
    vertical = jnp.sqrt(jnp.maximum(argument, 0.0)) * DEPTH_STEP
    evanescent = jnp.sqrt(jnp.maximum(-argument, 0.0)) * DEPTH_STEP
    factor = jnp.exp(-evanescent)
    theta = OMEGA * (slow_planes - slow_refs[:, None, None]) * DEPTH_STEP
    return (
        factor * jnp.cos(vertical),
        -factor * jnp.sin(vertical),
        jnp.cos(theta),
        -jnp.sin(theta),
    )


def row_shards(
    down_real,
    down_imaginary,
    up_real,
    up_imaginary,
    slowness,
    ref_slow,
    reflectivity,
    source_real,
    source_imaginary,
):
    levels = down_real.shape[0]
    lat_count = lax.axis_size("lat")
    lat_index = lax.axis_index("lat")
    top_mask = (lax.axis_index("depth") == 0).astype(jnp.float32)
    width_x = down_real.shape[1] * lat_count
    cos_y, sin_y = tables(down_real.shape[2])
    cos_x, sin_x = tables(width_x)
    all_tables = (cos_y, sin_y, cos_x, sin_x)
    slow_planes = jnp.concatenate([slowness, slowness], axis=0)
    slow_refs = jnp.concatenate([ref_slow, ref_slow], axis=0)
    mult_real, mult_imag, corr_real, corr_imag = media_factors(
        slow_planes, slow_refs, lat_count, lat_index
    )
    for _ in range(TICKS):
        joined_real = jnp.concatenate([down_real, up_real], axis=0)
        joined_imag = jnp.concatenate([down_imaginary, up_imaginary], axis=0)
        prop_real, prop_imag = spectral(
            joined_real,
            joined_imag,
            mult_real,
            mult_imag,
            corr_real,
            corr_imag,
            all_tables,
            lat_count,
        )
        above_real, above_imag = passed_along(
            (prop_real[levels - 1], prop_imag[levels - 1]), "depth", 1
        )
        below_real, below_imag = passed_along((prop_real[levels], prop_imag[levels]), "depth", -1)
        head_real = above_real + top_mask * source_real
        head_imag = above_imag + top_mask * source_imaginary
        in_down_real = jnp.concatenate([head_real[None], prop_real[: levels - 1]], axis=0)
        in_down_imag = jnp.concatenate([head_imag[None], prop_imag[: levels - 1]], axis=0)
        in_up_real = jnp.concatenate([prop_real[levels + 1 :], below_real[None]], axis=0)
        in_up_imag = jnp.concatenate([prop_imag[levels + 1 :], below_imag[None]], axis=0)
        down_real = in_down_real - reflectivity * in_up_real
        down_imaginary = in_down_imag - reflectivity * in_up_imag
        up_real = in_up_real + reflectivity * in_down_real
        up_imaginary = in_up_imag + reflectivity * in_down_imag
    return (down_real, down_imaginary, up_real, up_imaginary)


def path_at(section, place, pairs):
    place = place if section % 2 == 0 else pairs - 1 - place
    return place ^ (place >> 1)


def place_on(section, pair, pairs):
    shift, place = 1, pair
    while (1 << shift) <= pairs:
        place = place ^ (pair >> shift)
        shift += 1
    return jnp.where(section % 2 == 0, place, pairs - 1 - place)


def level_pairs(sections, pairs, parity):
    where = [
        g * pairs * 2 + path_at(g, l, pairs) * 2 for g in range(sections) for l in range(pairs)
    ]
    edges = []
    for z in range(parity, len(where) - 1, 2):
        for core in range(2):
            here, below = where[z] + core, where[z + 1] + core
            edges += [(here, below), (below, here)]
    return edges


def section_pairs(sections, pairs, parity):
    width = 2 * pairs
    edges = []
    for g in range(parity, sections - 1, 2):
        for n in range(width):
            edges += [(g * width + n, (g + 1) * width + n), ((g + 1) * width + n, g * width + n)]
    return edges


def transform_tables(count, order, transposed):
    index = np.arange(count)
    angle = (index[:, None] * np.asarray(order)[None, :] % count) * (2.0 * math.pi / count)
    if transposed:
        angle = angle.T
    parts = []
    for table in (np.cos(angle), np.sin(angle)):
        high = table.astype(np.float32).astype(jnp.bfloat16)
        parts += [high, (table - high.astype(np.float64)).astype(np.float32).astype(jnp.bfloat16)]
    return parts


def halves(value):
    high = value.astype(jnp.bfloat16)
    low = (value - high.astype(jnp.float32)).astype(jnp.bfloat16)
    return high, low


def cos_sin(angle):
    square = angle * angle
    sine = 1.0
    for n in (13, 11, 9, 7, 5, 3):
        scale = -1.0 / (n * (n - 1))
        sine = 1.0 + square * (scale * sine)
    cosine = 1.0
    for n in (14, 12, 10, 8, 6, 4, 2):
        scale = -1.0 / (n * (n - 1))
        cosine = 1.0 + square * (scale * cosine)
    return cosine, angle * sine


def multiplier(ref, rows, columns, first, here_columns):
    def wave(count, axis, start):
        index = lax.broadcasted_iota(jnp.int32, (rows, here_columns), axis) + start
        folded = jnp.where(index < count // 2, index, index - count)
        return folded.astype(jnp.float32) * (2.0 * math.pi / count)

    wave_x, wave_y = wave(rows, 0, 0), wave(columns, 1, first)
    argument = (OMEGA * ref) ** 2 - (wave_x * wave_x + wave_y * wave_y)
    vertical = jnp.sqrt(jnp.maximum(argument, 0.0)) * DEPTH_STEP
    evanescent = jnp.sqrt(jnp.maximum(-argument, 0.0)) * DEPTH_STEP
    factor = jnp.exp(-evanescent) * (1.0 / (rows * columns))
    cosine, sine = cos_sin(0.5 * vertical)
    return factor * (1.0 - 2.0 * sine * sine), factor * (-2.0 * sine * cosine)


def terms(a, b, inverse):
    a_high, a_low = halves(a)
    b_high, b_low = halves(b)
    if inverse:
        real = [a_high, a_low, a_high, -b_high, -b_low, -b_high]
        imag = [b_high, b_low, b_high, a_high, a_low, a_high]
    else:
        real = [a_high, a_low, a_high, b_high, b_low, b_high]
        imag = [b_high, b_low, b_high, -a_high, -a_low, -a_high]
    return real, imag


def table_of(parts, axis):
    cos_high, cos_low, sin_high, sin_low = (part[...] for part in parts)
    return jnp.concatenate(
        [cos_high, cos_high, cos_low, sin_high, sin_high, sin_low], axis=axis
    )


def along_y(a, b, parts, inverse):
    count = a.shape[0]
    real, imag = (jnp.concatenate(t, axis=1) for t in terms(a, b, inverse))
    out = jnp.dot(
        jnp.concatenate([real, imag], axis=0),
        table_of(parts, 0),
        preferred_element_type=jnp.float32,
    )
    return out[:count], out[count:]


def along_x(a, b, parts, inverse):
    count = a.shape[1]
    real, imag = (jnp.concatenate(t, axis=0) for t in terms(a, b, inverse))
    out = jnp.dot(
        table_of(parts, 1),
        jnp.concatenate([real, imag], axis=1),
        preferred_element_type=jnp.float32,
    )
    return out[:, :count], out[:, count:]


class Place:
    def __init__(self, pairs):
        index = lax.axis_index("lat")
        self.section = lax.axis_index("depth")
        self.pair = index // 2
        self.core = index % 2
        self.level = place_on(self.section, self.pair, pairs)
        self.first = self.level == 0
        self.last = self.level == pairs - 1


def local_call(body, out_shapes, spaces, scratch=(), limit=24 << 20):
    memory = {"v": pltpu.VMEM, "s": pltpu.SMEM, "h": pltpu.HBM}
    return pl.pallas_call(
        body,
        out_shape=[jax.ShapeDtypeStruct(shape, jnp.float32) for shape in out_shapes],
        in_specs=[pl.BlockSpec(memory_space=memory[space]) for space in spaces],
        out_specs=[pl.BlockSpec(memory_space=pltpu.VMEM) for _ in out_shapes],
        scratch_shapes=list(scratch),
        compiler_params=pltpu.CompilerParams(vmem_limit_bytes=limit),
    )


def plane_shards(
    down_real,
    down_imaginary,
    up_real,
    up_imaginary,
    slowness,
    ref_slow,
    reflectivity,
    source_real,
    source_imaginary,
):
    levels, block, columns = down_real.shape
    sections = lax.axis_size("depth")
    lat_count = lax.axis_size("lat")
    pairs = lat_count // 2
    rows = block * lat_count
    tall = rows // 2
    wide = columns // 2
    two, four = 2 * block, 4 * block
    swap = [(index, index ^ 1) for index in range(lat_count)]
    place = np.arange(rows)
    order = place % tall // block * two + place // tall * block + place % block
    y_tables = [jnp.asarray(t) for t in transform_tables(columns, np.arange(columns), False)]
    x_tables = [jnp.asarray(t) for t in transform_tables(rows, order, False)]
    back_tables = [jnp.asarray(t) for t in transform_tables(rows, order, True)]
    f32 = jnp.float32
    local = (2 * tall, columns)
    part = (2 * tall, wide)

    def across(step):
        return [(index, index ^ (2 * step)) for index in range(lat_count)]

    def top(here):
        return here.first & (here.section == 0)

    def split_body(dr, di, ur, ui, slow, refl, sr, si, *rest):
        planes, media, sems = rest[:pairs], rest[pairs : 2 * pairs], rest[2 * pairs]
        here = Place(pairs)

        def pieces(step, first, second):
            level = place_on(here.section, here.pair ^ step, pairs)
            out = []
            for n, array in enumerate(first + second):
                source = array if len(array.shape) == 2 else array.at[level]
                out.append((source, planes[step].at[pl.ds(n * block, block), :]))
            out.append((slow.at[level], media[step].at[pl.ds(0, block), :]))
            out.append((refl.at[level], media[step].at[pl.ds(block, block), :]))
            return [
                pltpu.make_async_copy(source, target, sems.at[step * 6 + n])
                for n, (source, target) in enumerate(out)
            ]

        def each(act):
            for step in range(pairs):
                level = place_on(here.section, here.pair ^ step, pairs)
                sourced = (level == 0) & (here.section == 0)

                @pl.when(sourced)
                def _():
                    for move in pieces(step, (dr, di), (sr, si)):
                        act(move)

                @pl.when((level % 2 == 0) & jnp.logical_not(sourced))
                def _():
                    for move in pieces(step, (dr, di), (ur, ui)):
                        act(move)

                @pl.when(level % 2 == 1)
                def _():
                    for move in pieces(step, (ur, ui), (dr, di)):
                        act(move)

        each(lambda move: move.start())
        each(lambda move: move.wait())

    outs = local_call(
        split_body,
        [(four, columns)] * pairs + [(two, columns)] * pairs,
        "h" * 8,
        [pltpu.SemaphoreType.DMA((6 * pairs,))],
    )(
        *(
            pltpu.with_memory_space_constraint(array, pltpu.HBM)
            for array in (
                down_real,
                down_imaginary,
                up_real,
                up_imaginary,
                slowness,
                reflectivity,
                source_real,
                source_imaginary,
            )
        )
    )

    def exchanged(pieces):
        moved = [pieces[0]]
        for step in range(1, pairs):
            moved.append(lax.ppermute(pieces[step], "lat", across(step)))
        return moved

    planes = exchanged(outs[:pairs])
    media = exchanged(outs[pairs:])

    def multiplier_body(ref_slow, out):
        here = Place(pairs)
        real, imag = multiplier(ref_slow[here.level], rows, columns, here.core * wide, wide)
        out[:rows] = real
        out[rows:] = imag

    mult = local_call(multiplier_body, [(2 * rows, wide)], "s")(ref_slow)[0]

    def media_body(*refs):
        pieces, ref_slow, corr, refl = refs[:pairs], refs[pairs], refs[pairs + 1], refs[pairs + 2]
        here = Place(pairs)
        ref = ref_slow[here.level]
        for step in range(pairs):
            start = (here.pair ^ step) * block
            theta = (pieces[step][pl.ds(0, block), :] - ref) * (OMEGA * DEPTH_STEP)
            cosine, sine = cos_sin(theta)
            corr[pl.ds(pl.multiple_of(start, block), block), :] = cosine
            corr[pl.ds(pl.multiple_of(tall + start, block), block), :] = sine
            refl[pl.ds(pl.multiple_of(start, block), block), :] = pieces[step][
                pl.ds(block, block), :
            ]

    corr, refl = local_call(media_body, [local, (tall, columns)], "v" * pairs + "s")(
        *media, ref_slow
    )

    def halved(real, imag, here, axis, keep, send):
        def put(mine, theirs):
            keep[:tall], keep[tall:] = mine
            send[:tall], send[tall:] = theirs

        if axis == 0:
            cuts = [(real[:tall], imag[:tall]), (real[tall:], imag[tall:])]
        else:
            cuts = [(real[:, :wide], imag[:, :wide]), (real[:, wide:], imag[:, wide:])]

        @pl.when(here.core == 0)
        def _():
            put(cuts[0], cuts[1])

        @pl.when(here.core == 1)
        def _():
            put(cuts[1], cuts[0])

    def enter(which):
        def body(*refs):
            pieces, tabs, keep, send = refs[:pairs], refs[pairs : pairs + 4], *refs[pairs + 4 : -1]
            whole = refs[-1]
            here = Place(pairs)
            for step in range(pairs):
                start = (here.pair ^ step) * block
                for n in range(2):
                    whole[pl.ds(pl.multiple_of(n * tall + start, block), block), :] = pieces[step][
                        pl.ds((2 * which + n) * block, block), :
                    ]
            halved(*along_y(whole[:tall], whole[tall:], tabs, False), here, 1, keep, send)

        return local_call(body, [part, part, local], "v" * (pairs + 4))(
            *planes, *y_tables
        )

    def mixed(which, ahead, behind, source):
        def body(ahead, behind, source, refl, *refs):
            tabs, keep, send = refs[:4], refs[4], refs[5]
            here = Place(pairs)
            sign = jnp.where((here.level % 2 == 0) == (which == 0), -1.0, 1.0)
            behind = jnp.where(top(here), source[...], behind[...])
            base, side = (behind, ahead[...]) if which == 0 else (ahead[...], behind)
            weight = refl[...] * sign
            real = base[:tall] + weight * side[:tall]
            imag = base[tall:] + weight * side[tall:]
            halved(*along_y(real, imag, tabs, False), here, 1, keep, send)

        return local_call(body, [part, part], "v" * 8)(ahead, behind, source, refl, *y_tables)

    def column(keep, got):
        def body(keep, got, mult, *refs):
            tabs, back, out, send, real, imag = refs[:4], refs[4:8], *refs[8:]
            here = Place(pairs)
            for piece, core in ((keep, here.core), (got, 1 - here.core)):
                take = pl.ds(pl.multiple_of(core * tall, tall), tall)
                real[take, :] = piece[:tall]
                imag[take, :] = piece[tall:]
            a, b = along_x(real[...], imag[...], tabs, False)
            mult_real, mult_imag = mult[:rows], mult[rows:]
            a, b = a * mult_real - b * mult_imag, a * mult_imag + b * mult_real
            halved(*along_x(a, b, back, True), here, 0, out, send)

        return local_call(
            body, [part, part], "v" * 11, [pltpu.VMEM((rows, wide), f32) for _ in range(2)]
        )(keep, got, mult, *x_tables, *back_tables)

    def corrected(keep, got, corr, tabs, here, whole):
        for piece, core in ((keep, here.core), (got, 1 - here.core)):
            whole[:, pl.ds(pl.multiple_of(core * wide, wide), wide)] = piece[...]
        real, imag = along_y(whole[:tall], whole[tall:], tabs, True)
        cosine, sine = corr[:tall], corr[tall:]
        return real * cosine + imag * sine, imag * cosine - real * sine

    def leave(keep, got, *held):
        def body(keep, got, corr, *refs):
            kept, tabs, outs = refs[: len(held)], refs[len(held) : len(held) + 4], refs[4 + len(held) :]
            whole = outs[-1]
            for source, target in zip(kept, outs[1:]):
                target[...] = source[...]
            real, imag = corrected(keep, got, corr, tabs, Place(pairs), whole)
            outs[0][:tall], outs[0][tall:] = real, imag

        return local_call(
            body, [local] * (1 + len(held)), "v" * (7 + len(held)), [pltpu.VMEM(local, f32)]
        )(keep, got, corr, *held, *y_tables)

    def leave_last(keep, got):
        def body(keep, got, corr, *refs):
            tabs, outs, whole = refs[:4], refs[4 : 4 + pairs], refs[4 + pairs]
            here = Place(pairs)
            real, imag = corrected(keep, got, corr, tabs, here, whole)
            whole[:tall], whole[tall:] = real, imag
            for step in range(pairs):
                start = (here.pair ^ step) * block
                for m in range(2):
                    outs[step][pl.ds(m * block, block), :] = whole[
                        pl.ds(pl.multiple_of(m * tall + start, block), block), :
                    ]

        return local_call(
            body, [(two, columns)] * pairs, "v" * 7, [pltpu.VMEM(local, f32)]
        )(keep, got, corr, *y_tables)

    def crossed(value):
        return lax.ppermute(value, "lat", swap)

    keep0, send0, _ = enter(0)
    got0 = crossed(send0)
    keep1, send1, source = enter(1)
    got1 = crossed(send1)
    for _ in range(TICKS - 1):
        keep0, send0 = column(keep0, got0)
        got0 = crossed(send0)
        keep1, send1 = column(keep1, got1)
        got1 = crossed(send1)
        first = leave(keep0, got0)[0]
        second, first = leave(keep1, got1, first)
        ahead = lax.ppermute(first, ("depth", "lat"), level_pairs(sections, pairs, 0))
        behind = lax.ppermute(second, ("depth", "lat"), level_pairs(sections, pairs, 1))
        keep1, send1 = mixed(1, ahead, behind, source)
        got1 = crossed(send1)
        keep0, send0 = mixed(0, ahead, behind, source)
        got0 = crossed(send0)
    keep1, send1 = column(keep1, got1)
    got1 = crossed(send1)
    keep0, send0 = column(keep0, got0)
    got0 = crossed(send0)
    back1 = exchanged(leave_last(keep1, got1))
    leaving = leave_last(keep0, got0)
    back0 = exchanged(leaving)

    def pick_body(*refs):
        pieces, even, odd = refs[:pairs], refs[pairs], refs[pairs + 1]
        here = Place(pairs)
        for step in range(pairs):
            level = place_on(here.section, here.pair ^ step, pairs)
            for edge, mine in ((pairs - 1, 0), (0, 1)):
                for target, parity in ((even, mine), (odd, 1 - mine)):

                    @pl.when((level == edge) & (here.section % 2 == parity))
                    def _():
                        target[...] = pieces[step][...]

    even, odd = local_call(pick_body, [(two, columns)] * 2, "v" * pairs)(*back1)
    even = lax.ppermute(even, ("depth", "lat"), section_pairs(sections, pairs, 0))
    odd = lax.ppermute(odd, ("depth", "lat"), section_pairs(sections, pairs, 1))

    def mix_body(*refs):
        first, second = refs[:pairs], refs[pairs : 2 * pairs]
        even, odd, refl, sr, si = refs[2 * pairs : 2 * pairs + 5]
        dr, di, ur, ui, down, up = refs[2 * pairs + 5 :]
        here = Place(pairs)
        for step in range(pairs):
            level = place_on(here.section, here.pair ^ step, pairs)
            below, above = (level + 1) % levels, (level + levels - 1) % levels

            @pl.when(level % 2 == 0)
            def _():
                down[below] = first[step][...]
                up[above] = second[step][...]

            @pl.when(level % 2 == 1)
            def _():
                down[below] = second[step][...]
                up[above] = first[step][...]

        @pl.when(here.section % 2 == 0)
        def _():
            down[0] = odd[...]
            up[levels - 1] = even[...]

        @pl.when(here.section % 2 == 1)
        def _():
            down[0] = even[...]
            up[levels - 1] = odd[...]

        @pl.when(here.section == 0)
        def _():
            down[0, pl.ds(0, block), :] = sr[...]
            down[0, pl.ds(block, block), :] = si[...]

        for n in range(levels):
            r = refl[n]
            d_real, d_imag = down[n, pl.ds(0, block), :], down[n, pl.ds(block, block), :]
            u_real, u_imag = up[n, pl.ds(0, block), :], up[n, pl.ds(block, block), :]
            dr[n] = d_real - r * u_real
            di[n] = d_imag - r * u_imag
            ur[n] = u_real + r * d_real
            ui[n] = u_imag + r * d_imag

    return tuple(
        local_call(
            mix_body,
            [(levels, block, columns)] * 4,
            "v" * (2 * pairs + 5),
            [pltpu.VMEM((levels, two, columns), f32) for _ in range(2)],
        )(*back0, *back1, even, odd, reflectivity, source_real, source_imaginary)
    )


def fits(shape, mesh):
    levels, rows, columns = shape
    levels = levels // mesh.shape["depth"]
    return (
        mesh.shape["lat"] == 2 * levels
        and levels >= 2
        and levels & (levels - 1) == 0
        and rows // mesh.shape["lat"] % 8 == 0
        and columns % 256 == 0
    )


def solution(mesh):
    rows = P("depth", "lat", None)
    placed = (rows,) * 5 + (P("depth"), rows, P("lat", None), P("lat", None))

    def mapped(body):
        return jax.shard_map(
            body, mesh=mesh, in_specs=placed, out_specs=(rows,) * 4, check_vma=False
        )

    by_planes = mapped(plane_shards)
    by_rows = mapped(row_shards)

    def run(*arrays):
        return (by_planes if fits(arrays[0].shape, mesh) else by_rows)(*arrays)

    return run
```

profile of v0, /device:TPU:16, one launch (start us, length us, event | category | flops | bytes accessed | tf_op | source)
XLA Modules:
  0.0 75.4 jit_solution(12314376844389332776)
XLA Ops:
  0.7 1.4 %shard_map.228 = (f32[128,256]{1,0:T(8,128)S(1)}, f32[128,256]{1,0:T(8,128)S(1)}, f32[128,256]{1,0:T(8,128)S(1)}, f32[128,256]{1,0:T(8,128)S(1)}, f32[64,256]{1,...) custom-call(f32[4,32,256]{2,1,0:T(8,128)} %dr.1, f32[4,32,256]{2,1,0:T(8,128)} %di.1, ...), custom_call_target="tpu_custom_call" | custom-call | tf_op jit(solution)/shard_map/pallas_call | solution.py:388
  2.1 1.6 %collective-permute-start = (f32[128,256]{1,0:T(8,128)S(1)}, f32[128,256]{1,0:T(8,128)S(1)}, u32[]{:S(2)}, u32[]{:S(2)}) collective-permute-start(f32[128,256]{1,0:T(8,128)S(1)} %get-tuple-element.54), channel_id=1, source_target_pairs={{0,2},{1,3},{2,0},{3,1},{4,6},{5,7},{6,4},{7,5},{8,10},{9,11},{10,... | collective-permute-start | bytes 393224 | tf_op jit(solution)/shard_map/ppermute | solution.py:412
  3.7 1.5 %collective-permute-start.1 = (f32[128,256]{1,0:T(8,128)S(1)}, f32[128,256]{1,0:T(8,128)S(1)}, u32[]{:S(2)}, u32[]{:S(2)}) collective-permute-start(f32[128,256]{1,0:T(8,128)S(1)} %get-tuple-element.55), channel_id=1, source_target_pairs={{0,4},{1,5},{2,6},{3,7},{4,0},{5,1},{6,2},{7,3},{8,12},{9,13},{10,... | collective-permute-start | bytes 393224 | tf_op jit(solution)/shard_map/ppermute | solution.py:412
  5.2 0.5 collective-permute-start.2
  5.7 2.1 %collective-permute-done.refs_1_ = f32[128,256]{1,0:T(8,128)S(1)} collective-permute-done((f32[128,256]{1,0:T(8,128)S(1)}, f32[128,256]{1,0:T(8,128)S(1)}, u32[]{:S(2)}, u32[]{:S(2)}) %collective-permute-start) | collective-permute-done | bytes 131104 | tf_op jit(solution)/shard_map/ppermute | solution.py:412
  7.8 3.6 %collective-permute-done.1.refs_2_ = f32[128,256]{1,0:T(8,128)S(1)} collective-permute-done((f32[128,256]{1,0:T(8,128)S(1)}, f32[128,256]{1,0:T(8,128)S(1)}, u32[]{:S(2)}, u32[]{:S(2)}) %collective-permute-start.1) | collective-permute-done | bytes 131104 | tf_op jit(solution)/shard_map/ppermute | solution.py:412
  11.5 1.1 %shard_map.233 = (f32[256,128]{1,0:T(8,128)S(1)}, f32[256,128]{1,0:T(8,128)S(1)}, f32[256,256]{1,0:T(8,128)}) custom-call(f32[128,256]{1,0:T(8,128)S(1)} %get-tuple-element.53.refs_0_, f32[128,256]{1,0:T(8,128)S(1)} %collective-permute-done.refs_1_, f32[128,256]{1,0:T(8,128)S(1)} %collective-permute-done.1.refs_2_, ...), custom_call_target="tpu_custom_call" | custom-call | tf_op jit(solution)/shard_map/pallas_call | solution.py:475
  13.1 0.6 collective-permute-start.3
  13.7 0.9 %shard_map.230.mult = f32[512,128]{1,0:T(8,128)S(1)} custom-call(f32[4]{0:T(128)S(1)} %copy-done.15), custom_call_target="tpu_custom_call" | custom-call | tf_op jit(solution)/shard_map/pallas_call | solution.py:424
  14.7 1.1 %shard_map.234 = (f32[256,128]{1,0:T(8,128)S(1)}, f32[256,128]{1,0:T(8,128)S(1)}) custom-call(f32[256,128]{1,0:T(8,128)S(1)} %get-tuple-element.66.keep, f32[256,128]{1,0:T(8,128)S(1)} %collective-permute-done.8.got, f32[512,128]{1,0:T(8,128)S(1)} %shard_map.230.mult, bf16[256,256]{1,0:T(8,128)(2,1)S(1)} %copy-done.4, bf16[256,256]{1,0:T(8,128)(2,1)S(1)} %copy-done.5, ...), custom_call_target="tpu_custom_call" | custom-call | tf_op jit(solution)/shard_map/pallas_call | solution.py:506
  15.8 0.6 collective-permute-start.9
  16.4 1.1 %shard_map.231 = (f32[256,128]{1,0:T(8,128)S(1)}, f32[256,128]{1,0:T(8,128)S(1)}) custom-call(f32[256,128]{1,0:T(8,128)S(1)} %get-tuple-element.57.keep, f32[256,128]{1,0:T(8,128)S(1)} %collective-permute-done.3.got, f32[512,128]{1,0:T(8,128)S(1)} %shard_map.230.mult, bf16[256,256]{1,0:T(8,128)(2,1)S(1)} %copy-done.4, bf16[256,256]{1,0:T(8,128)(2,1)S(1)} %copy-done.5, ...), custom_call_target="tpu_custom_call" | custom-call | tf_op jit(solution)/shard_map/pallas_call | solution.py:506
  17.6 1.2 %collective-permute-start.5 = (f32[64,256]{1,0:T(8,128)S(1)}, f32[64,256]{1,0:T(8,128)S(1)}, u32[]{:S(2)}, u32[]{:S(2)}) collective-permute-start(f32[64,256]{1,0:T(8,128)S(1)} %get-tuple-element.62), channel_id=1, source_target_pairs={{0,2},{1,3},{2,0},{3,1},{4,6},{5,7},{6,4},{7,5},{8,10},{9,11},{10,... | collective-permute-start | bytes 196616 | tf_op jit(solution)/shard_map/ppermute | solution.py:412
  18.9 0.8 %collective-permute-start.6 = (f32[64,256]{1,0:T(8,128)S(1)}, f32[64,256]{1,0:T(8,128)S(1)}, u32[]{:S(2)}, u32[]{:S(2)}) collective-permute-start(f32[64,256]{1,0:T(8,128)S(1)} %get-tuple-element.63), channel_id=1, source_target_pairs={{0,4},{1,5},{2,6},{3,7},{4,0},{5,1},{6,2},{7,3},{8,12},{9,13},{10,... | collective-permute-start | bytes 196616 | tf_op jit(solution)/shard_map/ppermute | solution.py:412
  19.7 1.4 %collective-permute-start.7 = (f32[64,256]{1,0:T(8,128)S(1)}, f32[64,256]{1,0:T(8,128)S(1)}, u32[]{:S(2)}, u32[]{:S(2)}) collective-permute-start(f32[64,256]{1,0:T(8,128)S(1)} %get-tuple-element.64), channel_id=1, source_target_pairs={{0,6},{1,7},{2,4},{3,5},{4,2},{5,3},{6,0},{7,1},{8,14},{9,15},{10,... | collective-permute-start | bytes 196616 | tf_op jit(solution)/shard_map/ppermute | solution.py:412
  21.1 0.9 %collective-permute-done.5.refs_1_ = f32[64,256]{1,0:T(8,128)S(1)} collective-permute-done((f32[64,256]{1,0:T(8,128)S(1)}, f32[64,256]{1,0:T(8,128)S(1)}, u32[]{:S(2)}, u32[]{:S(2)}) %collective-permute-start.5) | collective-permute-done | bytes 65568 | tf_op jit(solution)/shard_map/ppermute | solution.py:412
  22.1 1.0 %collective-permute-done.6.refs_2_ = f32[64,256]{1,0:T(8,128)S(1)} collective-permute-done((f32[64,256]{1,0:T(8,128)S(1)}, f32[64,256]{1,0:T(8,128)S(1)}, u32[]{:S(2)}, u32[]{:S(2)}) %collective-permute-start.6) | collective-permute-done | bytes 65568 | tf_op jit(solution)/shard_map/ppermute | solution.py:412
  23.1 1.7 %collective-permute-done.7.refs_3_ = f32[64,256]{1,0:T(8,128)S(1)} collective-permute-done((f32[64,256]{1,0:T(8,128)S(1)}, f32[64,256]{1,0:T(8,128)S(1)}, u32[]{:S(2)}, u32[]{:S(2)}) %collective-permute-start.7) | collective-permute-done | bytes 65568 | tf_op jit(solution)/shard_map/ppermute | solution.py:412
  24.9 0.7 shard_map.232
  26.5 1.5 %collective-permute-start.10 = (f32[256,256]{1,0:T(8,128)S(1)}, f32[256,256]{1,0:T(8,128)S(1)}, u32[]{:S(2)}, u32[]{:S(2)}) collective-permute-start(f32[256,256]{1,0:T(8,128)S(1)} %get-tuple-element.70), channel_id=1, source_target_pairs={{0,2},{2,0},{1,3},{3,1},{6,4},{4,6},{7,5},{5,7},{12,14},{14,12},{1... | collective-permute-start | bytes 786440 | tf_op jit(solution)/shard_map/ppermute | solution.py:561
  28.0 2.4 %collective-permute-start.11 = (f32[256,256]{1,0:T(8,128)S(1)}, f32[256,256]{1,0:T(8,128)S(1)}, u32[]{:S(2)}, u32[]{:S(2)}) collective-permute-start(f32[256,256]{1,0:T(8,128)S(1)} %get-tuple-element.71), channel_id=1, source_target_pairs={{2,6},{6,2},{3,7},{7,3},{4,12},{12,4},{5,13},{13,5},{14,10},{10,14... | collective-permute-start | bytes 786440 | tf_op jit(solution)/shard_map/ppermute | solution.py:562
  30.4 3.1 %collective-permute-done.10.ahead = f32[256,256]{1,0:T(8,128)S(1)} collective-permute-done((f32[256,256]{1,0:T(8,128)S(1)}, f32[256,256]{1,0:T(8,128)S(1)}, u32[]{:S(2)}, u32[]{:S(2)}) %collective-permute-start.10) | collective-permute-done | bytes 262176 | tf_op jit(solution)/shard_map/ppermute | solution.py:561
  33.5 3.0 %collective-permute-done.11.behind = f32[256,256]{1,0:T(8,128)S(1)} collective-permute-done((f32[256,256]{1,0:T(8,128)S(1)}, f32[256,256]{1,0:T(8,128)S(1)}, u32[]{:S(2)}, u32[]{:S(2)}) %collective-permute-start.11) | collective-permute-done | bytes 262176 | tf_op jit(solution)/shard_map/ppermute | solution.py:562
  37.4 0.6 collective-permute-start.12
  38.4 1.1 %shard_map.240 = (f32[256,128]{1,0:T(8,128)S(1)}, f32[256,128]{1,0:T(8,128)S(1)}) custom-call(f32[256,128]{1,0:T(8,128)S(1)} %get-tuple-element.78.keep, f32[256,128]{1,0:T(8,128)S(1)} %collective-permute-done.14.got, f32[512,128]{1,0:T(8,128)S(1)} %shard_map.230.mult, bf16[256,256]{1,0:T(8,128)(2,1)S(1)} %copy-done.4, bf16[256,256]{1,0:T(8,128)(2,1)S(1)} %copy-done.5, ...), custom_call_target="tpu_custom_call" | custom-call | tf_op jit(solution)/shard_map/pallas_call | solution.py:506
  39.7 1.1 %shard_map.238 = (f32[256,128]{1,0:T(8,128)S(1)}, f32[256,128]{1,0:T(8,128)S(1)}) custom-call(f32[256,128]{1,0:T(8,128)S(1)} %get-tuple-element.74.keep, f32[256,128]{1,0:T(8,128)S(1)} %collective-permute-done.12.got, f32[512,128]{1,0:T(8,128)S(1)} %shard_map.230.mult, bf16[256,256]{1,0:T(8,128)(2,1)S(1)} %copy-done.4, bf16[256,256]{1,0:T(8,128)(2,1)S(1)} %copy-done.5, ...), custom_call_target="tpu_custom_call" | custom-call | tf_op jit(solution)/shard_map/pallas_call | solution.py:506
  40.8 0.4 collective-permute-start.13
  41.7 0.6 collective-permute-done.13.got
  42.7 0.7 collective-permute-start.16
  43.3 2.4 %collective-permute-start.17 = (f32[256,256]{1,0:T(8,128)S(1)}, f32[256,256]{1,0:T(8,128)S(1)}, u32[]{:S(2)}, u32[]{:S(2)}) collective-permute-start(f32[256,256]{1,0:T(8,128)S(1)} %get-tuple-element.83), channel_id=1, source_target_pairs={{2,6},{6,2},{3,7},{7,3},{4,12},{12,4},{5,13},{13,5},{14,10},{10,14... | collective-permute-start | bytes 786440 | tf_op jit(solution)/shard_map/ppermute | solution.py:562
  45.7 5.6 %collective-permute-done.16.ahead = f32[256,256]{1,0:T(8,128)S(1)} collective-permute-done((f32[256,256]{1,0:T(8,128)S(1)}, f32[256,256]{1,0:T(8,128)S(1)}, u32[]{:S(2)}, u32[]{:S(2)}) %collective-permute-start.16) | collective-permute-done | bytes 262176 | tf_op jit(solution)/shard_map/ppermute | solution.py:561
  51.3 2.2 %collective-permute-done.17.behind = f32[256,256]{1,0:T(8,128)S(1)} collective-permute-done((f32[256,256]{1,0:T(8,128)S(1)}, f32[256,256]{1,0:T(8,128)S(1)}, u32[]{:S(2)}, u32[]{:S(2)}) %collective-permute-start.17) | collective-permute-done | bytes 262176 | tf_op jit(solution)/shard_map/ppermute | solution.py:562
  54.4 0.6 collective-permute-start.18
  55.3 1.1 %shard_map.247 = (f32[256,128]{1,0:T(8,128)S(1)}, f32[256,128]{1,0:T(8,128)S(1)}) custom-call(f32[256,128]{1,0:T(8,128)S(1)} %get-tuple-element.92.keep, f32[256,128]{1,0:T(8,128)S(1)} %collective-permute-done.23.got, f32[512,128]{1,0:T(8,128)S(1)} %shard_map.230.mult, bf16[256,256]{1,0:T(8,128)(2,1)S(1)} %copy-done.4, bf16[256,256]{1,0:T(8,128)(2,1)S(1)} %copy-done.5, ...), custom_call_target="tpu_custom_call" | custom-call | tf_op jit(solution)/shard_map/pallas_call | solution.py:506
  56.7 1.1 %shard_map.244 = (f32[256,128]{1,0:T(8,128)S(1)}, f32[256,128]{1,0:T(8,128)S(1)}) custom-call(f32[256,128]{1,0:T(8,128)S(1)} %get-tuple-element.84.keep, f32[256,128]{1,0:T(8,128)S(1)} %collective-permute-done.18.got, f32[512,128]{1,0:T(8,128)S(1)} %shard_map.230.mult, bf16[256,256]{1,0:T(8,128)(2,1)S(1)} %copy-done.4, bf16[256,256]{1,0:T(8,128)(2,1)S(1)} %copy-done.5, ...), custom_call_target="tpu_custom_call" | custom-call | tf_op jit(solution)/shard_map/pallas_call | solution.py:506
  57.8 0.4 collective-permute-start.19
  58.6 1.5 %collective-permute-start.25 = (f32[64,256]{1,0:T(8,128)S(1)}, f32[64,256]{1,0:T(8,128)S(1)}, u32[]{:S(2)}, u32[]{:S(2)}) collective-permute-start(f32[64,256]{1,0:T(8,128)S(1)} %get-tuple-element.97), channel_id=1, source_target_pairs={{0,2},{1,3},{2,0},{3,1},{4,6},{5,7},{6,4},{7,5},{8,10},{9,11},{10,... | collective-permute-start | bytes 196616 | tf_op jit(solution)/shard_map/ppermute | solution.py:412
  60.1 0.6 collective-permute-start.26
  60.8 1.4 %collective-permute-start.27 = (f32[64,256]{1,0:T(8,128)S(1)}, f32[64,256]{1,0:T(8,128)S(1)}, u32[]{:S(2)}, u32[]{:S(2)}) collective-permute-start(f32[64,256]{1,0:T(8,128)S(1)} %get-tuple-element.99), channel_id=1, source_target_pairs={{0,6},{1,7},{2,4},{3,5},{4,2},{5,3},{6,0},{7,1},{8,14},{9,15},{10,... | collective-permute-start | bytes 196616 | tf_op jit(solution)/shard_map/ppermute | solution.py:412
  62.6 1.5 %collective-permute-start.20 = (f32[64,256]{1,0:T(8,128)S(1)}, f32[64,256]{1,0:T(8,128)S(1)}, u32[]{:S(2)}, u32[]{:S(2)}) collective-permute-start(f32[64,256]{1,0:T(8,128)S(1)} %get-tuple-element.89), channel_id=1, source_target_pairs={{0,2},{1,3},{2,0},{3,1},{4,6},{5,7},{6,4},{7,5},{8,10},{9,11},{10,... | collective-permute-start | bytes 196616 | tf_op jit(solution)/shard_map/ppermute | solution.py:412
  64.1 0.6 collective-permute-start.21
  64.8 1.4 %collective-permute-start.22 = (f32[64,256]{1,0:T(8,128)S(1)}, f32[64,256]{1,0:T(8,128)S(1)}, u32[]{:S(2)}, u32[]{:S(2)}) collective-permute-start(f32[64,256]{1,0:T(8,128)S(1)} %get-tuple-element.91), channel_id=1, source_target_pairs={{0,6},{1,7},{2,4},{3,5},{4,2},{5,3},{6,0},{7,1},{8,14},{9,15},{10,... | collective-permute-start | bytes 196616 | tf_op jit(solution)/shard_map/ppermute | solution.py:412
  66.2 0.5 collective-permute-done.27.refs_3_.refs_7_
  66.8 1.6 %collective-permute-start.28 = (f32[64,256]{1,0:T(8,128)S(1)}, f32[64,256]{1,0:T(8,128)S(1)}, u32[]{:S(2)}, u32[]{:S(2)}) collective-permute-start(f32[64,256]{1,0:T(8,128)S(1)} %get-tuple-element.100), channel_id=1, source_target_pairs={{0,8},{8,0},{1,9},{9,1},{2,10},{10,2},{3,11},{11,3},{4,12},{12,4},... | collective-permute-start | bytes 196616 | tf_op jit(solution)/shard_map/ppermute | solution.py:588
  68.3 1.9 %collective-permute-start.29 = (f32[64,256]{1,0:T(8,128)S(1)}, f32[64,256]{1,0:T(8,128)S(1)}, u32[]{:S(2)}, u32[]{:S(2)}) collective-permute-start(f32[64,256]{1,0:T(8,128)S(1)} %get-tuple-element.101), channel_id=1, source_target_pairs={{8,16},{16,8},{9,17},{17,9},{10,18},{18,10},{11,19},{19,11},{12,20... | collective-permute-start | bytes 196616 | tf_op jit(solution)/shard_map/ppermute | solution.py:589
  70.3 0.8 %collective-permute-done.28.refs_8_ = f32[64,256]{1,0:T(8,128)S(1)} collective-permute-done((f32[64,256]{1,0:T(8,128)S(1)}, f32[64,256]{1,0:T(8,128)S(1)}, u32[]{:S(2)}, u32[]{:S(2)}) %collective-permute-start.28) | collective-permute-done | bytes 65568 | tf_op jit(solution)/shard_map/ppermute | solution.py:588
  71.1 3.4 %collective-permute-done.29.refs_9_ = f32[64,256]{1,0:T(8,128)S(1)} collective-permute-done((f32[64,256]{1,0:T(8,128)S(1)}, f32[64,256]{1,0:T(8,128)S(1)}, u32[]{:S(2)}, u32[]{:S(2)}) %collective-permute-start.29) | collective-permute-done | bytes 65568 | tf_op jit(solution)/shard_map/ppermute | solution.py:589
  74.5 1.0 %shard_map.250 = (f32[4,32,256]{2,1,0:T(8,128)}, f32[4,32,256]{2,1,0:T(8,128)}, f32[4,32,256]{2,1,0:T(8,128)}, f32[4,32,256]{2,1,0:T(8,128)}) custom-call(f32[64,256]{1,0:T(8,128)S(1)} %get-tuple-element.88.refs_0_, f32[64,256]{1,0:T(8,128)S(1)} %collective-permute-done.20.refs_1_, f32[64,256]{1,0:T(8,128)S(1)} %collective-permute-done.21.refs_2_, ...), custom_call_target="tpu_custom_call" | custom-call | tf_op jit(solution)/shard_map/pallas_call | solution.py:635
  (67 shorter events, 6.1 us)
Async XLA Ops:
  0.6 10.8 %copy-start = (bf16[256,256]{1,0:T(8,128)(2,1)S(1)}, bf16[256,256]{1,0:T(8,128)(2,1)}, u32[]{:S(2)}) copy-start(bf16[256,256]{1,0:T(8,128)(2,1)} %constant.24.clone.refs_4_.refs_0_.refs_1_) | copy-start | bytes 393220
  0.6 10.8 %copy-start.1 = (bf16[256,256]{1,0:T(8,128)(2,1)S(1)}, bf16[256,256]{1,0:T(8,128)(2,1)}, u32[]{:S(2)}) copy-start(bf16[256,256]{1,0:T(8,128)(2,1)} %constant.25.clone.refs_5_.refs_1_.refs_2_) | copy-start | bytes 393220
  0.7 10.8 %copy-start.2 = (bf16[256,256]{1,0:T(8,128)(2,1)S(1)}, bf16[256,256]{1,0:T(8,128)(2,1)}, u32[]{:S(2)}) copy-start(bf16[256,256]{1,0:T(8,128)(2,1)} %constant.26.clone.refs_6_.refs_2_.refs_3_) | copy-start | bytes 393220
  0.7 10.8 %copy-start.3 = (bf16[256,256]{1,0:T(8,128)(2,1)S(1)}, bf16[256,256]{1,0:T(8,128)(2,1)}, u32[]{:S(2)}) copy-start(bf16[256,256]{1,0:T(8,128)(2,1)} %constant.27.clone.refs_7_.refs_3_.refs_4_) | copy-start | bytes 393220
  2.1 5.7 %collective-permute-start = (f32[128,256]{1,0:T(8,128)S(1)}, f32[128,256]{1,0:T(8,128)S(1)}, u32[]{:S(2)}, u32[]{:S(2)}) collective-permute-start(f32[128,256]{1,0:T(8,128)S(1)} %get-tuple-element.54), channel_id=1, source_target_pairs={{0,2},{1,3},{2,0},{3,1},{4,6},{5,7},{6,4},{7,5},{8,10},{9,11},{10,... | collective-permute-start | bytes 393224 | tf_op jit(solution)/shard_map/ppermute | solution.py:412
  3.7 7.8 %collective-permute-start.1 = (f32[128,256]{1,0:T(8,128)S(1)}, f32[128,256]{1,0:T(8,128)S(1)}, u32[]{:S(2)}, u32[]{:S(2)}) collective-permute-start(f32[128,256]{1,0:T(8,128)S(1)} %get-tuple-element.55), channel_id=1, source_target_pairs={{0,4},{1,5},{2,6},{3,7},{4,0},{5,1},{6,2},{7,3},{8,12},{9,13},{10,... | collective-permute-start | bytes 393224 | tf_op jit(solution)/shard_map/ppermute | solution.py:412
  5.2 6.3 %collective-permute-start.2 = (f32[128,256]{1,0:T(8,128)S(1)}, f32[128,256]{1,0:T(8,128)S(1)}, u32[]{:S(2)}, u32[]{:S(2)}) collective-permute-start(f32[128,256]{1,0:T(8,128)S(1)} %get-tuple-element.56), channel_id=1, source_target_pairs={{0,6},{1,7},{2,4},{3,5},{4,2},{5,3},{6,0},{7,1},{8,14},{9,15},{10,... | collective-permute-start | bytes 393224 | tf_op jit(solution)/shard_map/ppermute | solution.py:412
  12.6 2.0 %collective-permute-start.8 = (f32[256,128]{1,0:T(8,128)S(1)}, f32[256,128]{1,0:T(8,128)S(1)}, u32[]{:S(2)}, u32[]{:S(2)}) collective-permute-start(f32[256,128]{1,0:T(8,128)S(1)} %get-tuple-element.67), channel_id=1, source_target_pairs={{0,1},{1,0},{2,3},{3,2},{4,5},{5,4},{6,7},{7,6},{8,9},{9,8},{10,11... | collective-permute-start | bytes 393224 | tf_op jit(solution)/shard_map/ppermute | solution.py:548
  12.6 2.0 %copy-start.6 = (bf16[256,256]{1,0:T(8,128)(2,1)S(1)}, bf16[256,256]{1,0:T(8,128)(2,1)}, u32[]{:S(2)}) copy-start(bf16[256,256]{1,0:T(8,128)(2,1)} %constant.30.clone.refs_2_) | copy-start | bytes 393220
  12.6 2.0 %copy-start.7 = (bf16[256,256]{1,0:T(8,128)(2,1)S(1)}, bf16[256,256]{1,0:T(8,128)(2,1)}, u32[]{:S(2)}) copy-start(bf16[256,256]{1,0:T(8,128)(2,1)} %constant.31.clone.refs_3_) | copy-start | bytes 393220
  12.6 2.0 %copy-start.8 = (bf16[256,256]{1,0:T(8,128)(2,1)S(1)}, bf16[256,256]{1,0:T(8,128)(2,1)}, u32[]{:S(2)}) copy-start(bf16[256,256]{1,0:T(8,128)(2,1)} %constant.32.clone.refs_4_) | copy-start | bytes 393220
  12.6 2.0 %copy-start.9 = (bf16[256,256]{1,0:T(8,128)(2,1)S(1)}, bf16[256,256]{1,0:T(8,128)(2,1)}, u32[]{:S(2)}) copy-start(bf16[256,256]{1,0:T(8,128)(2,1)} %constant.33.clone.refs_5_) | copy-start | bytes 393220
  12.6 2.0 %copy-start.10 = (bf16[256,256]{1,0:T(8,128)(2,1)S(1)}, bf16[256,256]{1,0:T(8,128)(2,1)}, u32[]{:S(2)}) copy-start(bf16[256,256]{1,0:T(8,128)(2,1)} %constant.34.clone.refs_6_) | copy-start | bytes 393220
  12.6 2.0 %copy-start.11 = (bf16[256,256]{1,0:T(8,128)(2,1)S(1)}, bf16[256,256]{1,0:T(8,128)(2,1)}, u32[]{:S(2)}) copy-start(bf16[256,256]{1,0:T(8,128)(2,1)} %constant.35.clone.refs_7_) | copy-start | bytes 393220
  13.0 0.7 copy-start.15
  13.0 1.6 %copy-start.4 = (bf16[256,256]{1,0:T(8,128)(2,1)S(1)}, bf16[256,256]{1,0:T(8,128)(2,1)}, u32[]{:S(2)}) copy-start(bf16[256,256]{1,0:T(8,128)(2,1)} %constant.28.clone.refs_0_) | copy-start | bytes 393220
  13.1 1.6 %copy-start.5 = (bf16[256,256]{1,0:T(8,128)(2,1)S(1)}, bf16[256,256]{1,0:T(8,128)(2,1)}, u32[]{:S(2)}) copy-start(bf16[256,256]{1,0:T(8,128)(2,1)} %constant.29.clone.refs_1_) | copy-start | bytes 393220
  13.1 3.3 %collective-permute-start.3 = (f32[256,128]{1,0:T(8,128)S(1)}, f32[256,128]{1,0:T(8,128)S(1)}, u32[]{:S(2)}, u32[]{:S(2)}) collective-permute-start(f32[256,128]{1,0:T(8,128)S(1)} %get-tuple-element.58), channel_id=1, source_target_pairs={{0,1},{1,0},{2,3},{3,2},{4,5},{5,4},{6,7},{7,6},{8,9},{9,8},{10,11... | collective-permute-start | bytes 393224 | tf_op jit(solution)/shard_map/ppermute | solution.py:548
  15.8 9.8 %collective-permute-start.9 = (f32[256,128]{1,0:T(8,128)S(1)}, f32[256,128]{1,0:T(8,128)S(1)}, u32[]{:S(2)}, u32[]{:S(2)}) collective-permute-start(f32[256,128]{1,0:T(8,128)S(1)} %get-tuple-element.69), channel_id=1, source_target_pairs={{0,1},{1,0},{2,3},{3,2},{4,5},{5,4},{6,7},{7,6},{8,9},{9,8},{10,11... | collective-permute-start | bytes 393224 | tf_op jit(solution)/shard_map/ppermute | solution.py:548
  17.5 8.5 %collective-permute-start.4 = (f32[256,128]{1,0:T(8,128)S(1)}, f32[256,128]{1,0:T(8,128)S(1)}, u32[]{:S(2)}, u32[]{:S(2)}) collective-permute-start(f32[256,128]{1,0:T(8,128)S(1)} %get-tuple-element.60), channel_id=1, source_target_pairs={{0,1},{1,0},{2,3},{3,2},{4,5},{5,4},{6,7},{7,6},{8,9},{9,8},{10,11... | collective-permute-start | bytes 393224 | tf_op jit(solution)/shard_map/ppermute | solution.py:548
  17.6 4.5 %collective-permute-start.5 = (f32[64,256]{1,0:T(8,128)S(1)}, f32[64,256]{1,0:T(8,128)S(1)}, u32[]{:S(2)}, u32[]{:S(2)}) collective-permute-start(f32[64,256]{1,0:T(8,128)S(1)} %get-tuple-element.62), channel_id=1, source_target_pairs={{0,2},{1,3},{2,0},{3,1},{4,6},{5,7},{6,4},{7,5},{8,10},{9,11},{10,... | collective-permute-start | bytes 196616 | tf_op jit(solution)/shard_map/ppermute | solution.py:412
  18.9 4.3 %collective-permute-start.6 = (f32[64,256]{1,0:T(8,128)S(1)}, f32[64,256]{1,0:T(8,128)S(1)}, u32[]{:S(2)}, u32[]{:S(2)}) collective-permute-start(f32[64,256]{1,0:T(8,128)S(1)} %get-tuple-element.63), channel_id=1, source_target_pairs={{0,4},{1,5},{2,6},{3,7},{4,0},{5,1},{6,2},{7,3},{8,12},{9,13},{10,... | collective-permute-start | bytes 196616 | tf_op jit(solution)/shard_map/ppermute | solution.py:412
  19.7 5.2 %collective-permute-start.7 = (f32[64,256]{1,0:T(8,128)S(1)}, f32[64,256]{1,0:T(8,128)S(1)}, u32[]{:S(2)}, u32[]{:S(2)}) collective-permute-start(f32[64,256]{1,0:T(8,128)S(1)} %get-tuple-element.64), channel_id=1, source_target_pairs={{0,6},{1,7},{2,4},{3,5},{4,2},{5,3},{6,0},{7,1},{8,14},{9,15},{10,... | collective-permute-start | bytes 196616 | tf_op jit(solution)/shard_map/ppermute | solution.py:412
  26.5 7.1 %collective-permute-start.10 = (f32[256,256]{1,0:T(8,128)S(1)}, f32[256,256]{1,0:T(8,128)S(1)}, u32[]{:S(2)}, u32[]{:S(2)}) collective-permute-start(f32[256,256]{1,0:T(8,128)S(1)} %get-tuple-element.70), channel_id=1, source_target_pairs={{0,2},{2,0},{1,3},{3,1},{6,4},{4,6},{7,5},{5,7},{12,14},{14,12},{1... | collective-permute-start | bytes 786440 | tf_op jit(solution)/shard_map/ppermute | solution.py:561
  28.0 8.5 %collective-permute-start.11 = (f32[256,256]{1,0:T(8,128)S(1)}, f32[256,256]{1,0:T(8,128)S(1)}, u32[]{:S(2)}, u32[]{:S(2)}) collective-permute-start(f32[256,256]{1,0:T(8,128)S(1)} %get-tuple-element.71), channel_id=1, source_target_pairs={{2,6},{6,2},{3,7},{7,3},{4,12},{12,4},{5,13},{13,5},{14,10},{10,14... | collective-permute-start | bytes 786440 | tf_op jit(solution)/shard_map/ppermute | solution.py:562
  37.0 1.4 %collective-permute-start.14 = (f32[256,128]{1,0:T(8,128)S(1)}, f32[256,128]{1,0:T(8,128)S(1)}, u32[]{:S(2)}, u32[]{:S(2)}) collective-permute-start(f32[256,128]{1,0:T(8,128)S(1)} %get-tuple-element.79), channel_id=1, source_target_pairs={{0,1},{1,0},{2,3},{3,2},{4,5},{5,4},{6,7},{7,6},{8,9},{9,8},{10,11... | collective-permute-start | bytes 393224 | tf_op jit(solution)/shard_map/ppermute | solution.py:548
  37.4 2.3 %collective-permute-start.12 = (f32[256,128]{1,0:T(8,128)S(1)}, f32[256,128]{1,0:T(8,128)S(1)}, u32[]{:S(2)}, u32[]{:S(2)}) collective-permute-start(f32[256,128]{1,0:T(8,128)S(1)} %get-tuple-element.75), channel_id=1, source_target_pairs={{0,1},{1,0},{2,3},{3,2},{4,5},{5,4},{6,7},{7,6},{8,9},{9,8},{10,11... | collective-permute-start | bytes 393224 | tf_op jit(solution)/shard_map/ppermute | solution.py:548
  39.5 1.8 %collective-permute-start.15 = (f32[256,128]{1,0:T(8,128)S(1)}, f32[256,128]{1,0:T(8,128)S(1)}, u32[]{:S(2)}, u32[]{:S(2)}) collective-permute-start(f32[256,128]{1,0:T(8,128)S(1)} %get-tuple-element.81), channel_id=1, source_target_pairs={{0,1},{1,0},{2,3},{3,2},{4,5},{5,4},{6,7},{7,6},{8,9},{9,8},{10,11... | collective-permute-start | bytes 393224 | tf_op jit(solution)/shard_map/ppermute | solution.py:548
  40.8 1.4 %collective-permute-start.13 = (f32[256,128]{1,0:T(8,128)S(1)}, f32[256,128]{1,0:T(8,128)S(1)}, u32[]{:S(2)}, u32[]{:S(2)}) collective-permute-start(f32[256,128]{1,0:T(8,128)S(1)} %get-tuple-element.77), channel_id=1, source_target_pairs={{0,1},{1,0},{2,3},{3,2},{4,5},{5,4},{6,7},{7,6},{8,9},{9,8},{10,11... | collective-permute-start | bytes 393224 | tf_op jit(solution)/shard_map/ppermute | solution.py:548
  42.7 8.6 %collective-permute-start.16 = (f32[256,256]{1,0:T(8,128)S(1)}, f32[256,256]{1,0:T(8,128)S(1)}, u32[]{:S(2)}, u32[]{:S(2)}) collective-permute-start(f32[256,256]{1,0:T(8,128)S(1)} %get-tuple-element.82), channel_id=1, source_target_pairs={{0,2},{2,0},{1,3},{3,1},{6,4},{4,6},{7,5},{5,7},{12,14},{14,12},{1... | collective-permute-start | bytes 786440 | tf_op jit(solution)/shard_map/ppermute | solution.py:561
  43.3 10.2 %collective-permute-start.17 = (f32[256,256]{1,0:T(8,128)S(1)}, f32[256,256]{1,0:T(8,128)S(1)}, u32[]{:S(2)}, u32[]{:S(2)}) collective-permute-start(f32[256,256]{1,0:T(8,128)S(1)} %get-tuple-element.83), channel_id=1, source_target_pairs={{2,6},{6,2},{3,7},{7,3},{4,12},{12,4},{5,13},{13,5},{14,10},{10,14... | collective-permute-start | bytes 786440 | tf_op jit(solution)/shard_map/ppermute | solution.py:562
  53.9 1.4 %collective-permute-start.23 = (f32[256,128]{1,0:T(8,128)S(1)}, f32[256,128]{1,0:T(8,128)S(1)}, u32[]{:S(2)}, u32[]{:S(2)}) collective-permute-start(f32[256,128]{1,0:T(8,128)S(1)} %get-tuple-element.93), channel_id=1, source_target_pairs={{0,1},{1,0},{2,3},{3,2},{4,5},{5,4},{6,7},{7,6},{8,9},{9,8},{10,11... | collective-permute-start | bytes 393224 | tf_op jit(solution)/shard_map/ppermute | solution.py:548
  54.4 2.3 %collective-permute-start.18 = (f32[256,128]{1,0:T(8,128)S(1)}, f32[256,128]{1,0:T(8,128)S(1)}, u32[]{:S(2)}, u32[]{:S(2)}) collective-permute-start(f32[256,128]{1,0:T(8,128)S(1)} %get-tuple-element.85), channel_id=1, source_target_pairs={{0,1},{1,0},{2,3},{3,2},{4,5},{5,4},{6,7},{7,6},{8,9},{9,8},{10,11... | collective-permute-start | bytes 393224 | tf_op jit(solution)/shard_map/ppermute | solution.py:548
  56.4 1.8 %collective-permute-start.24 = (f32[256,128]{1,0:T(8,128)S(1)}, f32[256,128]{1,0:T(8,128)S(1)}, u32[]{:S(2)}, u32[]{:S(2)}) collective-permute-start(f32[256,128]{1,0:T(8,128)S(1)} %get-tuple-element.95), channel_id=1, source_target_pairs={{0,1},{1,0},{2,3},{3,2},{4,5},{5,4},{6,7},{7,6},{8,9},{9,8},{10,11... | collective-permute-start | bytes 393224 | tf_op jit(solution)/shard_map/ppermute | solution.py:548
  57.8 4.4 %collective-permute-start.19 = (f32[256,128]{1,0:T(8,128)S(1)}, f32[256,128]{1,0:T(8,128)S(1)}, u32[]{:S(2)}, u32[]{:S(2)}) collective-permute-start(f32[256,128]{1,0:T(8,128)S(1)} %get-tuple-element.87), channel_id=1, source_target_pairs={{0,1},{1,0},{2,3},{3,2},{4,5},{5,4},{6,7},{7,6},{8,9},{9,8},{10,11... | collective-permute-start | bytes 393224 | tf_op jit(solution)/shard_map/ppermute | solution.py:548
  58.6 6.1 %collective-permute-start.25 = (f32[64,256]{1,0:T(8,128)S(1)}, f32[64,256]{1,0:T(8,128)S(1)}, u32[]{:S(2)}, u32[]{:S(2)}) collective-permute-start(f32[64,256]{1,0:T(8,128)S(1)} %get-tuple-element.97), channel_id=1, source_target_pairs={{0,2},{1,3},{2,0},{3,1},{4,6},{5,7},{6,4},{7,5},{8,10},{9,11},{10,... | collective-permute-start | bytes 196616 | tf_op jit(solution)/shard_map/ppermute | solution.py:412
  60.1 6.1 %collective-permute-start.26 = (f32[64,256]{1,0:T(8,128)S(1)}, f32[64,256]{1,0:T(8,128)S(1)}, u32[]{:S(2)}, u32[]{:S(2)}) collective-permute-start(f32[64,256]{1,0:T(8,128)S(1)} %get-tuple-element.98), channel_id=1, source_target_pairs={{0,4},{1,5},{2,6},{3,7},{4,0},{5,1},{6,2},{7,3},{8,12},{9,13},{10,... | collective-permute-start | bytes 196616 | tf_op jit(solution)/shard_map/ppermute | solution.py:412
  60.8 5.9 %collective-permute-start.27 = (f32[64,256]{1,0:T(8,128)S(1)}, f32[64,256]{1,0:T(8,128)S(1)}, u32[]{:S(2)}, u32[]{:S(2)}) collective-permute-start(f32[64,256]{1,0:T(8,128)S(1)} %get-tuple-element.99), channel_id=1, source_target_pairs={{0,6},{1,7},{2,4},{3,5},{4,2},{5,3},{6,0},{7,1},{8,14},{9,15},{10,... | collective-permute-start | bytes 196616 | tf_op jit(solution)/shard_map/ppermute | solution.py:412
  62.6 7.6 %collective-permute-start.20 = (f32[64,256]{1,0:T(8,128)S(1)}, f32[64,256]{1,0:T(8,128)S(1)}, u32[]{:S(2)}, u32[]{:S(2)}) collective-permute-start(f32[64,256]{1,0:T(8,128)S(1)} %get-tuple-element.89), channel_id=1, source_target_pairs={{0,2},{1,3},{2,0},{3,1},{4,6},{5,7},{6,4},{7,5},{8,10},{9,11},{10,... | collective-permute-start | bytes 196616 | tf_op jit(solution)/shard_map/ppermute | solution.py:412
  64.1 6.1 %collective-permute-start.21 = (f32[64,256]{1,0:T(8,128)S(1)}, f32[64,256]{1,0:T(8,128)S(1)}, u32[]{:S(2)}, u32[]{:S(2)}) collective-permute-start(f32[64,256]{1,0:T(8,128)S(1)} %get-tuple-element.90), channel_id=1, source_target_pairs={{0,4},{1,5},{2,6},{3,7},{4,0},{5,1},{6,2},{7,3},{8,12},{9,13},{10,... | collective-permute-start | bytes 196616 | tf_op jit(solution)/shard_map/ppermute | solution.py:412
  64.8 5.5 %collective-permute-start.22 = (f32[64,256]{1,0:T(8,128)S(1)}, f32[64,256]{1,0:T(8,128)S(1)}, u32[]{:S(2)}, u32[]{:S(2)}) collective-permute-start(f32[64,256]{1,0:T(8,128)S(1)} %get-tuple-element.91), channel_id=1, source_target_pairs={{0,6},{1,7},{2,4},{3,5},{4,2},{5,3},{6,0},{7,1},{8,14},{9,15},{10,... | collective-permute-start | bytes 196616 | tf_op jit(solution)/shard_map/ppermute | solution.py:412
  66.7 7.8 %copy-start.12 = (f32[4,32,256]{2,1,0:T(8,128)S(1)}, f32[4,32,256]{2,1,0:T(8,128)}, u32[]{:S(2)}) copy-start(f32[4,32,256]{2,1,0:T(8,128)} %refs_10_.1) | copy-start | bytes 393220
  66.7 7.8 %copy-start.13 = (f32[32,256]{1,0:T(8,128)S(1)}, f32[32,256]{1,0:T(8,128)}, u32[]{:S(2)}) copy-start(f32[32,256]{1,0:T(8,128)} %refs_11_.1) | copy-start | bytes 98308
  66.7 7.8 %copy-start.14 = (f32[32,256]{1,0:T(8,128)S(1)}, f32[32,256]{1,0:T(8,128)}, u32[]{:S(2)}) copy-start(f32[32,256]{1,0:T(8,128)} %refs_12_.1) | copy-start | bytes 98308
  66.8 4.3 %collective-permute-start.28 = (f32[64,256]{1,0:T(8,128)S(1)}, f32[64,256]{1,0:T(8,128)S(1)}, u32[]{:S(2)}, u32[]{:S(2)}) collective-permute-start(f32[64,256]{1,0:T(8,128)S(1)} %get-tuple-element.100), channel_id=1, source_target_pairs={{0,8},{8,0},{1,9},{9,1},{2,10},{10,2},{3,11},{11,3},{4,12},{12,4},... | collective-permute-start | bytes 196616 | tf_op jit(solution)/shard_map/ppermute | solution.py:588
  68.3 6.1 %collective-permute-start.29 = (f32[64,256]{1,0:T(8,128)S(1)}, f32[64,256]{1,0:T(8,128)S(1)}, u32[]{:S(2)}, u32[]{:S(2)}) collective-permute-start(f32[64,256]{1,0:T(8,128)S(1)} %get-tuple-element.101), channel_id=1, source_target_pairs={{8,16},{16,8},{9,17},{17,9},{10,18},{18,10},{11,19},{19,11},{12,20... | collective-permute-start | bytes 196616 | tf_op jit(solution)/shard_map/ppermute | solution.py:589
where the time goes:
time: 75.6 us; the launch traced here: 75.4 us
  waiting for transfers between devices  29.5 us (39%)
  starting transfers between devices  28.4 us (38%)
  Pallas kernels  16.3 us (22%)
  between operations  1.08 us (1%)
    ppermute x12, starting transfers between devices, exchanged(): moved.append(lax.ppermute(pieces[step], 'lat', across(step)))  14.2 us
    ppermute x12, waiting for transfers between devices, exchanged(): moved.append(lax.ppermute(pieces[step], 'lat', across(step)))  10 us
    ppermute x2, waiting for transfers between devices, plane_shards(): lax.ppermute(first, ('depth', 'lat'), level_pairs(sections, pairs, 0))  8.75 us
    pallas_call x6, Pallas kernels, column(): local_call(body, [part, part], 'v' * 11, [pltpu.VMEM((rows, wide), f32) f...  6.65 us
    ppermute x2, waiting for transfers between devices, plane_shards(): lax.ppermute(second, ('depth', 'lat'), level_pairs(sections, pairs, 1))  5.23 us
    ppermute x2, starting transfers between devices, plane_shards(): lax.ppermute(second, ('depth', 'lat'), level_pairs(sections, pairs, 1))  4.72 us
    ppermute x12, starting transfers between devices, crossed(): return lax.ppermute(value, 'lat', swap)  3.86 us
    ppermute x1, waiting for transfers between devices, plane_shards(): odd = lax.ppermute(odd, ('depth', 'lat'), section_pairs(sections, pairs, 1))  3.38 us
  transfers between devices with their start and end apart: 30, of which 15 were waited for; matrix products, arithmetic and copies ran while one was open for 0% of the time, Pallas kernels for 15%

commit v1 on v0

--- a/solution.py
+++ b/solution.py
@@ -200,16 +200,29 @@
     return edges
 
 
-def transform_tables(count, order, transposed):
-    index = np.arange(count)
-    angle = (index[:, None] * np.asarray(order)[None, :] % count) * (2.0 * math.pi / count)
-    if transposed:
+def split_table(table):
+    high = table.astype(np.float32).astype(jnp.bfloat16)
+    return high, (table - high.astype(np.float64)).astype(np.float32).astype(jnp.bfloat16)
+
+
+def half_tables(order, inverse):
+    count = len(order)
+    angle = (np.arange(count)[None, :] * np.asarray(order)[:, None] % count) * (
+        2.0 * math.pi / count
+    )
+    if inverse:
         angle = angle.T
-    parts = []
-    for table in (np.cos(angle), np.sin(angle)):
-        high = table.astype(np.float32).astype(jnp.bfloat16)
-        parts += [high, (table - high.astype(np.float64)).astype(np.float32).astype(jnp.bfloat16)]
-    return parts
+    (cos_high, cos_low), (sin_high, sin_low) = split_table(np.cos(angle)), split_table(
+        np.sin(angle) * (-1.0 if inverse else 1.0)
+    )
+    real = [np.concatenate([c, -s], axis=1) for c, s in ((cos_high, sin_high), (cos_low, sin_low))]
+    imag = [np.concatenate([s, c], axis=1) for c, s in ((cos_high, sin_high), (cos_low, sin_low))]
+    return np.concatenate([real[0], real[0], real[1], imag[0], imag[0], imag[1]], axis=0)
+
+
+def turn_tables(order):
+    angle = np.asarray(order) * (math.pi / len(order))
+    return np.stack([np.cos(angle), np.sin(angle)]).astype(np.float32)
 
 
 def halves(value):
@@ -231,13 +244,17 @@
     return cosine, angle * sine
 
 
-def multiplier(ref, rows, columns, first, here_columns):
-    def wave(count, axis, start):
-        index = lax.broadcasted_iota(jnp.int32, (rows, here_columns), axis) + start
+def multiplier(ref, rows, columns, core):
+    shape = (rows // 2, columns)
+    along = lax.broadcasted_iota(jnp.int32, shape, 1)
+    odd = (along >= columns // 2).astype(jnp.int32)
+
+    def wave(count, index):
         folded = jnp.where(index < count // 2, index, index - count)
         return folded.astype(jnp.float32) * (2.0 * math.pi / count)
 
-    wave_x, wave_y = wave(rows, 0, 0), wave(columns, 1, first)
+    wave_x = wave(rows, 2 * lax.broadcasted_iota(jnp.int32, shape, 0) + odd)
+    wave_y = wave(columns, 2 * (along - odd * (columns // 2)) + core)
     argument = (OMEGA * ref) ** 2 - (wave_x * wave_x + wave_y * wave_y)
     vertical = jnp.sqrt(jnp.maximum(argument, 0.0)) * DEPTH_STEP
     evanescent = jnp.sqrt(jnp.maximum(-argument, 0.0)) * DEPTH_STEP
@@ -246,45 +263,37 @@
     return factor * (1.0 - 2.0 * sine * sine), factor * (-2.0 * sine * cosine)
 
 
-def terms(a, b, inverse):
+def parts_of(a, b, axis):
     a_high, a_low = halves(a)
     b_high, b_low = halves(b)
-    if inverse:
-        real = [a_high, a_low, a_high, -b_high, -b_low, -b_high]
-        imag = [b_high, b_low, b_high, a_high, a_low, a_high]
-    else:
-        real = [a_high, a_low, a_high, b_high, b_low, b_high]
-        imag = [b_high, b_low, b_high, -a_high, -a_low, -a_high]
-    return real, imag
-
-
-def table_of(parts, axis):
-    cos_high, cos_low, sin_high, sin_low = (part[...] for part in parts)
-    return jnp.concatenate(
-        [cos_high, cos_high, cos_low, sin_high, sin_high, sin_low], axis=axis
-    )
-
-
-def along_y(a, b, parts, inverse):
-    count = a.shape[0]
-    real, imag = (jnp.concatenate(t, axis=1) for t in terms(a, b, inverse))
-    out = jnp.dot(
-        jnp.concatenate([real, imag], axis=0),
-        table_of(parts, 0),
-        preferred_element_type=jnp.float32,
-    )
-    return out[:count], out[count:]
-
-
-def along_x(a, b, parts, inverse):
-    count = a.shape[1]
-    real, imag = (jnp.concatenate(t, axis=0) for t in terms(a, b, inverse))
-    out = jnp.dot(
-        table_of(parts, 1),
-        jnp.concatenate([real, imag], axis=1),
-        preferred_element_type=jnp.float32,
-    )
-    return out[:, :count], out[:, count:]
+    return jnp.concatenate([a_high, a_low, a_high, b_high, b_low, b_high], axis=axis)
+
+
+def forward_y(real, imag, table, turn):
+    count, wide = real.shape[0], real.shape[1] // 2
+    cosine, sine = turn[0:1, :], turn[1:2, :]
+    d_real, d_imag = real[:, :wide] - real[:, wide:], imag[:, :wide] - imag[:, wide:]
+    a = jnp.concatenate(
+        [real[:, :wide] + real[:, wide:], d_real * cosine + d_imag * sine], axis=0
+    )
+    b = jnp.concatenate(
+        [imag[:, :wide] + imag[:, wide:], d_imag * cosine - d_real * sine], axis=0
+    )
+    out = jnp.dot(parts_of(a, b, 1), table[...], preferred_element_type=jnp.float32)
+    return (out[:count, :wide], out[:count, wide:]), (out[count:, :wide], out[count:, wide:])
+
+
+def inverse_y(a, b, table, turn):
+    count, wide = a.shape[0] // 2, a.shape[1]
+    cosine, sine = turn[0:1, :], turn[1:2, :]
+    out = jnp.dot(parts_of(a, b, 1), table[...], preferred_element_type=jnp.float32)
+    e_real, e_imag = out[:count, :wide], out[:count, wide:]
+    o_real, o_imag = out[count:, :wide], out[count:, wide:]
+    o_real, o_imag = o_real * cosine - o_imag * sine, o_imag * cosine + o_real * sine
+    return (
+        jnp.concatenate([e_real + o_real, e_real - o_real], axis=1),
+        jnp.concatenate([e_imag + o_imag, e_imag - o_imag], axis=1),
+    )
 
 
 class Place:
@@ -330,11 +339,16 @@
     wide = columns // 2
     two, four = 2 * block, 4 * block
     swap = [(index, index ^ 1) for index in range(lat_count)]
-    place = np.arange(rows)
-    order = place % tall // block * two + place // tall * block + place % block
-    y_tables = [jnp.asarray(t) for t in transform_tables(columns, np.arange(columns), False)]
-    x_tables = [jnp.asarray(t) for t in transform_tables(rows, order, False)]
-    back_tables = [jnp.asarray(t) for t in transform_tables(rows, order, True)]
+    quarter = tall // 2
+    place = np.arange(tall)
+    order = place % quarter // block * two + place // quarter * block + place % block
+    straight = np.arange(wide)
+    y_table, y_back = (jnp.asarray(half_tables(straight, inverse)) for inverse in (False, True))
+    x_table, x_back = (jnp.asarray(half_tables(order, inverse).T) for inverse in (False, True))
+    y_turn = jnp.asarray(turn_tables(straight))
+    x_turn = jnp.asarray(
+        np.broadcast_to(turn_tables(order)[:, :, None], (2, tall, wide)).copy()
+    )
     f32 = jnp.float32
     local = (2 * tall, columns)
     part = (2 * tall, wide)
@@ -417,11 +431,9 @@
 
     def multiplier_body(ref_slow, out):
         here = Place(pairs)
-        real, imag = multiplier(ref_slow[here.level], rows, columns, here.core * wide, wide)
-        out[:rows] = real
-        out[rows:] = imag
-
-    mult = local_call(multiplier_body, [(2 * rows, wide)], "s")(ref_slow)[0]
+        out[:tall], out[tall:] = multiplier(ref_slow[here.level], rows, columns, here.core)
+
+    mult = local_call(multiplier_body, [local], "s")(ref_slow)[0]
 
     def media_body(*refs):
         pieces, ref_slow, corr, refl = refs[:pairs], refs[pairs], refs[pairs + 1], refs[pairs + 2]
@@ -441,28 +453,22 @@
         *media, ref_slow
     )
 
-    def halved(real, imag, here, axis, keep, send):
+    def shared(first, second, here, keep, send):
         def put(mine, theirs):
             keep[:tall], keep[tall:] = mine
             send[:tall], send[tall:] = theirs
 
-        if axis == 0:
-            cuts = [(real[:tall], imag[:tall]), (real[tall:], imag[tall:])]
-        else:
-            cuts = [(real[:, :wide], imag[:, :wide]), (real[:, wide:], imag[:, wide:])]
-
         @pl.when(here.core == 0)
         def _():
-            put(cuts[0], cuts[1])
+            put(first, second)
 
         @pl.when(here.core == 1)
         def _():
-            put(cuts[1], cuts[0])
+            put(second, first)
 
     def enter(which):
         def body(*refs):
-            pieces, tabs, keep, send = refs[:pairs], refs[pairs : pairs + 4], *refs[pairs + 4 : -1]
-            whole = refs[-1]
+            pieces, (table, turn, keep, send, whole) = refs[:pairs], refs[pairs:]
             here = Place(pairs)
             for step in range(pairs):
                 start = (here.pair ^ step) * block
@@ -470,15 +476,12 @@
                     whole[pl.ds(pl.multiple_of(n * tall + start, block), block), :] = pieces[step][
                         pl.ds((2 * which + n) * block, block), :
                     ]
-            halved(*along_y(whole[:tall], whole[tall:], tabs, False), here, 1, keep, send)
-
-        return local_call(body, [part, part, local], "v" * (pairs + 4))(
-            *planes, *y_tables
-        )
+            shared(*forward_y(whole[:tall], whole[tall:], table, turn), here, keep, send)
+
+        return local_call(body, [part, part, local], "v" * (pairs + 2))(*planes, y_table, y_turn)
 
     def mixed(which, ahead, behind, source):
-        def body(ahead, behind, source, refl, *refs):
-            tabs, keep, send = refs[:4], refs[4], refs[5]
+        def body(ahead, behind, source, refl, table, turn, keep, send):
             here = Place(pairs)
             sign = jnp.where((here.level % 2 == 0) == (which == 0), -1.0, 1.0)
             behind = jnp.where(top(here), source[...], behind[...])
@@ -486,52 +489,75 @@
             weight = refl[...] * sign
             real = base[:tall] + weight * side[:tall]
             imag = base[tall:] + weight * side[tall:]
-            halved(*along_y(real, imag, tabs, False), here, 1, keep, send)
-
-        return local_call(body, [part, part], "v" * 8)(ahead, behind, source, refl, *y_tables)
+            shared(*forward_y(real, imag, table, turn), here, keep, send)
+
+        return local_call(body, [part, part], "v" * 6)(ahead, behind, source, refl, y_table, y_turn)
 
     def column(keep, got):
-        def body(keep, got, mult, *refs):
-            tabs, back, out, send, real, imag = refs[:4], refs[4:8], *refs[8:]
+        def body(keep, got, mult, table, back, turn, out, send, near, far):
             here = Place(pairs)
             for piece, core in ((keep, here.core), (got, 1 - here.core)):
-                take = pl.ds(pl.multiple_of(core * tall, tall), tall)
-                real[take, :] = piece[:tall]
-                imag[take, :] = piece[tall:]
-            a, b = along_x(real[...], imag[...], tabs, False)
-            mult_real, mult_imag = mult[:rows], mult[rows:]
-            a, b = a * mult_real - b * mult_imag, a * mult_imag + b * mult_real
-            halved(*along_x(a, b, back, True), here, 0, out, send)
+                for n in range(2):
+                    take = pl.ds(pl.multiple_of(n * tall + core * quarter, quarter), quarter)
+                    near[take, :] = piece[pl.ds(n * tall, quarter), :]
+                    far[take, :] = piece[pl.ds(n * tall + quarter, quarter), :]
+            cosine, sine = turn[0], turn[1]
+            d_real, d_imag = near[:tall] - far[:tall], near[tall:] - far[tall:]
+            a = jnp.concatenate(
+                [near[:tall] + far[:tall], d_real * cosine + d_imag * sine], axis=1
+            )
+            b = jnp.concatenate(
+                [near[tall:] + far[tall:], d_imag * cosine - d_real * sine], axis=1
+            )
+            spec = jnp.dot(table[...], parts_of(a, b, 0), preferred_element_type=f32)
+            a = spec[:tall] * mult[:tall] - spec[tall:] * mult[tall:]
+            b = spec[:tall] * mult[tall:] + spec[tall:] * mult[:tall]
+            moved = jnp.dot(back[...], parts_of(a, b, 0), preferred_element_type=f32)
+            o_real, o_imag = moved[:tall, wide:], moved[tall:, wide:]
+            o_real, o_imag = o_real * cosine - o_imag * sine, o_imag * cosine + o_real * sine
+            e_real, e_imag = moved[:tall, :wide], moved[tall:, :wide]
+            joined = []
+            for even, odd in ((e_real, o_real), (e_imag, o_imag)):
+                low, high = even + odd, even - odd
+                joined.append(
+                    [
+                        jnp.concatenate([low[take], high[take]], axis=0)
+                        for take in (slice(0, quarter), slice(quarter, tall))
+                    ]
+                )
+            shared(*zip(*joined), here, out, send)
 
         return local_call(
-            body, [part, part], "v" * 11, [pltpu.VMEM((rows, wide), f32) for _ in range(2)]
-        )(keep, got, mult, *x_tables, *back_tables)
-
-    def corrected(keep, got, corr, tabs, here, whole):
+            body, [part, part], "v" * 6, [pltpu.VMEM(part, f32) for _ in range(2)]
+        )(keep, got, mult, x_table, x_back, x_turn)
+
+    def corrected(keep, got, corr, table, turn, here, whole):
         for piece, core in ((keep, here.core), (got, 1 - here.core)):
-            whole[:, pl.ds(pl.multiple_of(core * wide, wide), wide)] = piece[...]
-        real, imag = along_y(whole[:tall], whole[tall:], tabs, True)
+            take = pl.ds(pl.multiple_of(core * tall, tall), tall)
+            whole[take, pl.ds(0, wide)] = piece[:tall]
+            whole[take, pl.ds(wide, wide)] = piece[tall:]
+        real, imag = inverse_y(whole[:, :wide], whole[:, wide:], table, turn)
         cosine, sine = corr[:tall], corr[tall:]
         return real * cosine + imag * sine, imag * cosine - real * sine
 
     def leave(keep, got, *held):
         def body(keep, got, corr, *refs):
-            kept, tabs, outs = refs[: len(held)], refs[len(held) : len(held) + 4], refs[4 + len(held) :]
+            kept, (table, turn), outs = refs[: len(held)], refs[len(held) :][:2], refs[2 + len(held) :]
             whole = outs[-1]
             for source, target in zip(kept, outs[1:]):
                 target[...] = source[...]
-            real, imag = corrected(keep, got, corr, tabs, Place(pairs), whole)
+            real, imag = corrected(keep, got, corr, table, turn, Place(pairs), whole)
             outs[0][:tall], outs[0][tall:] = real, imag
 
         return local_call(
-            body, [local] * (1 + len(held)), "v" * (7 + len(held)), [pltpu.VMEM(local, f32)]
-        )(keep, got, corr, *held, *y_tables)
+            body, [local] * (1 + len(held)), "v" * (5 + len(held)), [pltpu.VMEM(local, f32)]
+        )(keep, got, corr, *held, y_back, y_turn)
 
     def leave_last(keep, got):
-        def body(keep, got, corr, *refs):
-            tabs, outs, whole = refs[:4], refs[4 : 4 + pairs], refs[4 + pairs]
+        def body(keep, got, corr, table, turn, *refs):
+            outs, whole = refs[:pairs], refs[pairs]
             here = Place(pairs)
-            real, imag = corrected(keep, got, corr, tabs, here, whole)
+            real, imag = corrected(keep, got, corr, table, turn, here, whole)
             whole[:tall], whole[tall:] = real, imag
             for step in range(pairs):
                 start = (here.pair ^ step) * block
@@ -541,8 +567,8 @@
                     ]
 
         return local_call(
-            body, [(two, columns)] * pairs, "v" * 7, [pltpu.VMEM(local, f32)]
-        )(keep, got, corr, *y_tables)
+            body, [(two, columns)] * pairs, "v" * 5, [pltpu.VMEM(local, f32)]
+        )(keep, got, corr, y_back, y_turn)
 
     def crossed(value):
         return lax.ppermute(value, "lat", swap)
@@ -648,7 +674,7 @@
         mesh.shape["lat"] == 2 * levels
         and levels >= 2
         and levels & (levels - 1) == 0
-        and rows // mesh.shape["lat"] % 8 == 0
+        and rows // mesh.shape["lat"] % 16 == 0
         and columns % 256 == 0
     )
 

time: 75.6 us -> 72.5 us (0.959)
  Pallas kernels: 16.3 us -> 13.1 us
    pallas_call x19, Pallas kernels: 13.1 us -> 9.9 us  [the longest x6 4.51 us: column(): local_call(body, [part, part], 'v' * 6, [pltpu.VMEM(part, f32) for _ in r...]
  transfers between devices with their start and end apart: 30 -> 30, of which waited for: 15 -> 15; matrix products, arithmetic and copies ran while one was open for 0% -> 0% of each run, Pallas kernels for 15% -> 12%
where the time goes in v1:
time: 72.5 us; the launch traced here: 72.4 us
  waiting for transfers between devices  29.8 us (41%)
  starting transfers between devices  28.4 us (39%)
  Pallas kernels  13.1 us (18%)
  between operations  0.98 us (1%)
    ppermute x12, starting transfers between devices, exchanged(): moved.append(lax.ppermute(pieces[step], 'lat', across(step)))  14.2 us
    ppermute x12, waiting for transfers between devices, exchanged(): moved.append(lax.ppermute(pieces[step], 'lat', across(step)))  10 us
    ppermute x2, waiting for transfers between devices, plane_shards(): lax.ppermute(first, ('depth', 'lat'), level_pairs(sections, pairs, 0))  8.76 us
    ppermute x2, waiting for transfers between devices, plane_shards(): lax.ppermute(second, ('depth', 'lat'), level_pairs(sections, pairs, 1))  5.23 us
    ppermute x2, starting transfers between devices, plane_shards(): lax.ppermute(second, ('depth', 'lat'), level_pairs(sections, pairs, 1))  4.71 us
    pallas_call x6, Pallas kernels, column(): local_call(body, [part, part], 'v' * 6, [pltpu.VMEM(part, f32) for _ in r...  4.51 us
    ppermute x12, starting transfers between devices, crossed(): return lax.ppermute(value, 'lat', swap)  3.86 us
    ppermute x1, waiting for transfers between devices, plane_shards(): odd = lax.ppermute(odd, ('depth', 'lat'), section_pairs(sections, pairs, 1))  3.38 us
  transfers between devices with their start and end apart: 30, of which 15 were waited for; matrix products, arithmetic and copies ran while one was open for 0% of the time, Pallas kernels for 12%

profile of v1, /device:TPU:16, one launch (start us, length us, event | category | flops | bytes accessed | tf_op | source)
XLA Modules:
  0.0 72.4 jit_solution(14053322176459643461)
XLA Ops:
  0.6 1.4 %shard_map.174 = (f32[128,256]{1,0:T(8,128)S(1)}, f32[128,256]{1,0:T(8,128)S(1)}, f32[128,256]{1,0:T(8,128)S(1)}, f32[128,256]{1,0:T(8,128)S(1)}, f32[64,256]{1,...) custom-call(f32[4,32,256]{2,1,0:T(8,128)} %dr.1, f32[4,32,256]{2,1,0:T(8,128)} %di.1, ...), custom_call_target="tpu_custom_call" | custom-call | tf_op jit(solution)/shard_map/pallas_call | solution.py:402
  2.0 1.6 %collective-permute-start = (f32[128,256]{1,0:T(8,128)S(1)}, f32[128,256]{1,0:T(8,128)S(1)}, u32[]{:S(2)}, u32[]{:S(2)}) collective-permute-start(f32[128,256]{1,0:T(8,128)S(1)} %get-tuple-element.54), channel_id=1, source_target_pairs={{0,2},{1,3},{2,0},{3,1},{4,6},{5,7},{6,4},{7,5},{8,10},{9,11},{10,... | collective-permute-start | bytes 393224 | tf_op jit(solution)/shard_map/ppermute | solution.py:426
  3.6 1.5 %collective-permute-start.1 = (f32[128,256]{1,0:T(8,128)S(1)}, f32[128,256]{1,0:T(8,128)S(1)}, u32[]{:S(2)}, u32[]{:S(2)}) collective-permute-start(f32[128,256]{1,0:T(8,128)S(1)} %get-tuple-element.55), channel_id=1, source_target_pairs={{0,4},{1,5},{2,6},{3,7},{4,0},{5,1},{6,2},{7,3},{8,12},{9,13},{10,... | collective-permute-start | bytes 393224 | tf_op jit(solution)/shard_map/ppermute | solution.py:426
  5.1 0.5 collective-permute-start.2
  5.6 2.2 %collective-permute-done.refs_1_ = f32[128,256]{1,0:T(8,128)S(1)} collective-permute-done((f32[128,256]{1,0:T(8,128)S(1)}, f32[128,256]{1,0:T(8,128)S(1)}, u32[]{:S(2)}, u32[]{:S(2)}) %collective-permute-start) | collective-permute-done | bytes 131104 | tf_op jit(solution)/shard_map/ppermute | solution.py:426
  7.7 3.6 %collective-permute-done.1.refs_2_ = f32[128,256]{1,0:T(8,128)S(1)} collective-permute-done((f32[128,256]{1,0:T(8,128)S(1)}, f32[128,256]{1,0:T(8,128)S(1)}, u32[]{:S(2)}, u32[]{:S(2)}) %collective-permute-start.1) | collective-permute-done | bytes 131104 | tf_op jit(solution)/shard_map/ppermute | solution.py:426
  11.4 1.0 %shard_map.179 = (f32[256,128]{1,0:T(8,128)S(1)}, f32[256,128]{1,0:T(8,128)S(1)}, f32[256,256]{1,0:T(8,128)}) custom-call(f32[128,256]{1,0:T(8,128)S(1)} %get-tuple-element.53.refs_0_, f32[128,256]{1,0:T(8,128)S(1)} %collective-permute-done.refs_1_, f32[128,256]{1,0:T(8,128)S(1)} %collective-permute-done.1.refs_2_, ...), custom_call_target="tpu_custom_call" | custom-call | tf_op jit(solution)/shard_map/pallas_call | solution.py:481
  12.7 0.6 collective-permute-start.3
  13.3 0.9 %shard_map.176.mult = f32[256,256]{1,0:T(8,128)S(1)} custom-call(f32[4]{0:T(128)S(1)} %copy-done.9), custom_call_target="tpu_custom_call" | custom-call | tf_op jit(solution)/shard_map/pallas_call | solution.py:436
  14.3 0.8 %shard_map.180 = (f32[256,128]{1,0:T(8,128)S(1)}, f32[256,128]{1,0:T(8,128)S(1)}) custom-call(f32[256,128]{1,0:T(8,128)S(1)} %get-tuple-element.66.keep, f32[256,128]{1,0:T(8,128)S(1)} %collective-permute-done.8.got, f32[256,256]{1,0:T(8,128)S(1)} %shard_map.176.mult, bf16[256,768]{1,0:T(8,128)(2,1)S(1)} %copy-done.2, bf16[256,768]{1,0:T(8,128)(2,1)S(1)} %copy-done.3, ...), custom_call_target="tpu_custom_call" | custom-call | tf_op jit(solution)/shard_map/pallas_call | solution.py:530
  15.0 0.6 collective-permute-start.9
  15.6 0.8 %shard_map.177 = (f32[256,128]{1,0:T(8,128)S(1)}, f32[256,128]{1,0:T(8,128)S(1)}) custom-call(f32[256,128]{1,0:T(8,128)S(1)} %get-tuple-element.57.keep, f32[256,128]{1,0:T(8,128)S(1)} %collective-permute-done.3.got, f32[256,256]{1,0:T(8,128)S(1)} %shard_map.176.mult, bf16[256,768]{1,0:T(8,128)(2,1)S(1)} %copy-done.2, bf16[256,768]{1,0:T(8,128)(2,1)S(1)} %copy-done.3, ...), custom_call_target="tpu_custom_call" | custom-call | tf_op jit(solution)/shard_map/pallas_call | solution.py:530
  16.5 1.2 %collective-permute-start.5 = (f32[64,256]{1,0:T(8,128)S(1)}, f32[64,256]{1,0:T(8,128)S(1)}, u32[]{:S(2)}, u32[]{:S(2)}) collective-permute-start(f32[64,256]{1,0:T(8,128)S(1)} %get-tuple-element.62), channel_id=1, source_target_pairs={{0,2},{1,3},{2,0},{3,1},{4,6},{5,7},{6,4},{7,5},{8,10},{9,11},{10,... | collective-permute-start | bytes 196616 | tf_op jit(solution)/shard_map/ppermute | solution.py:426
  17.7 0.8 %collective-permute-start.6 = (f32[64,256]{1,0:T(8,128)S(1)}, f32[64,256]{1,0:T(8,128)S(1)}, u32[]{:S(2)}, u32[]{:S(2)}) collective-permute-start(f32[64,256]{1,0:T(8,128)S(1)} %get-tuple-element.63), channel_id=1, source_target_pairs={{0,4},{1,5},{2,6},{3,7},{4,0},{5,1},{6,2},{7,3},{8,12},{9,13},{10,... | collective-permute-start | bytes 196616 | tf_op jit(solution)/shard_map/ppermute | solution.py:426
  18.6 1.4 %collective-permute-start.7 = (f32[64,256]{1,0:T(8,128)S(1)}, f32[64,256]{1,0:T(8,128)S(1)}, u32[]{:S(2)}, u32[]{:S(2)}) collective-permute-start(f32[64,256]{1,0:T(8,128)S(1)} %get-tuple-element.64), channel_id=1, source_target_pairs={{0,6},{1,7},{2,4},{3,5},{4,2},{5,3},{6,0},{7,1},{8,14},{9,15},{10,... | collective-permute-start | bytes 196616 | tf_op jit(solution)/shard_map/ppermute | solution.py:426
  20.0 0.9 %collective-permute-done.5.refs_1_ = f32[64,256]{1,0:T(8,128)S(1)} collective-permute-done((f32[64,256]{1,0:T(8,128)S(1)}, f32[64,256]{1,0:T(8,128)S(1)}, u32[]{:S(2)}, u32[]{:S(2)}) %collective-permute-start.5) | collective-permute-done | bytes 65568 | tf_op jit(solution)/shard_map/ppermute | solution.py:426
  21.0 1.1 %collective-permute-done.6.refs_2_ = f32[64,256]{1,0:T(8,128)S(1)} collective-permute-done((f32[64,256]{1,0:T(8,128)S(1)}, f32[64,256]{1,0:T(8,128)S(1)}, u32[]{:S(2)}, u32[]{:S(2)}) %collective-permute-start.6) | collective-permute-done | bytes 65568 | tf_op jit(solution)/shard_map/ppermute | solution.py:426
  22.0 1.7 %collective-permute-done.7.refs_3_ = f32[64,256]{1,0:T(8,128)S(1)} collective-permute-done((f32[64,256]{1,0:T(8,128)S(1)}, f32[64,256]{1,0:T(8,128)S(1)}, u32[]{:S(2)}, u32[]{:S(2)}) %collective-permute-start.7) | collective-permute-done | bytes 65568 | tf_op jit(solution)/shard_map/ppermute | solution.py:426
  23.7 0.7 %shard_map.178 = (f32[256,256]{1,0:T(8,128)S(1)}, f32[128,256]{1,0:T(8,128)S(1)}) custom-call(f32[64,256]{1,0:T(8,128)S(1)} %get-tuple-element.61.refs_0_, f32[64,256]{1,0:T(8,128)S(1)} %collective-permute-done.5.refs_1_, f32[64,256]{1,0:T(8,128)S(1)} %collective-permute-done.6.refs_2_, f32[64,256]{1,0:T(8,128)S(1)} %collective-permute-done.7.refs_3_, ...), custom_call_target="tpu_custom_call" | custom-call | tf_op jit(solution)/shard_map/pallas_call | solution.py:452
  25.2 1.5 %collective-permute-start.10 = (f32[256,256]{1,0:T(8,128)S(1)}, f32[256,256]{1,0:T(8,128)S(1)}, u32[]{:S(2)}, u32[]{:S(2)}) collective-permute-start(f32[256,256]{1,0:T(8,128)S(1)} %get-tuple-element.70), channel_id=1, source_target_pairs={{0,2},{2,0},{1,3},{3,1},{6,4},{4,6},{7,5},{5,7},{12,14},{14,12},{1... | collective-permute-start | bytes 786440 | tf_op jit(solution)/shard_map/ppermute | solution.py:587
  26.8 2.4 %collective-permute-start.11 = (f32[256,256]{1,0:T(8,128)S(1)}, f32[256,256]{1,0:T(8,128)S(1)}, u32[]{:S(2)}, u32[]{:S(2)}) collective-permute-start(f32[256,256]{1,0:T(8,128)S(1)} %get-tuple-element.71), channel_id=1, source_target_pairs={{2,6},{6,2},{3,7},{7,3},{4,12},{12,4},{5,13},{13,5},{14,10},{10,14... | collective-permute-start | bytes 786440 | tf_op jit(solution)/shard_map/ppermute | solution.py:588
  29.1 3.2 %collective-permute-done.10.ahead = f32[256,256]{1,0:T(8,128)S(1)} collective-permute-done((f32[256,256]{1,0:T(8,128)S(1)}, f32[256,256]{1,0:T(8,128)S(1)}, u32[]{:S(2)}, u32[]{:S(2)}) %collective-permute-start.10) | collective-permute-done | bytes 262176 | tf_op jit(solution)/shard_map/ppermute | solution.py:587
  32.3 3.0 %collective-permute-done.11.behind = f32[256,256]{1,0:T(8,128)S(1)} collective-permute-done((f32[256,256]{1,0:T(8,128)S(1)}, f32[256,256]{1,0:T(8,128)S(1)}, u32[]{:S(2)}, u32[]{:S(2)}) %collective-permute-start.11) | collective-permute-done | bytes 262176 | tf_op jit(solution)/shard_map/ppermute | solution.py:588
  36.0 0.6 collective-permute-start.12
  36.6 0.5 collective-permute-done.14.got
  37.0 0.8 %shard_map.186 = (f32[256,128]{1,0:T(8,128)S(1)}, f32[256,128]{1,0:T(8,128)S(1)}) custom-call(f32[256,128]{1,0:T(8,128)S(1)} %get-tuple-element.78.keep, f32[256,128]{1,0:T(8,128)S(1)} %collective-permute-done.14.got, f32[256,256]{1,0:T(8,128)S(1)} %shard_map.176.mult, bf16[256,768]{1,0:T(8,128)(2,1)S(1)} %copy-done.2, bf16[256,768]{1,0:T(8,128)(2,1)S(1)} %copy-done.3, ...), custom_call_target="tpu_custom_call" | custom-call | tf_op jit(solution)/shard_map/pallas_call | solution.py:530
  38.0 0.8 %shard_map.184 = (f32[256,128]{1,0:T(8,128)S(1)}, f32[256,128]{1,0:T(8,128)S(1)}) custom-call(f32[256,128]{1,0:T(8,128)S(1)} %get-tuple-element.74.keep, f32[256,128]{1,0:T(8,128)S(1)} %collective-permute-done.12.got, f32[256,256]{1,0:T(8,128)S(1)} %shard_map.176.mult, bf16[256,768]{1,0:T(8,128)(2,1)S(1)} %copy-done.2, bf16[256,768]{1,0:T(8,128)(2,1)S(1)} %copy-done.3, ...), custom_call_target="tpu_custom_call" | custom-call | tf_op jit(solution)/shard_map/pallas_call | solution.py:530
  39.5 0.6 collective-permute-done.13.got
  40.5 0.7 collective-permute-start.16
  41.2 2.4 %collective-permute-start.17 = (f32[256,256]{1,0:T(8,128)S(1)}, f32[256,256]{1,0:T(8,128)S(1)}, u32[]{:S(2)}, u32[]{:S(2)}) collective-permute-start(f32[256,256]{1,0:T(8,128)S(1)} %get-tuple-element.83), channel_id=1, source_target_pairs={{2,6},{6,2},{3,7},{7,3},{4,12},{12,4},{5,13},{13,5},{14,10},{10,14... | collective-permute-start | bytes 786440 | tf_op jit(solution)/shard_map/ppermute | solution.py:588
  43.6 5.6 %collective-permute-done.16.ahead = f32[256,256]{1,0:T(8,128)S(1)} collective-permute-done((f32[256,256]{1,0:T(8,128)S(1)}, f32[256,256]{1,0:T(8,128)S(1)}, u32[]{:S(2)}, u32[]{:S(2)}) %collective-permute-start.16) | collective-permute-done | bytes 262176 | tf_op jit(solution)/shard_map/ppermute | solution.py:587
  49.2 2.2 %collective-permute-done.17.behind = f32[256,256]{1,0:T(8,128)S(1)} collective-permute-done((f32[256,256]{1,0:T(8,128)S(1)}, f32[256,256]{1,0:T(8,128)S(1)}, u32[]{:S(2)}, u32[]{:S(2)}) %collective-permute-start.17) | collective-permute-done | bytes 262176 | tf_op jit(solution)/shard_map/ppermute | solution.py:588
  52.1 0.6 collective-permute-start.18
  52.6 0.5 collective-permute-done.23.got
  53.1 0.8 %shard_map.193 = (f32[256,128]{1,0:T(8,128)S(1)}, f32[256,128]{1,0:T(8,128)S(1)}) custom-call(f32[256,128]{1,0:T(8,128)S(1)} %get-tuple-element.92.keep, f32[256,128]{1,0:T(8,128)S(1)} %collective-permute-done.23.got, f32[256,256]{1,0:T(8,128)S(1)} %shard_map.176.mult, bf16[256,768]{1,0:T(8,128)(2,1)S(1)} %copy-done.2, bf16[256,768]{1,0:T(8,128)(2,1)S(1)} %copy-done.3, ...), custom_call_target="tpu_custom_call" | custom-call | tf_op jit(solution)/shard_map/pallas_call | solution.py:530
  54.1 0.8 %shard_map.190 = (f32[256,128]{1,0:T(8,128)S(1)}, f32[256,128]{1,0:T(8,128)S(1)}) custom-call(f32[256,128]{1,0:T(8,128)S(1)} %get-tuple-element.84.keep, f32[256,128]{1,0:T(8,128)S(1)} %collective-permute-done.18.got, f32[256,256]{1,0:T(8,128)S(1)} %shard_map.176.mult, bf16[256,768]{1,0:T(8,128)(2,1)S(1)} %copy-done.2, bf16[256,768]{1,0:T(8,128)(2,1)S(1)} %copy-done.3, ...), custom_call_target="tpu_custom_call" | custom-call | tf_op jit(solution)/shard_map/pallas_call | solution.py:530
  55.6 1.5 %collective-permute-start.25 = (f32[64,256]{1,0:T(8,128)S(1)}, f32[64,256]{1,0:T(8,128)S(1)}, u32[]{:S(2)}, u32[]{:S(2)}) collective-permute-start(f32[64,256]{1,0:T(8,128)S(1)} %get-tuple-element.97), channel_id=1, source_target_pairs={{0,2},{1,3},{2,0},{3,1},{4,6},{5,7},{6,4},{7,5},{8,10},{9,11},{10,... | collective-permute-start | bytes 196616 | tf_op jit(solution)/shard_map/ppermute | solution.py:426
  57.1 0.6 collective-permute-start.26
  57.7 1.4 %collective-permute-start.27 = (f32[64,256]{1,0:T(8,128)S(1)}, f32[64,256]{1,0:T(8,128)S(1)}, u32[]{:S(2)}, u32[]{:S(2)}) collective-permute-start(f32[64,256]{1,0:T(8,128)S(1)} %get-tuple-element.99), channel_id=1, source_target_pairs={{0,6},{1,7},{2,4},{3,5},{4,2},{5,3},{6,0},{7,1},{8,14},{9,15},{10,... | collective-permute-start | bytes 196616 | tf_op jit(solution)/shard_map/ppermute | solution.py:426
  59.5 1.5 %collective-permute-start.20 = (f32[64,256]{1,0:T(8,128)S(1)}, f32[64,256]{1,0:T(8,128)S(1)}, u32[]{:S(2)}, u32[]{:S(2)}) collective-permute-start(f32[64,256]{1,0:T(8,128)S(1)} %get-tuple-element.89), channel_id=1, source_target_pairs={{0,2},{1,3},{2,0},{3,1},{4,6},{5,7},{6,4},{7,5},{8,10},{9,11},{10,... | collective-permute-start | bytes 196616 | tf_op jit(solution)/shard_map/ppermute | solution.py:426
  61.0 0.6 collective-permute-start.21
  61.7 1.4 %collective-permute-start.22 = (f32[64,256]{1,0:T(8,128)S(1)}, f32[64,256]{1,0:T(8,128)S(1)}, u32[]{:S(2)}, u32[]{:S(2)}) collective-permute-start(f32[64,256]{1,0:T(8,128)S(1)} %get-tuple-element.91), channel_id=1, source_target_pairs={{0,6},{1,7},{2,4},{3,5},{4,2},{5,3},{6,0},{7,1},{8,14},{9,15},{10,... | collective-permute-start | bytes 196616 | tf_op jit(solution)/shard_map/ppermute | solution.py:426
  63.1 0.5 collective-permute-done.27.refs_3_.refs_7_
  63.7 1.6 %collective-permute-start.28 = (f32[64,256]{1,0:T(8,128)S(1)}, f32[64,256]{1,0:T(8,128)S(1)}, u32[]{:S(2)}, u32[]{:S(2)}) collective-permute-start(f32[64,256]{1,0:T(8,128)S(1)} %get-tuple-element.100), channel_id=1, source_target_pairs={{0,8},{8,0},{1,9},{9,1},{2,10},{10,2},{3,11},{11,3},{4,12},{12,4},... | collective-permute-start | bytes 196616 | tf_op jit(solution)/shard_map/ppermute | solution.py:614
  65.2 1.9 %collective-permute-start.29 = (f32[64,256]{1,0:T(8,128)S(1)}, f32[64,256]{1,0:T(8,128)S(1)}, u32[]{:S(2)}, u32[]{:S(2)}) collective-permute-start(f32[64,256]{1,0:T(8,128)S(1)} %get-tuple-element.101), channel_id=1, source_target_pairs={{8,16},{16,8},{9,17},{17,9},{10,18},{18,10},{11,19},{19,11},{12,20... | collective-permute-start | bytes 196616 | tf_op jit(solution)/shard_map/ppermute | solution.py:615
  67.2 0.8 %collective-permute-done.28.refs_8_ = f32[64,256]{1,0:T(8,128)S(1)} collective-permute-done((f32[64,256]{1,0:T(8,128)S(1)}, f32[64,256]{1,0:T(8,128)S(1)}, u32[]{:S(2)}, u32[]{:S(2)}) %collective-permute-start.28) | collective-permute-done | bytes 65568 | tf_op jit(solution)/shard_map/ppermute | solution.py:614
  68.0 3.4 %collective-permute-done.29.refs_9_ = f32[64,256]{1,0:T(8,128)S(1)} collective-permute-done((f32[64,256]{1,0:T(8,128)S(1)}, f32[64,256]{1,0:T(8,128)S(1)}, u32[]{:S(2)}, u32[]{:S(2)}) %collective-permute-start.29) | collective-permute-done | bytes 65568 | tf_op jit(solution)/shard_map/ppermute | solution.py:615
  71.4 1.0 %shard_map.196 = (f32[4,32,256]{2,1,0:T(8,128)}, f32[4,32,256]{2,1,0:T(8,128)}, f32[4,32,256]{2,1,0:T(8,128)}, f32[4,32,256]{2,1,0:T(8,128)}) custom-call(f32[64,256]{1,0:T(8,128)S(1)} %get-tuple-element.88.refs_0_, f32[64,256]{1,0:T(8,128)S(1)} %collective-permute-done.20.refs_1_, f32[64,256]{1,0:T(8,128)S(1)} %collective-permute-done.21.refs_2_, ...), custom_call_target="tpu_custom_call" | custom-call | tf_op jit(solution)/shard_map/pallas_call | solution.py:661
  (55 shorter events, 5.3 us)
Async XLA Ops:
  0.6 10.7 %copy-start.1 = (bf16[768,256]{1,0:T(8,128)(2,1)S(1)}, bf16[768,256]{1,0:T(8,128)(2,1)}, u32[]{:S(2)}) copy-start(bf16[768,256]{1,0:T(8,128)(2,1)} %constant.12.clone.refs_4_.table) | copy-start | bytes 1179652
  2.0 5.7 %collective-permute-start = (f32[128,256]{1,0:T(8,128)S(1)}, f32[128,256]{1,0:T(8,128)S(1)}, u32[]{:S(2)}, u32[]{:S(2)}) collective-permute-start(f32[128,256]{1,0:T(8,128)S(1)} %get-tuple-element.54), channel_id=1, source_target_pairs={{0,2},{1,3},{2,0},{3,1},{4,6},{5,7},{6,4},{7,5},{8,10},{9,11},{10,... | collective-permute-start | bytes 393224 | tf_op jit(solution)/shard_map/ppermute | solution.py:426
  3.6 7.8 %collective-permute-start.1 = (f32[128,256]{1,0:T(8,128)S(1)}, f32[128,256]{1,0:T(8,128)S(1)}, u32[]{:S(2)}, u32[]{:S(2)}) collective-permute-start(f32[128,256]{1,0:T(8,128)S(1)} %get-tuple-element.55), channel_id=1, source_target_pairs={{0,4},{1,5},{2,6},{3,7},{4,0},{5,1},{6,2},{7,3},{8,12},{9,13},{10,... | collective-permute-start | bytes 393224 | tf_op jit(solution)/shard_map/ppermute | solution.py:426
  5.1 6.3 %copy-start.6 = (f32[2,128]{1,0:T(2,128)S(1)}, f32[2,128]{1,0:T(2,128)}, u32[]{:S(2)}) copy-start(f32[2,128]{1,0:T(2,128)} %constant.16.clone.refs_5_.refs_1_.refs_2_.turn) | copy-start | bytes 3076
  5.1 6.3 %collective-permute-start.2 = (f32[128,256]{1,0:T(8,128)S(1)}, f32[128,256]{1,0:T(8,128)S(1)}, u32[]{:S(2)}, u32[]{:S(2)}) collective-permute-start(f32[128,256]{1,0:T(8,128)S(1)} %get-tuple-element.56), channel_id=1, source_target_pairs={{0,6},{1,7},{2,4},{3,5},{4,2},{5,3},{6,0},{7,1},{8,14},{9,15},{10,... | collective-permute-start | bytes 393224 | tf_op jit(solution)/shard_map/ppermute | solution.py:426
  12.4 1.9 %copy-start.2 = (bf16[256,768]{1,0:T(8,128)(2,1)S(1)}, bf16[256,768]{1,0:T(8,128)(2,1)}, u32[]{:S(2)}) copy-start(bf16[256,768]{1,0:T(8,128)(2,1)} %constant.14.clone.table) | copy-start | bytes 1179652
  12.4 1.9 %copy-start.3 = (bf16[256,768]{1,0:T(8,128)(2,1)S(1)}, bf16[256,768]{1,0:T(8,128)(2,1)}, u32[]{:S(2)}) copy-start(bf16[256,768]{1,0:T(8,128)(2,1)} %constant.15.clone.back) | copy-start | bytes 1179652
  12.4 1.9 %collective-permute-start.8 = (f32[256,128]{1,0:T(8,128)S(1)}, f32[256,128]{1,0:T(8,128)S(1)}, u32[]{:S(2)}, u32[]{:S(2)}) collective-permute-start(f32[256,128]{1,0:T(8,128)S(1)} %get-tuple-element.67), channel_id=1, source_target_pairs={{0,1},{1,0},{2,3},{3,2},{4,5},{5,4},{6,7},{7,6},{8,9},{9,8},{10,11... | collective-permute-start | bytes 393224 | tf_op jit(solution)/shard_map/ppermute | solution.py:574
  12.7 0.7 copy-start.9
  12.7 1.6 %copy-start.4 = (f32[2,128,128]{2,1,0:T(8,128)S(1)}, f32[2,128,128]{2,1,0:T(8,128)}, u32[]{:S(2)}) copy-start(f32[2,128,128]{2,1,0:T(8,128)} %constant.17.clone.turn) | copy-start | bytes 393220
  12.7 2.9 %collective-permute-start.3 = (f32[256,128]{1,0:T(8,128)S(1)}, f32[256,128]{1,0:T(8,128)S(1)}, u32[]{:S(2)}, u32[]{:S(2)}) collective-permute-start(f32[256,128]{1,0:T(8,128)S(1)} %get-tuple-element.58), channel_id=1, source_target_pairs={{0,1},{1,0},{2,3},{3,2},{4,5},{5,4},{6,7},{7,6},{8,9},{9,8},{10,11... | collective-permute-start | bytes 393224 | tf_op jit(solution)/shard_map/ppermute | solution.py:574
  15.0 9.5 %collective-permute-start.9 = (f32[256,128]{1,0:T(8,128)S(1)}, f32[256,128]{1,0:T(8,128)S(1)}, u32[]{:S(2)}, u32[]{:S(2)}) collective-permute-start(f32[256,128]{1,0:T(8,128)S(1)} %get-tuple-element.69), channel_id=1, source_target_pairs={{0,1},{1,0},{2,3},{3,2},{4,5},{5,4},{6,7},{7,6},{8,9},{9,8},{10,11... | collective-permute-start | bytes 393224 | tf_op jit(solution)/shard_map/ppermute | solution.py:574
  15.6 8.9 %copy-start = (bf16[768,256]{1,0:T(8,128)(2,1)S(1)}, bf16[768,256]{1,0:T(8,128)(2,1)}, u32[]{:S(2)}) copy-start(bf16[768,256]{1,0:T(8,128)(2,1)} %constant.13.clone.refs_0_.refs_1_.table) | copy-start | bytes 1179652
  16.4 8.5 %collective-permute-start.4 = (f32[256,128]{1,0:T(8,128)S(1)}, f32[256,128]{1,0:T(8,128)S(1)}, u32[]{:S(2)}, u32[]{:S(2)}) collective-permute-start(f32[256,128]{1,0:T(8,128)S(1)} %get-tuple-element.60), channel_id=1, source_target_pairs={{0,1},{1,0},{2,3},{3,2},{4,5},{5,4},{6,7},{7,6},{8,9},{9,8},{10,11... | collective-permute-start | bytes 393224 | tf_op jit(solution)/shard_map/ppermute | solution.py:574
  16.5 4.5 %collective-permute-start.5 = (f32[64,256]{1,0:T(8,128)S(1)}, f32[64,256]{1,0:T(8,128)S(1)}, u32[]{:S(2)}, u32[]{:S(2)}) collective-permute-start(f32[64,256]{1,0:T(8,128)S(1)} %get-tuple-element.62), channel_id=1, source_target_pairs={{0,2},{1,3},{2,0},{3,1},{4,6},{5,7},{6,4},{7,5},{8,10},{9,11},{10,... | collective-permute-start | bytes 196616 | tf_op jit(solution)/shard_map/ppermute | solution.py:426
  17.7 4.3 %collective-permute-start.6 = (f32[64,256]{1,0:T(8,128)S(1)}, f32[64,256]{1,0:T(8,128)S(1)}, u32[]{:S(2)}, u32[]{:S(2)}) collective-permute-start(f32[64,256]{1,0:T(8,128)S(1)} %get-tuple-element.63), channel_id=1, source_target_pairs={{0,4},{1,5},{2,6},{3,7},{4,0},{5,1},{6,2},{7,3},{8,12},{9,13},{10,... | collective-permute-start | bytes 196616 | tf_op jit(solution)/shard_map/ppermute | solution.py:426
  18.6 5.2 %collective-permute-start.7 = (f32[64,256]{1,0:T(8,128)S(1)}, f32[64,256]{1,0:T(8,128)S(1)}, u32[]{:S(2)}, u32[]{:S(2)}) collective-permute-start(f32[64,256]{1,0:T(8,128)S(1)} %get-tuple-element.64), channel_id=1, source_target_pairs={{0,6},{1,7},{2,4},{3,5},{4,2},{5,3},{6,0},{7,1},{8,14},{9,15},{10,... | collective-permute-start | bytes 196616 | tf_op jit(solution)/shard_map/ppermute | solution.py:426
  25.2 7.1 %collective-permute-start.10 = (f32[256,256]{1,0:T(8,128)S(1)}, f32[256,256]{1,0:T(8,128)S(1)}, u32[]{:S(2)}, u32[]{:S(2)}) collective-permute-start(f32[256,256]{1,0:T(8,128)S(1)} %get-tuple-element.70), channel_id=1, source_target_pairs={{0,2},{2,0},{1,3},{3,1},{6,4},{4,6},{7,5},{5,7},{12,14},{14,12},{1... | collective-permute-start | bytes 786440 | tf_op jit(solution)/shard_map/ppermute | solution.py:587
  26.8 8.5 %collective-permute-start.11 = (f32[256,256]{1,0:T(8,128)S(1)}, f32[256,256]{1,0:T(8,128)S(1)}, u32[]{:S(2)}, u32[]{:S(2)}) collective-permute-start(f32[256,256]{1,0:T(8,128)S(1)} %get-tuple-element.71), channel_id=1, source_target_pairs={{2,6},{6,2},{3,7},{7,3},{4,12},{12,4},{5,13},{13,5},{14,10},{10,14... | collective-permute-start | bytes 786440 | tf_op jit(solution)/shard_map/ppermute | solution.py:588
  35.6 1.4 %collective-permute-start.14 = (f32[256,128]{1,0:T(8,128)S(1)}, f32[256,128]{1,0:T(8,128)S(1)}, u32[]{:S(2)}, u32[]{:S(2)}) collective-permute-start(f32[256,128]{1,0:T(8,128)S(1)} %get-tuple-element.79), channel_id=1, source_target_pairs={{0,1},{1,0},{2,3},{3,2},{4,5},{5,4},{6,7},{7,6},{8,9},{9,8},{10,11... | collective-permute-start | bytes 393224 | tf_op jit(solution)/shard_map/ppermute | solution.py:574
  36.0 2.0 %collective-permute-start.12 = (f32[256,128]{1,0:T(8,128)S(1)}, f32[256,128]{1,0:T(8,128)S(1)}, u32[]{:S(2)}, u32[]{:S(2)}) collective-permute-start(f32[256,128]{1,0:T(8,128)S(1)} %get-tuple-element.75), channel_id=1, source_target_pairs={{0,1},{1,0},{2,3},{3,2},{4,5},{5,4},{6,7},{7,6},{8,9},{9,8},{10,11... | collective-permute-start | bytes 393224 | tf_op jit(solution)/shard_map/ppermute | solution.py:574
  37.8 1.4 %collective-permute-start.15 = (f32[256,128]{1,0:T(8,128)S(1)}, f32[256,128]{1,0:T(8,128)S(1)}, u32[]{:S(2)}, u32[]{:S(2)}) collective-permute-start(f32[256,128]{1,0:T(8,128)S(1)} %get-tuple-element.81), channel_id=1, source_target_pairs={{0,1},{1,0},{2,3},{3,2},{4,5},{5,4},{6,7},{7,6},{8,9},{9,8},{10,11... | collective-permute-start | bytes 393224 | tf_op jit(solution)/shard_map/ppermute | solution.py:574
  38.8 1.4 %collective-permute-start.13 = (f32[256,128]{1,0:T(8,128)S(1)}, f32[256,128]{1,0:T(8,128)S(1)}, u32[]{:S(2)}, u32[]{:S(2)}) collective-permute-start(f32[256,128]{1,0:T(8,128)S(1)} %get-tuple-element.77), channel_id=1, source_target_pairs={{0,1},{1,0},{2,3},{3,2},{4,5},{5,4},{6,7},{7,6},{8,9},{9,8},{10,11... | collective-permute-start | bytes 393224 | tf_op jit(solution)/shard_map/ppermute | solution.py:574
  40.5 8.6 %collective-permute-start.16 = (f32[256,256]{1,0:T(8,128)S(1)}, f32[256,256]{1,0:T(8,128)S(1)}, u32[]{:S(2)}, u32[]{:S(2)}) collective-permute-start(f32[256,256]{1,0:T(8,128)S(1)} %get-tuple-element.82), channel_id=1, source_target_pairs={{0,2},{2,0},{1,3},{3,1},{6,4},{4,6},{7,5},{5,7},{12,14},{14,12},{1... | collective-permute-start | bytes 786440 | tf_op jit(solution)/shard_map/ppermute | solution.py:587
  41.2 10.2 %collective-permute-start.17 = (f32[256,256]{1,0:T(8,128)S(1)}, f32[256,256]{1,0:T(8,128)S(1)}, u32[]{:S(2)}, u32[]{:S(2)}) collective-permute-start(f32[256,256]{1,0:T(8,128)S(1)} %get-tuple-element.83), channel_id=1, source_target_pairs={{2,6},{6,2},{3,7},{7,3},{4,12},{12,4},{5,13},{13,5},{14,10},{10,14... | collective-permute-start | bytes 786440 | tf_op jit(solution)/shard_map/ppermute | solution.py:588
  51.7 1.4 %collective-permute-start.23 = (f32[256,128]{1,0:T(8,128)S(1)}, f32[256,128]{1,0:T(8,128)S(1)}, u32[]{:S(2)}, u32[]{:S(2)}) collective-permute-start(f32[256,128]{1,0:T(8,128)S(1)} %get-tuple-element.93), channel_id=1, source_target_pairs={{0,1},{1,0},{2,3},{3,2},{4,5},{5,4},{6,7},{7,6},{8,9},{9,8},{10,11... | collective-permute-start | bytes 393224 | tf_op jit(solution)/shard_map/ppermute | solution.py:574
  52.1 2.0 %collective-permute-start.18 = (f32[256,128]{1,0:T(8,128)S(1)}, f32[256,128]{1,0:T(8,128)S(1)}, u32[]{:S(2)}, u32[]{:S(2)}) collective-permute-start(f32[256,128]{1,0:T(8,128)S(1)} %get-tuple-element.85), channel_id=1, source_target_pairs={{0,1},{1,0},{2,3},{3,2},{4,5},{5,4},{6,7},{7,6},{8,9},{9,8},{10,11... | collective-permute-start | bytes 393224 | tf_op jit(solution)/shard_map/ppermute | solution.py:574
  53.9 1.4 %collective-permute-start.24 = (f32[256,128]{1,0:T(8,128)S(1)}, f32[256,128]{1,0:T(8,128)S(1)}, u32[]{:S(2)}, u32[]{:S(2)}) collective-permute-start(f32[256,128]{1,0:T(8,128)S(1)} %get-tuple-element.95), channel_id=1, source_target_pairs={{0,1},{1,0},{2,3},{3,2},{4,5},{5,4},{6,7},{7,6},{8,9},{9,8},{10,11... | collective-permute-start | bytes 393224 | tf_op jit(solution)/shard_map/ppermute | solution.py:574
  54.8 4.3 %collective-permute-start.19 = (f32[256,128]{1,0:T(8,128)S(1)}, f32[256,128]{1,0:T(8,128)S(1)}, u32[]{:S(2)}, u32[]{:S(2)}) collective-permute-start(f32[256,128]{1,0:T(8,128)S(1)} %get-tuple-element.87), channel_id=1, source_target_pairs={{0,1},{1,0},{2,3},{3,2},{4,5},{5,4},{6,7},{7,6},{8,9},{9,8},{10,11... | collective-permute-start | bytes 393224 | tf_op jit(solution)/shard_map/ppermute | solution.py:574
  55.6 6.0 %collective-permute-start.25 = (f32[64,256]{1,0:T(8,128)S(1)}, f32[64,256]{1,0:T(8,128)S(1)}, u32[]{:S(2)}, u32[]{:S(2)}) collective-permute-start(f32[64,256]{1,0:T(8,128)S(1)} %get-tuple-element.97), channel_id=1, source_target_pairs={{0,2},{1,3},{2,0},{3,1},{4,6},{5,7},{6,4},{7,5},{8,10},{9,11},{10,... | collective-permute-start | bytes 196616 | tf_op jit(solution)/shard_map/ppermute | solution.py:426
  57.1 6.0 %collective-permute-start.26 = (f32[64,256]{1,0:T(8,128)S(1)}, f32[64,256]{1,0:T(8,128)S(1)}, u32[]{:S(2)}, u32[]{:S(2)}) collective-permute-start(f32[64,256]{1,0:T(8,128)S(1)} %get-tuple-element.98), channel_id=1, source_target_pairs={{0,4},{1,5},{2,6},{3,7},{4,0},{5,1},{6,2},{7,3},{8,12},{9,13},{10,... | collective-permute-start | bytes 196616 | tf_op jit(solution)/shard_map/ppermute | solution.py:426
  57.7 5.8 %collective-permute-start.27 = (f32[64,256]{1,0:T(8,128)S(1)}, f32[64,256]{1,0:T(8,128)S(1)}, u32[]{:S(2)}, u32[]{:S(2)}) collective-permute-start(f32[64,256]{1,0:T(8,128)S(1)} %get-tuple-element.99), channel_id=1, source_target_pairs={{0,6},{1,7},{2,4},{3,5},{4,2},{5,3},{6,0},{7,1},{8,14},{9,15},{10,... | collective-permute-start | bytes 196616 | tf_op jit(solution)/shard_map/ppermute | solution.py:426
  59.5 7.6 %collective-permute-start.20 = (f32[64,256]{1,0:T(8,128)S(1)}, f32[64,256]{1,0:T(8,128)S(1)}, u32[]{:S(2)}, u32[]{:S(2)}) collective-permute-start(f32[64,256]{1,0:T(8,128)S(1)} %get-tuple-element.89), channel_id=1, source_target_pairs={{0,2},{1,3},{2,0},{3,1},{4,6},{5,7},{6,4},{7,5},{8,10},{9,11},{10,... | collective-permute-start | bytes 196616 | tf_op jit(solution)/shard_map/ppermute | solution.py:426
  61.0 6.1 %collective-permute-start.21 = (f32[64,256]{1,0:T(8,128)S(1)}, f32[64,256]{1,0:T(8,128)S(1)}, u32[]{:S(2)}, u32[]{:S(2)}) collective-permute-start(f32[64,256]{1,0:T(8,128)S(1)} %get-tuple-element.90), channel_id=1, source_target_pairs={{0,4},{1,5},{2,6},{3,7},{4,0},{5,1},{6,2},{7,3},{8,12},{9,13},{10,... | collective-permute-start | bytes 196616 | tf_op jit(solution)/shard_map/ppermute | solution.py:426
  61.7 5.5 %collective-permute-start.22 = (f32[64,256]{1,0:T(8,128)S(1)}, f32[64,256]{1,0:T(8,128)S(1)}, u32[]{:S(2)}, u32[]{:S(2)}) collective-permute-start(f32[64,256]{1,0:T(8,128)S(1)} %get-tuple-element.91), channel_id=1, source_target_pairs={{0,6},{1,7},{2,4},{3,5},{4,2},{5,3},{6,0},{7,1},{8,14},{9,15},{10,... | collective-permute-start | bytes 196616 | tf_op jit(solution)/shard_map/ppermute | solution.py:426
  63.6 7.8 %copy-start.5 = (f32[4,32,256]{2,1,0:T(8,128)S(1)}, f32[4,32,256]{2,1,0:T(8,128)}, u32[]{:S(2)}) copy-start(f32[4,32,256]{2,1,0:T(8,128)} %refs_10_.1) | copy-start | bytes 393220
  63.6 7.8 %copy-start.7 = (f32[32,256]{1,0:T(8,128)S(1)}, f32[32,256]{1,0:T(8,128)}, u32[]{:S(2)}) copy-start(f32[32,256]{1,0:T(8,128)} %refs_11_.1) | copy-start | bytes 98308
  63.6 7.8 %copy-start.8 = (f32[32,256]{1,0:T(8,128)S(1)}, f32[32,256]{1,0:T(8,128)}, u32[]{:S(2)}) copy-start(f32[32,256]{1,0:T(8,128)} %refs_12_.1) | copy-start | bytes 98308
  63.7 4.3 %collective-permute-start.28 = (f32[64,256]{1,0:T(8,128)S(1)}, f32[64,256]{1,0:T(8,128)S(1)}, u32[]{:S(2)}, u32[]{:S(2)}) collective-permute-start(f32[64,256]{1,0:T(8,128)S(1)} %get-tuple-element.100), channel_id=1, source_target_pairs={{0,8},{8,0},{1,9},{9,1},{2,10},{10,2},{3,11},{11,3},{4,12},{12,4},... | collective-permute-start | bytes 196616 | tf_op jit(solution)/shard_map/ppermute | solution.py:614
  65.2 6.1 %collective-permute-start.29 = (f32[64,256]{1,0:T(8,128)S(1)}, f32[64,256]{1,0:T(8,128)S(1)}, u32[]{:S(2)}, u32[]{:S(2)}) collective-permute-start(f32[64,256]{1,0:T(8,128)S(1)} %get-tuple-element.101), channel_id=1, source_target_pairs={{8,16},{16,8},{9,17},{17,9},{10,18},{18,10},{11,19},{19,11},{12,20... | collective-permute-start | bytes 196616 | tf_op jit(solution)/shard_map/ppermute | solution.py:615

commit v2 on v1

--- a/solution.py
+++ b/solution.py
@@ -311,7 +311,10 @@
     memory = {"v": pltpu.VMEM, "s": pltpu.SMEM, "h": pltpu.HBM}
     return pl.pallas_call(
         body,
-        out_shape=[jax.ShapeDtypeStruct(shape, jnp.float32) for shape in out_shapes],
+        out_shape=[
+            jax.ShapeDtypeStruct(shape, jnp.float32) if isinstance(shape, tuple) else shape
+            for shape in out_shapes
+        ],
         in_specs=[pl.BlockSpec(memory_space=memory[space]) for space in spaces],
         out_specs=[pl.BlockSpec(memory_space=pltpu.VMEM) for _ in out_shapes],
         scratch_shapes=list(scratch),
@@ -429,19 +432,22 @@
     planes = exchanged(outs[:pairs])
     media = exchanged(outs[pairs:])
 
-    def multiplier_body(ref_slow, out):
+    def factor_body(ref_slow, out, ref):
         here = Place(pairs)
-        out[:tall], out[tall:] = multiplier(ref_slow[here.level], rows, columns, here.core)
-
-    mult = local_call(multiplier_body, [local], "s")(ref_slow)[0]
+        value = ref_slow[here.level]
+        out[:tall], out[tall:] = multiplier(value, rows, columns, here.core)
+        ref[...] = jnp.full((block, columns), value, f32)
+
+    mult, ref_here = local_call(factor_body, [local, (block, columns)], "s")(
+        ref_slow
+    )
 
     def media_body(*refs):
-        pieces, ref_slow, corr, refl = refs[:pairs], refs[pairs], refs[pairs + 1], refs[pairs + 2]
+        pieces, (ref, corr, refl) = refs[:pairs], refs[pairs:]
         here = Place(pairs)
-        ref = ref_slow[here.level]
         for step in range(pairs):
             start = (here.pair ^ step) * block
-            theta = (pieces[step][pl.ds(0, block), :] - ref) * (OMEGA * DEPTH_STEP)
+            theta = (pieces[step][pl.ds(0, block), :] - ref[...]) * (OMEGA * DEPTH_STEP)
             cosine, sine = cos_sin(theta)
             corr[pl.ds(pl.multiple_of(start, block), block), :] = cosine
             corr[pl.ds(pl.multiple_of(tall + start, block), block), :] = sine
@@ -449,8 +455,8 @@
                 pl.ds(block, block), :
             ]
 
-    corr, refl = local_call(media_body, [local, (tall, columns)], "v" * pairs + "s")(
-        *media, ref_slow
+    corr, refl = local_call(media_body, [local, (tall, columns)], "v" * pairs + "v")(
+        *media, ref_here
     )
 
     def shared(first, second, here, keep, send):
@@ -478,7 +484,12 @@
                     ]
             shared(*forward_y(whole[:tall], whole[tall:], table, turn), here, keep, send)
 
-        return local_call(body, [part, part, local], "v" * (pairs + 2))(*planes, y_table, y_turn)
+        outs, scratch = [part, part], [pltpu.VMEM(local, f32)]
+        if which == 1:
+            outs, scratch = outs + [local], []
+        return local_call(body, outs, "v" * (pairs + 2), scratch)(
+            *planes, y_table, y_turn
+        )
 
     def mixed(which, ahead, behind, source):
         def body(ahead, behind, source, refl, table, turn, keep, send):
@@ -540,18 +551,14 @@
         cosine, sine = corr[:tall], corr[tall:]
         return real * cosine + imag * sine, imag * cosine - real * sine
 
-    def leave(keep, got, *held):
-        def body(keep, got, corr, *refs):
-            kept, (table, turn), outs = refs[: len(held)], refs[len(held) :][:2], refs[2 + len(held) :]
-            whole = outs[-1]
-            for source, target in zip(kept, outs[1:]):
-                target[...] = source[...]
+    def leave(keep, got):
+        def body(keep, got, corr, table, turn, out, whole):
             real, imag = corrected(keep, got, corr, table, turn, Place(pairs), whole)
-            outs[0][:tall], outs[0][tall:] = real, imag
-
-        return local_call(
-            body, [local] * (1 + len(held)), "v" * (5 + len(held)), [pltpu.VMEM(local, f32)]
-        )(keep, got, corr, *held, y_back, y_turn)
+            out[:tall], out[tall:] = real, imag
+
+        return local_call(body, [local], "v" * 5, [pltpu.VMEM(local, f32)])(
+            keep, got, corr, y_back, y_turn
+        )[0]
 
     def leave_last(keep, got):
         def body(keep, got, corr, table, turn, *refs):
@@ -573,7 +580,7 @@
     def crossed(value):
         return lax.ppermute(value, "lat", swap)
 
-    keep0, send0, _ = enter(0)
+    keep0, send0 = enter(0)
     got0 = crossed(send0)
     keep1, send1, source = enter(1)
     got1 = crossed(send1)
@@ -582,9 +589,9 @@
         got0 = crossed(send0)
         keep1, send1 = column(keep1, got1)
         got1 = crossed(send1)
-        first = leave(keep0, got0)[0]
-        second, first = leave(keep1, got1, first)
+        first = leave(keep0, got0)
         ahead = lax.ppermute(first, ("depth", "lat"), level_pairs(sections, pairs, 0))
+        second = leave(keep1, got1)
         behind = lax.ppermute(second, ("depth", "lat"), level_pairs(sections, pairs, 1))
         keep1, send1 = mixed(1, ahead, behind, source)
         got1 = crossed(send1)

time: 72.5 us -> 70.6 us (0.974)
  Pallas kernels: 13.1 us -> 11.8 us
  waiting for transfers between devices: 29.8 us -> 28.9 us
    pallas_call x8, Pallas kernels: 4.27 us -> 2.95 us  [the longest x4 1.3 us: leave(): local_call(body, [local], 'v' * 5, [pltpu.VMEM(local, f32)])]
    ppermute x2, waiting for transfers between devices: 5.23 us -> 6.38 us  [plane_shards(): lax.ppermute(second, ('depth', 'lat'), level_pairs(sections, pairs, 1))]
    ppermute x2, waiting for transfers between devices: 8.76 us -> 7.86 us  [plane_shards(): lax.ppermute(first, ('depth', 'lat'), level_pairs(sections, pairs, 0))]
  transfers between devices with their start and end apart: 30 -> 30, of which waited for: 15 -> 13; matrix products, arithmetic and copies ran while one was open for 0% -> 0% of each run, Pallas kernels for 12% -> 12%
where the time goes in v2:
time: 70.6 us; the launch traced here: 70.4 us
  waiting for transfers between devices  28.9 us (41%)
  starting transfers between devices  28.6 us (41%)
  Pallas kernels  11.8 us (17%)
  between operations  0.99 us (1%)
    ppermute x12, starting transfers between devices, exchanged(): moved.append(lax.ppermute(pieces[step], 'lat', across(step)))  14.2 us
    ppermute x12, waiting for transfers between devices, exchanged(): moved.append(lax.ppermute(pieces[step], 'lat', across(step)))  9.54 us
    ppermute x2, waiting for transfers between devices, plane_shards(): lax.ppermute(first, ('depth', 'lat'), level_pairs(sections, pairs, 0))  7.86 us
    ppermute x2, waiting for transfers between devices, plane_shards(): lax.ppermute(second, ('depth', 'lat'), level_pairs(sections, pairs, 1))  6.38 us
    ppermute x2, starting transfers between devices, plane_shards(): lax.ppermute(second, ('depth', 'lat'), level_pairs(sections, pairs, 1))  4.73 us
    pallas_call x6, Pallas kernels, column(): local_call(body, [part, part], 'v' * 6, [pltpu.VMEM(part, f32) for _ in r...  4.49 us
    ppermute x12, starting transfers between devices, crossed(): return lax.ppermute(value, 'lat', swap)  3.9 us
    ppermute x1, waiting for transfers between devices, plane_shards(): odd = lax.ppermute(odd, ('depth', 'lat'), section_pairs(sections, pairs, 1))  3.44 us
  transfers between devices with their start and end apart: 30, of which 13 were waited for; matrix products, arithmetic and copies ran while one was open for 0% of the time, Pallas kernels for 12%

profile of v2, /device:TPU:16, one launch (start us, length us, event | category | flops | bytes accessed | tf_op | source)
XLA Modules:
  0.0 70.4 jit_solution(3839306331857246009)
XLA Ops:
  0.6 1.4 %shard_map.174 = (f32[128,256]{1,0:T(8,128)S(1)}, f32[128,256]{1,0:T(8,128)S(1)}, f32[128,256]{1,0:T(8,128)S(1)}, f32[128,256]{1,0:T(8,128)S(1)}, f32[64,256]{1,...) custom-call(f32[4,32,256]{2,1,0:T(8,128)} %dr.1, f32[4,32,256]{2,1,0:T(8,128)} %di.1, ...), custom_call_target="tpu_custom_call" | custom-call | tf_op jit(solution)/shard_map/pallas_call | solution.py:405
  2.0 1.6 %collective-permute-start = (f32[128,256]{1,0:T(8,128)S(1)}, f32[128,256]{1,0:T(8,128)S(1)}, u32[]{:S(2)}, u32[]{:S(2)}) collective-permute-start(f32[128,256]{1,0:T(8,128)S(1)} %get-tuple-element.52), channel_id=1, source_target_pairs={{0,2},{1,3},{2,0},{3,1},{4,6},{5,7},{6,4},{7,5},{8,10},{9,11},{10,... | collective-permute-start | bytes 393224 | tf_op jit(solution)/shard_map/ppermute | solution.py:429
  3.6 1.5 %collective-permute-start.1 = (f32[128,256]{1,0:T(8,128)S(1)}, f32[128,256]{1,0:T(8,128)S(1)}, u32[]{:S(2)}, u32[]{:S(2)}) collective-permute-start(f32[128,256]{1,0:T(8,128)S(1)} %get-tuple-element.53), channel_id=1, source_target_pairs={{0,4},{1,5},{2,6},{3,7},{4,0},{5,1},{6,2},{7,3},{8,12},{9,13},{10,... | collective-permute-start | bytes 393224 | tf_op jit(solution)/shard_map/ppermute | solution.py:429
  5.1 0.5 collective-permute-start.2
  5.6 2.2 %collective-permute-done.refs_1_ = f32[128,256]{1,0:T(8,128)S(1)} collective-permute-done((f32[128,256]{1,0:T(8,128)S(1)}, f32[128,256]{1,0:T(8,128)S(1)}, u32[]{:S(2)}, u32[]{:S(2)}) %collective-permute-start) | collective-permute-done | bytes 131104 | tf_op jit(solution)/shard_map/ppermute | solution.py:429
  7.7 3.6 %collective-permute-done.1.refs_2_ = f32[128,256]{1,0:T(8,128)S(1)} collective-permute-done((f32[128,256]{1,0:T(8,128)S(1)}, f32[128,256]{1,0:T(8,128)S(1)}, u32[]{:S(2)}, u32[]{:S(2)}) %collective-permute-start.1) | collective-permute-done | bytes 131104 | tf_op jit(solution)/shard_map/ppermute | solution.py:429
  12.1 0.6 collective-permute-start.9
  12.7 0.9 %shard_map.176 = (f32[256,256]{1,0:T(8,128)S(1)}, f32[32,256]{1,0:T(8,128)S(1)}) custom-call(f32[4]{0:T(128)S(1)} %copy-done.9), custom_call_target="tpu_custom_call" | custom-call | tf_op jit(solution)/shard_map/pallas_call | solution.py:441
  13.7 0.7 %shard_map.177 = (f32[256,128]{1,0:T(8,128)S(1)}, f32[256,128]{1,0:T(8,128)S(1)}) custom-call(f32[256,128]{1,0:T(8,128)S(1)} %get-tuple-element.55.keep, f32[256,128]{1,0:T(8,128)S(1)} %collective-permute-done.3.got, f32[256,256]{1,0:T(8,128)S(1)} %get-tuple-element.57.mult, bf16[256,768]{1,0:T(8,128)(2,1)S(1)} %copy-done.3, bf16[256,768]{1,0:T(8,128)(2,1)S(1)} %copy-done.2, ...), custom_call_target="tpu_custom_call" | custom-call | tf_op jit(solution)/shard_map/pallas_call | solution.py:541
  14.4 0.6 collective-permute-start.4
  15.0 0.7 %shard_map.181 = (f32[256,128]{1,0:T(8,128)S(1)}, f32[256,128]{1,0:T(8,128)S(1)}) custom-call(f32[256,128]{1,0:T(8,128)S(1)} %get-tuple-element.66.keep, f32[256,128]{1,0:T(8,128)S(1)} %collective-permute-done.9.got, f32[256,256]{1,0:T(8,128)S(1)} %get-tuple-element.57.mult, bf16[256,768]{1,0:T(8,128)(2,1)S(1)} %copy-done.3, bf16[256,768]{1,0:T(8,128)(2,1)S(1)} %copy-done.2, ...), custom_call_target="tpu_custom_call" | custom-call | tf_op jit(solution)/shard_map/pallas_call | solution.py:541
  15.9 1.2 %collective-permute-start.5 = (f32[64,256]{1,0:T(8,128)S(1)}, f32[64,256]{1,0:T(8,128)S(1)}, u32[]{:S(2)}, u32[]{:S(2)}) collective-permute-start(f32[64,256]{1,0:T(8,128)S(1)} %get-tuple-element.61), channel_id=1, source_target_pairs={{0,2},{1,3},{2,0},{3,1},{4,6},{5,7},{6,4},{7,5},{8,10},{9,11},{10,... | collective-permute-start | bytes 196616 | tf_op jit(solution)/shard_map/ppermute | solution.py:429
  17.1 0.8 %collective-permute-start.6 = (f32[64,256]{1,0:T(8,128)S(1)}, f32[64,256]{1,0:T(8,128)S(1)}, u32[]{:S(2)}, u32[]{:S(2)}) collective-permute-start(f32[64,256]{1,0:T(8,128)S(1)} %get-tuple-element.62), channel_id=1, source_target_pairs={{0,4},{1,5},{2,6},{3,7},{4,0},{5,1},{6,2},{7,3},{8,12},{9,13},{10,... | collective-permute-start | bytes 196616 | tf_op jit(solution)/shard_map/ppermute | solution.py:429
  18.0 1.4 %collective-permute-start.7 = (f32[64,256]{1,0:T(8,128)S(1)}, f32[64,256]{1,0:T(8,128)S(1)}, u32[]{:S(2)}, u32[]{:S(2)}) collective-permute-start(f32[64,256]{1,0:T(8,128)S(1)} %get-tuple-element.63), channel_id=1, source_target_pairs={{0,6},{1,7},{2,4},{3,5},{4,2},{5,3},{6,0},{7,1},{8,14},{9,15},{10,... | collective-permute-start | bytes 196616 | tf_op jit(solution)/shard_map/ppermute | solution.py:429
  19.4 0.9 %collective-permute-done.5.refs_1_ = f32[64,256]{1,0:T(8,128)S(1)} collective-permute-done((f32[64,256]{1,0:T(8,128)S(1)}, f32[64,256]{1,0:T(8,128)S(1)}, u32[]{:S(2)}, u32[]{:S(2)}) %collective-permute-start.5) | collective-permute-done | bytes 65568 | tf_op jit(solution)/shard_map/ppermute | solution.py:429
  20.4 1.1 %collective-permute-done.6.refs_2_ = f32[64,256]{1,0:T(8,128)S(1)} collective-permute-done((f32[64,256]{1,0:T(8,128)S(1)}, f32[64,256]{1,0:T(8,128)S(1)}, u32[]{:S(2)}, u32[]{:S(2)}) %collective-permute-start.6) | collective-permute-done | bytes 65568 | tf_op jit(solution)/shard_map/ppermute | solution.py:429
  21.4 1.7 %collective-permute-done.7.refs_3_ = f32[64,256]{1,0:T(8,128)S(1)} collective-permute-done((f32[64,256]{1,0:T(8,128)S(1)}, f32[64,256]{1,0:T(8,128)S(1)}, u32[]{:S(2)}, u32[]{:S(2)}) %collective-permute-start.7) | collective-permute-done | bytes 65568 | tf_op jit(solution)/shard_map/ppermute | solution.py:429
  23.7 1.5 %collective-permute-start.8 = (f32[256,256]{1,0:T(8,128)S(1)}, f32[256,256]{1,0:T(8,128)S(1)}, u32[]{:S(2)}, u32[]{:S(2)}) collective-permute-start(f32[256,256]{1,0:T(8,128)S(1)} %shard_map.179), channel_id=1, source_target_pairs={{0,2},{2,0},{1,3},{3,1},{6,4},{4,6},{7,5},{5,7},{12,14},{14,12},{1... | collective-permute-start | bytes 786440 | tf_op jit(solution)/shard_map/ppermute | solution.py:593
  25.6 2.4 %collective-permute-start.11 = (f32[256,256]{1,0:T(8,128)S(1)}, f32[256,256]{1,0:T(8,128)S(1)}, u32[]{:S(2)}, u32[]{:S(2)}) collective-permute-start(f32[256,256]{1,0:T(8,128)S(1)} %shard_map.182), channel_id=1, source_target_pairs={{2,6},{6,2},{3,7},{7,3},{4,12},{12,4},{5,13},{13,5},{14,10},{10,14... | collective-permute-start | bytes 786440 | tf_op jit(solution)/shard_map/ppermute | solution.py:595
  27.9 2.8 %collective-permute-done.8.ahead = f32[256,256]{1,0:T(8,128)S(1)} collective-permute-done((f32[256,256]{1,0:T(8,128)S(1)}, f32[256,256]{1,0:T(8,128)S(1)}, u32[]{:S(2)}, u32[]{:S(2)}) %collective-permute-start.8) | collective-permute-done | bytes 262176 | tf_op jit(solution)/shard_map/ppermute | solution.py:593
  30.7 3.4 %collective-permute-done.11.behind = f32[256,256]{1,0:T(8,128)S(1)} collective-permute-done((f32[256,256]{1,0:T(8,128)S(1)}, f32[256,256]{1,0:T(8,128)S(1)}, u32[]{:S(2)}, u32[]{:S(2)}) %collective-permute-start.11) | collective-permute-done | bytes 262176 | tf_op jit(solution)/shard_map/ppermute | solution.py:595
  34.8 0.6 collective-permute-start.15
  35.4 0.5 collective-permute-done.12.got
  35.8 0.7 %shard_map.184 = (f32[256,128]{1,0:T(8,128)S(1)}, f32[256,128]{1,0:T(8,128)S(1)}) custom-call(f32[256,128]{1,0:T(8,128)S(1)} %get-tuple-element.72.keep, f32[256,128]{1,0:T(8,128)S(1)} %collective-permute-done.12.got, f32[256,256]{1,0:T(8,128)S(1)} %get-tuple-element.57.mult, bf16[256,768]{1,0:T(8,128)(2,1)S(1)} %copy-done.3, ...), custom_call_target="tpu_custom_call" | custom-call | tf_op jit(solution)/shard_map/pallas_call | solution.py:541
  36.8 0.7 %shard_map.187 = (f32[256,128]{1,0:T(8,128)S(1)}, f32[256,128]{1,0:T(8,128)S(1)}) custom-call(f32[256,128]{1,0:T(8,128)S(1)} %get-tuple-element.76.keep, f32[256,128]{1,0:T(8,128)S(1)} %collective-permute-done.15.got, f32[256,256]{1,0:T(8,128)S(1)} %get-tuple-element.57.mult, bf16[256,768]{1,0:T(8,128)(2,1)S(1)} %copy-done.3, ...), custom_call_target="tpu_custom_call" | custom-call | tf_op jit(solution)/shard_map/pallas_call | solution.py:541
  37.6 0.4 collective-permute-start.16
  38.3 0.7 collective-permute-start.14
  39.3 2.4 %collective-permute-start.17 = (f32[256,256]{1,0:T(8,128)S(1)}, f32[256,256]{1,0:T(8,128)S(1)}, u32[]{:S(2)}, u32[]{:S(2)}) collective-permute-start(f32[256,256]{1,0:T(8,128)S(1)} %shard_map.188), channel_id=1, source_target_pairs={{2,6},{6,2},{3,7},{7,3},{4,12},{12,4},{5,13},{13,5},{14,10},{10,14... | collective-permute-start | bytes 786440 | tf_op jit(solution)/shard_map/ppermute | solution.py:595
  41.7 5.0 %collective-permute-done.14.ahead = f32[256,256]{1,0:T(8,128)S(1)} collective-permute-done((f32[256,256]{1,0:T(8,128)S(1)}, f32[256,256]{1,0:T(8,128)S(1)}, u32[]{:S(2)}, u32[]{:S(2)}) %collective-permute-start.14) | collective-permute-done | bytes 262176 | tf_op jit(solution)/shard_map/ppermute | solution.py:593
  46.8 3.0 %collective-permute-done.17.behind = f32[256,256]{1,0:T(8,128)S(1)} collective-permute-done((f32[256,256]{1,0:T(8,128)S(1)}, f32[256,256]{1,0:T(8,128)S(1)}, u32[]{:S(2)}, u32[]{:S(2)}) %collective-permute-start.17) | collective-permute-done | bytes 262176 | tf_op jit(solution)/shard_map/ppermute | solution.py:595
  50.5 0.6 collective-permute-start.18
  51.0 0.5 collective-permute-done.23.got
  51.5 0.7 %shard_map.193 = (f32[256,128]{1,0:T(8,128)S(1)}, f32[256,128]{1,0:T(8,128)S(1)}) custom-call(f32[256,128]{1,0:T(8,128)S(1)} %get-tuple-element.88.keep, f32[256,128]{1,0:T(8,128)S(1)} %collective-permute-done.23.got, f32[256,256]{1,0:T(8,128)S(1)} %get-tuple-element.57.mult, bf16[256,768]{1,0:T(8,128)(2,1)S(1)} %copy-done.3, ...), custom_call_target="tpu_custom_call" | custom-call | tf_op jit(solution)/shard_map/pallas_call | solution.py:541
  52.5 0.7 %shard_map.190 = (f32[256,128]{1,0:T(8,128)S(1)}, f32[256,128]{1,0:T(8,128)S(1)}) custom-call(f32[256,128]{1,0:T(8,128)S(1)} %get-tuple-element.80.keep, f32[256,128]{1,0:T(8,128)S(1)} %collective-permute-done.18.got, f32[256,256]{1,0:T(8,128)S(1)} %get-tuple-element.57.mult, bf16[256,768]{1,0:T(8,128)(2,1)S(1)} %copy-done.3, ...), custom_call_target="tpu_custom_call" | custom-call | tf_op jit(solution)/shard_map/pallas_call | solution.py:541
  53.2 0.4 collective-permute-start.19
  53.7 0.3 shard_map.194
  54.0 1.0 %collective-permute-start.25 = (f32[64,256]{1,0:T(8,128)S(1)}, f32[64,256]{1,0:T(8,128)S(1)}, u32[]{:S(2)}, u32[]{:S(2)}) collective-permute-start(f32[64,256]{1,0:T(8,128)S(1)} %get-tuple-element.93), channel_id=1, source_target_pairs={{0,2},{1,3},{2,0},{3,1},{4,6},{5,7},{6,4},{7,5},{8,10},{9,11},{10,... | collective-permute-start | bytes 196616 | tf_op jit(solution)/shard_map/ppermute | solution.py:429
  55.0 0.8 %collective-permute-start.26 = (f32[64,256]{1,0:T(8,128)S(1)}, f32[64,256]{1,0:T(8,128)S(1)}, u32[]{:S(2)}, u32[]{:S(2)}) collective-permute-start(f32[64,256]{1,0:T(8,128)S(1)} %get-tuple-element.94), channel_id=1, source_target_pairs={{0,4},{1,5},{2,6},{3,7},{4,0},{5,1},{6,2},{7,3},{8,12},{9,13},{10,... | collective-permute-start | bytes 196616 | tf_op jit(solution)/shard_map/ppermute | solution.py:429
  55.8 1.8 %collective-permute-start.27 = (f32[64,256]{1,0:T(8,128)S(1)}, f32[64,256]{1,0:T(8,128)S(1)}, u32[]{:S(2)}, u32[]{:S(2)}) collective-permute-start(f32[64,256]{1,0:T(8,128)S(1)} %get-tuple-element.95), channel_id=1, source_target_pairs={{0,6},{1,7},{2,4},{3,5},{4,2},{5,3},{6,0},{7,1},{8,14},{9,15},{10,... | collective-permute-start | bytes 196616 | tf_op jit(solution)/shard_map/ppermute | solution.py:429
  57.6 0.3 shard_map.191
  57.9 1.0 %collective-permute-start.20 = (f32[64,256]{1,0:T(8,128)S(1)}, f32[64,256]{1,0:T(8,128)S(1)}, u32[]{:S(2)}, u32[]{:S(2)}) collective-permute-start(f32[64,256]{1,0:T(8,128)S(1)} %get-tuple-element.85), channel_id=1, source_target_pairs={{0,2},{1,3},{2,0},{3,1},{4,6},{5,7},{6,4},{7,5},{8,10},{9,11},{10,... | collective-permute-start | bytes 196616 | tf_op jit(solution)/shard_map/ppermute | solution.py:429
  59.0 0.8 %collective-permute-start.21 = (f32[64,256]{1,0:T(8,128)S(1)}, f32[64,256]{1,0:T(8,128)S(1)}, u32[]{:S(2)}, u32[]{:S(2)}) collective-permute-start(f32[64,256]{1,0:T(8,128)S(1)} %get-tuple-element.86), channel_id=1, source_target_pairs={{0,4},{1,5},{2,6},{3,7},{4,0},{5,1},{6,2},{7,3},{8,12},{9,13},{10,... | collective-permute-start | bytes 196616 | tf_op jit(solution)/shard_map/ppermute | solution.py:429
  59.7 1.7 %collective-permute-start.22 = (f32[64,256]{1,0:T(8,128)S(1)}, f32[64,256]{1,0:T(8,128)S(1)}, u32[]{:S(2)}, u32[]{:S(2)}) collective-permute-start(f32[64,256]{1,0:T(8,128)S(1)} %get-tuple-element.87), channel_id=1, source_target_pairs={{0,6},{1,7},{2,4},{3,5},{4,2},{5,3},{6,0},{7,1},{8,14},{9,15},{10,... | collective-permute-start | bytes 196616 | tf_op jit(solution)/shard_map/ppermute | solution.py:429
  61.6 1.6 %collective-permute-start.28 = (f32[64,256]{1,0:T(8,128)S(1)}, f32[64,256]{1,0:T(8,128)S(1)}, u32[]{:S(2)}, u32[]{:S(2)}) collective-permute-start(f32[64,256]{1,0:T(8,128)S(1)} %get-tuple-element.96), channel_id=1, source_target_pairs={{0,8},{8,0},{1,9},{9,1},{2,10},{10,2},{3,11},{11,3},{4,12},{12,4},... | collective-permute-start | bytes 196616 | tf_op jit(solution)/shard_map/ppermute | solution.py:621
  63.3 1.9 %collective-permute-start.29 = (f32[64,256]{1,0:T(8,128)S(1)}, f32[64,256]{1,0:T(8,128)S(1)}, u32[]{:S(2)}, u32[]{:S(2)}) collective-permute-start(f32[64,256]{1,0:T(8,128)S(1)} %get-tuple-element.97), channel_id=1, source_target_pairs={{8,16},{16,8},{9,17},{17,9},{10,18},{18,10},{11,19},{19,11},{12,20... | collective-permute-start | bytes 196616 | tf_op jit(solution)/shard_map/ppermute | solution.py:622
  65.2 0.8 %collective-permute-done.28.refs_8_ = f32[64,256]{1,0:T(8,128)S(1)} collective-permute-done((f32[64,256]{1,0:T(8,128)S(1)}, f32[64,256]{1,0:T(8,128)S(1)}, u32[]{:S(2)}, u32[]{:S(2)}) %collective-permute-start.28) | collective-permute-done | bytes 65568 | tf_op jit(solution)/shard_map/ppermute | solution.py:621
  66.0 3.4 %collective-permute-done.29.refs_9_ = f32[64,256]{1,0:T(8,128)S(1)} collective-permute-done((f32[64,256]{1,0:T(8,128)S(1)}, f32[64,256]{1,0:T(8,128)S(1)}, u32[]{:S(2)}, u32[]{:S(2)}) %collective-permute-start.29) | collective-permute-done | bytes 65568 | tf_op jit(solution)/shard_map/ppermute | solution.py:622
  69.4 1.0 %shard_map.196 = (f32[4,32,256]{2,1,0:T(8,128)}, f32[4,32,256]{2,1,0:T(8,128)}, f32[4,32,256]{2,1,0:T(8,128)}, f32[4,32,256]{2,1,0:T(8,128)}) custom-call(f32[64,256]{1,0:T(8,128)S(1)} %get-tuple-element.84.refs_0_, f32[64,256]{1,0:T(8,128)S(1)} %collective-permute-done.20.refs_1_, f32[64,256]{1,0:T(8,128)S(1)} %collective-permute-done.21.refs_2_, ...), custom_call_target="tpu_custom_call" | custom-call | tf_op jit(solution)/shard_map/pallas_call | solution.py:668
  (55 shorter events, 4.3 us)
Async XLA Ops:
  0.6 10.7 %copy-start.1 = (bf16[768,256]{1,0:T(8,128)(2,1)S(1)}, bf16[768,256]{1,0:T(8,128)(2,1)}, u32[]{:S(2)}) copy-start(bf16[768,256]{1,0:T(8,128)(2,1)} %constant.12.clone.refs_4_.table) | copy-start | bytes 1179652
  2.0 5.7 %collective-permute-start = (f32[128,256]{1,0:T(8,128)S(1)}, f32[128,256]{1,0:T(8,128)S(1)}, u32[]{:S(2)}, u32[]{:S(2)}) collective-permute-start(f32[128,256]{1,0:T(8,128)S(1)} %get-tuple-element.52), channel_id=1, source_target_pairs={{0,2},{1,3},{2,0},{3,1},{4,6},{5,7},{6,4},{7,5},{8,10},{9,11},{10,... | collective-permute-start | bytes 393224 | tf_op jit(solution)/shard_map/ppermute | solution.py:429
  3.6 7.8 %collective-permute-start.1 = (f32[128,256]{1,0:T(8,128)S(1)}, f32[128,256]{1,0:T(8,128)S(1)}, u32[]{:S(2)}, u32[]{:S(2)}) collective-permute-start(f32[128,256]{1,0:T(8,128)S(1)} %get-tuple-element.53), channel_id=1, source_target_pairs={{0,4},{1,5},{2,6},{3,7},{4,0},{5,1},{6,2},{7,3},{8,12},{9,13},{10,... | collective-permute-start | bytes 393224 | tf_op jit(solution)/shard_map/ppermute | solution.py:429
  5.1 6.3 %copy-start.6 = (f32[2,128]{1,0:T(2,128)S(1)}, f32[2,128]{1,0:T(2,128)}, u32[]{:S(2)}) copy-start(f32[2,128]{1,0:T(2,128)} %constant.16.clone.refs_5_.turn) | copy-start | bytes 3076
  5.1 6.3 %collective-permute-start.2 = (f32[128,256]{1,0:T(8,128)S(1)}, f32[128,256]{1,0:T(8,128)S(1)}, u32[]{:S(2)}, u32[]{:S(2)}) collective-permute-start(f32[128,256]{1,0:T(8,128)S(1)} %get-tuple-element.54), channel_id=1, source_target_pairs={{0,6},{1,7},{2,4},{3,5},{4,2},{5,3},{6,0},{7,1},{8,14},{9,15},{10,... | collective-permute-start | bytes 393224 | tf_op jit(solution)/shard_map/ppermute | solution.py:429
  11.7 2.0 %copy-start.2 = (bf16[256,768]{1,0:T(8,128)(2,1)S(1)}, bf16[256,768]{1,0:T(8,128)(2,1)}, u32[]{:S(2)}) copy-start(bf16[256,768]{1,0:T(8,128)(2,1)} %constant.15.clone.back) | copy-start | bytes 1179652
  11.7 2.0 %copy-start.3 = (bf16[256,768]{1,0:T(8,128)(2,1)S(1)}, bf16[256,768]{1,0:T(8,128)(2,1)}, u32[]{:S(2)}) copy-start(bf16[256,768]{1,0:T(8,128)(2,1)} %constant.14.clone.table) | copy-start | bytes 1179652
  11.7 2.0 %copy-start.4 = (f32[2,128,128]{2,1,0:T(8,128)S(1)}, f32[2,128,128]{2,1,0:T(8,128)}, u32[]{:S(2)}) copy-start(f32[2,128,128]{2,1,0:T(8,128)} %constant.17.clone.turn) | copy-start | bytes 393220
  11.7 1.9 %collective-permute-start.3 = (f32[256,128]{1,0:T(8,128)S(1)}, f32[256,128]{1,0:T(8,128)S(1)}, u32[]{:S(2)}, u32[]{:S(2)}) collective-permute-start(f32[256,128]{1,0:T(8,128)S(1)} %get-tuple-element.56), channel_id=1, source_target_pairs={{0,1},{1,0},{2,3},{3,2},{4,5},{5,4},{6,7},{7,6},{8,9},{9,8},{10,11... | collective-permute-start | bytes 393224 | tf_op jit(solution)/shard_map/ppermute | solution.py:581
  12.1 0.7 copy-start.9
  12.1 2.9 %collective-permute-start.9 = (f32[256,128]{1,0:T(8,128)S(1)}, f32[256,128]{1,0:T(8,128)S(1)}, u32[]{:S(2)}, u32[]{:S(2)}) collective-permute-start(f32[256,128]{1,0:T(8,128)S(1)} %get-tuple-element.67), channel_id=1, source_target_pairs={{0,1},{1,0},{2,3},{3,2},{4,5},{5,4},{6,7},{7,6},{8,9},{9,8},{10,11... | collective-permute-start | bytes 393224 | tf_op jit(solution)/shard_map/ppermute | solution.py:581
  14.4 8.9 %collective-permute-start.4 = (f32[256,128]{1,0:T(8,128)S(1)}, f32[256,128]{1,0:T(8,128)S(1)}, u32[]{:S(2)}, u32[]{:S(2)}) collective-permute-start(f32[256,128]{1,0:T(8,128)S(1)} %get-tuple-element.59), channel_id=1, source_target_pairs={{0,1},{1,0},{2,3},{3,2},{4,5},{5,4},{6,7},{7,6},{8,9},{9,8},{10,11... | collective-permute-start | bytes 393224 | tf_op jit(solution)/shard_map/ppermute | solution.py:581
  15.0 8.3 %copy-start = (bf16[768,256]{1,0:T(8,128)(2,1)S(1)}, bf16[768,256]{1,0:T(8,128)(2,1)}, u32[]{:S(2)}) copy-start(bf16[768,256]{1,0:T(8,128)(2,1)} %constant.13.clone.table) | copy-start | bytes 1179652
  15.8 9.5 %collective-permute-start.10 = (f32[256,128]{1,0:T(8,128)S(1)}, f32[256,128]{1,0:T(8,128)S(1)}, u32[]{:S(2)}, u32[]{:S(2)}) collective-permute-start(f32[256,128]{1,0:T(8,128)S(1)} %get-tuple-element.69), channel_id=1, source_target_pairs={{0,1},{1,0},{2,3},{3,2},{4,5},{5,4},{6,7},{7,6},{8,9},{9,8},{10,11... | collective-permute-start | bytes 393224 | tf_op jit(solution)/shard_map/ppermute | solution.py:581
  15.9 4.5 %collective-permute-start.5 = (f32[64,256]{1,0:T(8,128)S(1)}, f32[64,256]{1,0:T(8,128)S(1)}, u32[]{:S(2)}, u32[]{:S(2)}) collective-permute-start(f32[64,256]{1,0:T(8,128)S(1)} %get-tuple-element.61), channel_id=1, source_target_pairs={{0,2},{1,3},{2,0},{3,1},{4,6},{5,7},{6,4},{7,5},{8,10},{9,11},{10,... | collective-permute-start | bytes 196616 | tf_op jit(solution)/shard_map/ppermute | solution.py:429
  17.1 4.3 %collective-permute-start.6 = (f32[64,256]{1,0:T(8,128)S(1)}, f32[64,256]{1,0:T(8,128)S(1)}, u32[]{:S(2)}, u32[]{:S(2)}) collective-permute-start(f32[64,256]{1,0:T(8,128)S(1)} %get-tuple-element.62), channel_id=1, source_target_pairs={{0,4},{1,5},{2,6},{3,7},{4,0},{5,1},{6,2},{7,3},{8,12},{9,13},{10,... | collective-permute-start | bytes 196616 | tf_op jit(solution)/shard_map/ppermute | solution.py:429
  18.0 5.2 %collective-permute-start.7 = (f32[64,256]{1,0:T(8,128)S(1)}, f32[64,256]{1,0:T(8,128)S(1)}, u32[]{:S(2)}, u32[]{:S(2)}) collective-permute-start(f32[64,256]{1,0:T(8,128)S(1)} %get-tuple-element.63), channel_id=1, source_target_pairs={{0,6},{1,7},{2,4},{3,5},{4,2},{5,3},{6,0},{7,1},{8,14},{9,15},{10,... | collective-permute-start | bytes 196616 | tf_op jit(solution)/shard_map/ppermute | solution.py:429
  23.7 7.1 %collective-permute-start.8 = (f32[256,256]{1,0:T(8,128)S(1)}, f32[256,256]{1,0:T(8,128)S(1)}, u32[]{:S(2)}, u32[]{:S(2)}) collective-permute-start(f32[256,256]{1,0:T(8,128)S(1)} %shard_map.179), channel_id=1, source_target_pairs={{0,2},{2,0},{1,3},{3,1},{6,4},{4,6},{7,5},{5,7},{12,14},{14,12},{1... | collective-permute-start | bytes 786440 | tf_op jit(solution)/shard_map/ppermute | solution.py:593
  25.6 8.5 %collective-permute-start.11 = (f32[256,256]{1,0:T(8,128)S(1)}, f32[256,256]{1,0:T(8,128)S(1)}, u32[]{:S(2)}, u32[]{:S(2)}) collective-permute-start(f32[256,256]{1,0:T(8,128)S(1)} %shard_map.182), channel_id=1, source_target_pairs={{2,6},{6,2},{3,7},{7,3},{4,12},{12,4},{5,13},{13,5},{14,10},{10,14... | collective-permute-start | bytes 786440 | tf_op jit(solution)/shard_map/ppermute | solution.py:595
  34.4 1.4 %collective-permute-start.12 = (f32[256,128]{1,0:T(8,128)S(1)}, f32[256,128]{1,0:T(8,128)S(1)}, u32[]{:S(2)}, u32[]{:S(2)}) collective-permute-start(f32[256,128]{1,0:T(8,128)S(1)} %get-tuple-element.73), channel_id=1, source_target_pairs={{0,1},{1,0},{2,3},{3,2},{4,5},{5,4},{6,7},{7,6},{8,9},{9,8},{10,11... | collective-permute-start | bytes 393224 | tf_op jit(solution)/shard_map/ppermute | solution.py:581
  34.8 2.0 %collective-permute-start.15 = (f32[256,128]{1,0:T(8,128)S(1)}, f32[256,128]{1,0:T(8,128)S(1)}, u32[]{:S(2)}, u32[]{:S(2)}) collective-permute-start(f32[256,128]{1,0:T(8,128)S(1)} %get-tuple-element.77), channel_id=1, source_target_pairs={{0,1},{1,0},{2,3},{3,2},{4,5},{5,4},{6,7},{7,6},{8,9},{9,8},{10,11... | collective-permute-start | bytes 393224 | tf_op jit(solution)/shard_map/ppermute | solution.py:581
  36.6 1.4 %collective-permute-start.13 = (f32[256,128]{1,0:T(8,128)S(1)}, f32[256,128]{1,0:T(8,128)S(1)}, u32[]{:S(2)}, u32[]{:S(2)}) collective-permute-start(f32[256,128]{1,0:T(8,128)S(1)} %get-tuple-element.75), channel_id=1, source_target_pairs={{0,1},{1,0},{2,3},{3,2},{4,5},{5,4},{6,7},{7,6},{8,9},{9,8},{10,11... | collective-permute-start | bytes 393224 | tf_op jit(solution)/shard_map/ppermute | solution.py:581
  37.6 1.4 %collective-permute-start.16 = (f32[256,128]{1,0:T(8,128)S(1)}, f32[256,128]{1,0:T(8,128)S(1)}, u32[]{:S(2)}, u32[]{:S(2)}) collective-permute-start(f32[256,128]{1,0:T(8,128)S(1)} %get-tuple-element.79), channel_id=1, source_target_pairs={{0,1},{1,0},{2,3},{3,2},{4,5},{5,4},{6,7},{7,6},{8,9},{9,8},{10,11... | collective-permute-start | bytes 393224 | tf_op jit(solution)/shard_map/ppermute | solution.py:581
  38.3 8.4 %collective-permute-start.14 = (f32[256,256]{1,0:T(8,128)S(1)}, f32[256,256]{1,0:T(8,128)S(1)}, u32[]{:S(2)}, u32[]{:S(2)}) collective-permute-start(f32[256,256]{1,0:T(8,128)S(1)} %shard_map.185), channel_id=1, source_target_pairs={{0,2},{2,0},{1,3},{3,1},{6,4},{4,6},{7,5},{5,7},{12,14},{14,12},{1... | collective-permute-start | bytes 786440 | tf_op jit(solution)/shard_map/ppermute | solution.py:593
  39.3 10.4 %collective-permute-start.17 = (f32[256,256]{1,0:T(8,128)S(1)}, f32[256,256]{1,0:T(8,128)S(1)}, u32[]{:S(2)}, u32[]{:S(2)}) collective-permute-start(f32[256,256]{1,0:T(8,128)S(1)} %shard_map.188), channel_id=1, source_target_pairs={{2,6},{6,2},{3,7},{7,3},{4,12},{12,4},{5,13},{13,5},{14,10},{10,14... | collective-permute-start | bytes 786440 | tf_op jit(solution)/shard_map/ppermute | solution.py:595
  50.1 1.4 %collective-permute-start.23 = (f32[256,128]{1,0:T(8,128)S(1)}, f32[256,128]{1,0:T(8,128)S(1)}, u32[]{:S(2)}, u32[]{:S(2)}) collective-permute-start(f32[256,128]{1,0:T(8,128)S(1)} %get-tuple-element.89), channel_id=1, source_target_pairs={{0,1},{1,0},{2,3},{3,2},{4,5},{5,4},{6,7},{7,6},{8,9},{9,8},{10,11... | collective-permute-start | bytes 393224 | tf_op jit(solution)/shard_map/ppermute | solution.py:581
  50.5 2.0 %collective-permute-start.18 = (f32[256,128]{1,0:T(8,128)S(1)}, f32[256,128]{1,0:T(8,128)S(1)}, u32[]{:S(2)}, u32[]{:S(2)}) collective-permute-start(f32[256,128]{1,0:T(8,128)S(1)} %get-tuple-element.81), channel_id=1, source_target_pairs={{0,1},{1,0},{2,3},{3,2},{4,5},{5,4},{6,7},{7,6},{8,9},{9,8},{10,11... | collective-permute-start | bytes 393224 | tf_op jit(solution)/shard_map/ppermute | solution.py:581
  52.3 1.4 %collective-permute-start.24 = (f32[256,128]{1,0:T(8,128)S(1)}, f32[256,128]{1,0:T(8,128)S(1)}, u32[]{:S(2)}, u32[]{:S(2)}) collective-permute-start(f32[256,128]{1,0:T(8,128)S(1)} %get-tuple-element.91), channel_id=1, source_target_pairs={{0,1},{1,0},{2,3},{3,2},{4,5},{5,4},{6,7},{7,6},{8,9},{9,8},{10,11... | collective-permute-start | bytes 393224 | tf_op jit(solution)/shard_map/ppermute | solution.py:581
  53.2 4.3 %collective-permute-start.19 = (f32[256,128]{1,0:T(8,128)S(1)}, f32[256,128]{1,0:T(8,128)S(1)}, u32[]{:S(2)}, u32[]{:S(2)}) collective-permute-start(f32[256,128]{1,0:T(8,128)S(1)} %get-tuple-element.83), channel_id=1, source_target_pairs={{0,1},{1,0},{2,3},{3,2},{4,5},{5,4},{6,7},{7,6},{8,9},{9,8},{10,11... | collective-permute-start | bytes 393224 | tf_op jit(solution)/shard_map/ppermute | solution.py:581
  54.0 5.7 %collective-permute-start.25 = (f32[64,256]{1,0:T(8,128)S(1)}, f32[64,256]{1,0:T(8,128)S(1)}, u32[]{:S(2)}, u32[]{:S(2)}) collective-permute-start(f32[64,256]{1,0:T(8,128)S(1)} %get-tuple-element.93), channel_id=1, source_target_pairs={{0,2},{1,3},{2,0},{3,1},{4,6},{5,7},{6,4},{7,5},{8,10},{9,11},{10,... | collective-permute-start | bytes 196616 | tf_op jit(solution)/shard_map/ppermute | solution.py:429
  55.0 6.4 %collective-permute-start.26 = (f32[64,256]{1,0:T(8,128)S(1)}, f32[64,256]{1,0:T(8,128)S(1)}, u32[]{:S(2)}, u32[]{:S(2)}) collective-permute-start(f32[64,256]{1,0:T(8,128)S(1)} %get-tuple-element.94), channel_id=1, source_target_pairs={{0,4},{1,5},{2,6},{3,7},{4,0},{5,1},{6,2},{7,3},{8,12},{9,13},{10,... | collective-permute-start | bytes 196616 | tf_op jit(solution)/shard_map/ppermute | solution.py:429
  55.8 5.7 %collective-permute-start.27 = (f32[64,256]{1,0:T(8,128)S(1)}, f32[64,256]{1,0:T(8,128)S(1)}, u32[]{:S(2)}, u32[]{:S(2)}) collective-permute-start(f32[64,256]{1,0:T(8,128)S(1)} %get-tuple-element.95), channel_id=1, source_target_pairs={{0,6},{1,7},{2,4},{3,5},{4,2},{5,3},{6,0},{7,1},{8,14},{9,15},{10,... | collective-permute-start | bytes 196616 | tf_op jit(solution)/shard_map/ppermute | solution.py:429
  57.9 7.3 %collective-permute-start.20 = (f32[64,256]{1,0:T(8,128)S(1)}, f32[64,256]{1,0:T(8,128)S(1)}, u32[]{:S(2)}, u32[]{:S(2)}) collective-permute-start(f32[64,256]{1,0:T(8,128)S(1)} %get-tuple-element.85), channel_id=1, source_target_pairs={{0,2},{1,3},{2,0},{3,1},{4,6},{5,7},{6,4},{7,5},{8,10},{9,11},{10,... | collective-permute-start | bytes 196616 | tf_op jit(solution)/shard_map/ppermute | solution.py:429
  59.0 6.2 %collective-permute-start.21 = (f32[64,256]{1,0:T(8,128)S(1)}, f32[64,256]{1,0:T(8,128)S(1)}, u32[]{:S(2)}, u32[]{:S(2)}) collective-permute-start(f32[64,256]{1,0:T(8,128)S(1)} %get-tuple-element.86), channel_id=1, source_target_pairs={{0,4},{1,5},{2,6},{3,7},{4,0},{5,1},{6,2},{7,3},{8,12},{9,13},{10,... | collective-permute-start | bytes 196616 | tf_op jit(solution)/shard_map/ppermute | solution.py:429
  59.7 5.5 %collective-permute-start.22 = (f32[64,256]{1,0:T(8,128)S(1)}, f32[64,256]{1,0:T(8,128)S(1)}, u32[]{:S(2)}, u32[]{:S(2)}) collective-permute-start(f32[64,256]{1,0:T(8,128)S(1)} %get-tuple-element.87), channel_id=1, source_target_pairs={{0,6},{1,7},{2,4},{3,5},{4,2},{5,3},{6,0},{7,1},{8,14},{9,15},{10,... | collective-permute-start | bytes 196616 | tf_op jit(solution)/shard_map/ppermute | solution.py:429
  61.5 7.9 %copy-start.5 = (f32[4,32,256]{2,1,0:T(8,128)S(1)}, f32[4,32,256]{2,1,0:T(8,128)}, u32[]{:S(2)}) copy-start(f32[4,32,256]{2,1,0:T(8,128)} %refs_10_.1) | copy-start | bytes 393220
  61.5 7.9 %copy-start.7 = (f32[32,256]{1,0:T(8,128)S(1)}, f32[32,256]{1,0:T(8,128)}, u32[]{:S(2)}) copy-start(f32[32,256]{1,0:T(8,128)} %refs_11_.1) | copy-start | bytes 98308
  61.5 7.9 %copy-start.8 = (f32[32,256]{1,0:T(8,128)S(1)}, f32[32,256]{1,0:T(8,128)}, u32[]{:S(2)}) copy-start(f32[32,256]{1,0:T(8,128)} %refs_12_.1) | copy-start | bytes 98308
  61.6 4.3 %collective-permute-start.28 = (f32[64,256]{1,0:T(8,128)S(1)}, f32[64,256]{1,0:T(8,128)S(1)}, u32[]{:S(2)}, u32[]{:S(2)}) collective-permute-start(f32[64,256]{1,0:T(8,128)S(1)} %get-tuple-element.96), channel_id=1, source_target_pairs={{0,8},{8,0},{1,9},{9,1},{2,10},{10,2},{3,11},{11,3},{4,12},{12,4},... | collective-permute-start | bytes 196616 | tf_op jit(solution)/shard_map/ppermute | solution.py:621
  63.3 6.1 %collective-permute-start.29 = (f32[64,256]{1,0:T(8,128)S(1)}, f32[64,256]{1,0:T(8,128)S(1)}, u32[]{:S(2)}, u32[]{:S(2)}) collective-permute-start(f32[64,256]{1,0:T(8,128)S(1)} %get-tuple-element.97), channel_id=1, source_target_pairs={{8,16},{16,8},{9,17},{17,9},{10,18},{18,10},{11,19},{19,11},{12,20... | collective-permute-start | bytes 196616 | tf_op jit(solution)/shard_map/ppermute | solution.py:622

commit v3 on v2

--- a/solution.py
+++ b/solution.py
@@ -386,17 +386,17 @@
 
                 @pl.when(sourced)
                 def _():
-                    for move in pieces(step, (dr, di), (sr, si)):
+                    for move in pieces(step, (sr, si), (dr, di)):
                         act(move)
 
                 @pl.when((level % 2 == 0) & jnp.logical_not(sourced))
                 def _():
-                    for move in pieces(step, (dr, di), (ur, ui)):
+                    for move in pieces(step, (ur, ui), (dr, di)):
                         act(move)
 
                 @pl.when(level % 2 == 1)
                 def _():
-                    for move in pieces(step, (ur, ui), (dr, di)):
+                    for move in pieces(step, (dr, di), (ur, ui)):
                         act(move)
 
         each(lambda move: move.start())
@@ -424,9 +424,9 @@
     )
 
     def exchanged(pieces):
-        moved = [pieces[0]]
+        moved = list(pieces)
         for step in range(1, pairs):
-            moved.append(lax.ppermute(pieces[step], "lat", across(step)))
+            moved[step] = lax.ppermute(pieces[step], "lat", across(step))
         return moved
 
     planes = exchanged(outs[:pairs])
@@ -485,7 +485,7 @@
             shared(*forward_y(whole[:tall], whole[tall:], table, turn), here, keep, send)
 
         outs, scratch = [part, part], [pltpu.VMEM(local, f32)]
-        if which == 1:
+        if which == 0:
             outs, scratch = outs + [local], []
         return local_call(body, outs, "v" * (pairs + 2), scratch)(
             *planes, y_table, y_turn
@@ -494,9 +494,9 @@
     def mixed(which, ahead, behind, source):
         def body(ahead, behind, source, refl, table, turn, keep, send):
             here = Place(pairs)
-            sign = jnp.where((here.level % 2 == 0) == (which == 0), -1.0, 1.0)
-            behind = jnp.where(top(here), source[...], behind[...])
-            base, side = (behind, ahead[...]) if which == 0 else (ahead[...], behind)
+            sign = jnp.where((here.level % 2 == 0) == (which == 0), 1.0, -1.0)
+            ahead = jnp.where(top(here), source[...], ahead[...])
+            base, side = (behind[...], ahead) if which == 0 else (ahead, behind[...])
             weight = refl[...] * sign
             real = base[:tall] + weight * side[:tall]
             imag = base[tall:] + weight * side[tall:]
@@ -580,9 +580,9 @@
     def crossed(value):
         return lax.ppermute(value, "lat", swap)
 
-    keep0, send0 = enter(0)
+    keep0, send0, source = enter(0)
     got0 = crossed(send0)
-    keep1, send1, source = enter(1)
+    keep1, send1 = enter(1)
     got1 = crossed(send1)
     for _ in range(TICKS - 1):
         keep0, send0 = column(keep0, got0)
@@ -590,20 +590,19 @@
         keep1, send1 = column(keep1, got1)
         got1 = crossed(send1)
         first = leave(keep0, got0)
-        ahead = lax.ppermute(first, ("depth", "lat"), level_pairs(sections, pairs, 0))
+        ahead = lax.ppermute(first, ("depth", "lat"), level_pairs(sections, pairs, 1))
         second = leave(keep1, got1)
-        behind = lax.ppermute(second, ("depth", "lat"), level_pairs(sections, pairs, 1))
+        behind = lax.ppermute(second, ("depth", "lat"), level_pairs(sections, pairs, 0))
+        keep0, send0 = mixed(0, ahead, behind, source)
+        got0 = crossed(send0)
         keep1, send1 = mixed(1, ahead, behind, source)
         got1 = crossed(send1)
-        keep0, send0 = mixed(0, ahead, behind, source)
-        got0 = crossed(send0)
+    keep0, send0 = column(keep0, got0)
+    got0 = crossed(send0)
     keep1, send1 = column(keep1, got1)
     got1 = crossed(send1)
-    keep0, send0 = column(keep0, got0)
-    got0 = crossed(send0)
+    back0 = exchanged(leave_last(keep0, got0))
     back1 = exchanged(leave_last(keep1, got1))
-    leaving = leave_last(keep0, got0)
-    back0 = exchanged(leaving)
 
     def pick_body(*refs):
         pieces, even, odd = refs[:pairs], refs[pairs], refs[pairs + 1]
@@ -617,7 +616,7 @@
                     def _():
                         target[...] = pieces[step][...]
 
-    even, odd = local_call(pick_body, [(two, columns)] * 2, "v" * pairs)(*back1)
+    even, odd = local_call(pick_body, [(two, columns)] * 2, "v" * pairs)(*back0)
     even = lax.ppermute(even, ("depth", "lat"), section_pairs(sections, pairs, 0))
     odd = lax.ppermute(odd, ("depth", "lat"), section_pairs(sections, pairs, 1))
 
@@ -632,13 +631,13 @@
 
             @pl.when(level % 2 == 0)
             def _():
+                down[below] = second[step][...]
+                up[above] = first[step][...]
+
+            @pl.when(level % 2 == 1)
+            def _():
                 down[below] = first[step][...]
                 up[above] = second[step][...]
-
-            @pl.when(level % 2 == 1)
-            def _():
-                down[below] = second[step][...]
-                up[above] = first[step][...]
 
         @pl.when(here.section % 2 == 0)
         def _():

time: 70.6 us -> 70 us (level)
  waiting for transfers between devices: 28.9 us -> 27.9 us
    ppermute x16, waiting for transfers between devices: 23.8 us -> 22.9 us  [the longest x12 9.92 us: exchanged(): moved[step] = lax.ppermute(pieces[step], 'lat', across(step))]
  transfers between devices with their start and end apart: 30 -> 30, of which waited for: 13 -> 15; matrix products, arithmetic and copies ran while one was open for 0% -> 0% of each run, Pallas kernels for 12% -> 12%
where the time goes in v3:
time: 70 us; the launch traced here: 69.8 us
  starting transfers between devices  29 us (41%)
  waiting for transfers between devices  27.9 us (40%)
  Pallas kernels  11.7 us (17%)
  between operations  0.99 us (1%)
    ppermute x12, starting transfers between devices, exchanged(): moved[step] = lax.ppermute(pieces[step], 'lat', across(step))  14.2 us
    ppermute x12, waiting for transfers between devices, exchanged(): moved[step] = lax.ppermute(pieces[step], 'lat', across(step))  9.92 us
    ppermute x2, waiting for transfers between devices, plane_shards(): lax.ppermute(first, ('depth', 'lat'), level_pairs(sections, pairs, 1))  9.57 us
    ppermute x2, starting transfers between devices, plane_shards(): lax.ppermute(first, ('depth', 'lat'), level_pairs(sections, pairs, 1))  4.73 us
    pallas_call x6, Pallas kernels, column(): local_call(body, [part, part], 'v' * 6, [pltpu.VMEM(part, f32) for _ in r...  4.48 us
    ppermute x12, starting transfers between devices, crossed(): return lax.ppermute(value, 'lat', swap)  3.9 us
    ppermute x2, waiting for transfers between devices, plane_shards(): lax.ppermute(second, ('depth', 'lat'), level_pairs(sections, pairs, 0))  3.42 us
    ppermute x1, waiting for transfers between devices, plane_shards(): odd = lax.ppermute(odd, ('depth', 'lat'), section_pairs(sections, pairs, 1))  3.21 us
  transfers between devices with their start and end apart: 30, of which 15 were waited for; matrix products, arithmetic and copies ran while one was open for 0% of the time, Pallas kernels for 12%

profile of v3, /device:TPU:16, one launch (start us, length us, event | category | flops | bytes accessed | tf_op | source)
XLA Modules:
  0.0 69.8 jit_solution(16896885597803380066)
XLA Ops:
  0.6 1.4 %shard_map.174 = (f32[128,256]{1,0:T(8,128)S(1)}, f32[128,256]{1,0:T(8,128)S(1)}, f32[128,256]{1,0:T(8,128)S(1)}, f32[128,256]{1,0:T(8,128)S(1)}, f32[64,256]{1,...) custom-call(f32[4,32,256]{2,1,0:T(8,128)} %dr.1, f32[4,32,256]{2,1,0:T(8,128)} %di.1, ...), custom_call_target="tpu_custom_call" | custom-call | tf_op jit(solution)/shard_map/pallas_call | solution.py:405
  2.0 1.6 %collective-permute-start = (f32[128,256]{1,0:T(8,128)S(1)}, f32[128,256]{1,0:T(8,128)S(1)}, u32[]{:S(2)}, u32[]{:S(2)}) collective-permute-start(f32[128,256]{1,0:T(8,128)S(1)} %get-tuple-element.52), channel_id=1, source_target_pairs={{0,2},{1,3},{2,0},{3,1},{4,6},{5,7},{6,4},{7,5},{8,10},{9,11},{10,... | collective-permute-start | bytes 393224 | tf_op jit(solution)/shard_map/ppermute | solution.py:429
  3.6 1.5 %collective-permute-start.1 = (f32[128,256]{1,0:T(8,128)S(1)}, f32[128,256]{1,0:T(8,128)S(1)}, u32[]{:S(2)}, u32[]{:S(2)}) collective-permute-start(f32[128,256]{1,0:T(8,128)S(1)} %get-tuple-element.53), channel_id=1, source_target_pairs={{0,4},{1,5},{2,6},{3,7},{4,0},{5,1},{6,2},{7,3},{8,12},{9,13},{10,... | collective-permute-start | bytes 393224 | tf_op jit(solution)/shard_map/ppermute | solution.py:429
  5.1 0.5 collective-permute-start.2
  5.6 2.2 %collective-permute-done.refs_1_ = f32[128,256]{1,0:T(8,128)S(1)} collective-permute-done((f32[128,256]{1,0:T(8,128)S(1)}, f32[128,256]{1,0:T(8,128)S(1)}, u32[]{:S(2)}, u32[]{:S(2)}) %collective-permute-start) | collective-permute-done | bytes 131104 | tf_op jit(solution)/shard_map/ppermute | solution.py:429
  7.7 3.6 %collective-permute-done.1.refs_2_ = f32[128,256]{1,0:T(8,128)S(1)} collective-permute-done((f32[128,256]{1,0:T(8,128)S(1)}, f32[128,256]{1,0:T(8,128)S(1)}, u32[]{:S(2)}, u32[]{:S(2)}) %collective-permute-start.1) | collective-permute-done | bytes 131104 | tf_op jit(solution)/shard_map/ppermute | solution.py:429
  12.1 0.6 collective-permute-start.3
  12.7 0.9 %shard_map.176 = (f32[256,256]{1,0:T(8,128)S(1)}, f32[32,256]{1,0:T(8,128)S(1)}) custom-call(f32[4]{0:T(128)S(1)} %copy-done.9), custom_call_target="tpu_custom_call" | custom-call | tf_op jit(solution)/shard_map/pallas_call | solution.py:441
  13.7 0.7 %shard_map.181 = (f32[256,128]{1,0:T(8,128)S(1)}, f32[256,128]{1,0:T(8,128)S(1)}) custom-call(f32[256,128]{1,0:T(8,128)S(1)} %get-tuple-element.66.keep, f32[256,128]{1,0:T(8,128)S(1)} %collective-permute-done.9.got, f32[256,256]{1,0:T(8,128)S(1)} %get-tuple-element.57.mult, bf16[256,768]{1,0:T(8,128)(2,1)S(1)} %copy-done.3, bf16[256,768]{1,0:T(8,128)(2,1)S(1)} %copy-done.2, ...), custom_call_target="tpu_custom_call" | custom-call | tf_op jit(solution)/shard_map/pallas_call | solution.py:541
  14.4 0.6 collective-permute-start.10
  15.0 0.7 %shard_map.177 = (f32[256,128]{1,0:T(8,128)S(1)}, f32[256,128]{1,0:T(8,128)S(1)}) custom-call(f32[256,128]{1,0:T(8,128)S(1)} %get-tuple-element.55.keep, f32[256,128]{1,0:T(8,128)S(1)} %collective-permute-done.3.got, f32[256,256]{1,0:T(8,128)S(1)} %get-tuple-element.57.mult, bf16[256,768]{1,0:T(8,128)(2,1)S(1)} %copy-done.3, bf16[256,768]{1,0:T(8,128)(2,1)S(1)} %copy-done.2, ...), custom_call_target="tpu_custom_call" | custom-call | tf_op jit(solution)/shard_map/pallas_call | solution.py:541
  15.9 1.2 %collective-permute-start.5 = (f32[64,256]{1,0:T(8,128)S(1)}, f32[64,256]{1,0:T(8,128)S(1)}, u32[]{:S(2)}, u32[]{:S(2)}) collective-permute-start(f32[64,256]{1,0:T(8,128)S(1)} %get-tuple-element.61), channel_id=1, source_target_pairs={{0,2},{1,3},{2,0},{3,1},{4,6},{5,7},{6,4},{7,5},{8,10},{9,11},{10,... | collective-permute-start | bytes 196616 | tf_op jit(solution)/shard_map/ppermute | solution.py:429
  17.1 0.8 %collective-permute-start.6 = (f32[64,256]{1,0:T(8,128)S(1)}, f32[64,256]{1,0:T(8,128)S(1)}, u32[]{:S(2)}, u32[]{:S(2)}) collective-permute-start(f32[64,256]{1,0:T(8,128)S(1)} %get-tuple-element.62), channel_id=1, source_target_pairs={{0,4},{1,5},{2,6},{3,7},{4,0},{5,1},{6,2},{7,3},{8,12},{9,13},{10,... | collective-permute-start | bytes 196616 | tf_op jit(solution)/shard_map/ppermute | solution.py:429
  18.0 1.4 %collective-permute-start.7 = (f32[64,256]{1,0:T(8,128)S(1)}, f32[64,256]{1,0:T(8,128)S(1)}, u32[]{:S(2)}, u32[]{:S(2)}) collective-permute-start(f32[64,256]{1,0:T(8,128)S(1)} %get-tuple-element.63), channel_id=1, source_target_pairs={{0,6},{1,7},{2,4},{3,5},{4,2},{5,3},{6,0},{7,1},{8,14},{9,15},{10,... | collective-permute-start | bytes 196616 | tf_op jit(solution)/shard_map/ppermute | solution.py:429
  19.4 0.9 %collective-permute-done.5.refs_1_ = f32[64,256]{1,0:T(8,128)S(1)} collective-permute-done((f32[64,256]{1,0:T(8,128)S(1)}, f32[64,256]{1,0:T(8,128)S(1)}, u32[]{:S(2)}, u32[]{:S(2)}) %collective-permute-start.5) | collective-permute-done | bytes 65568 | tf_op jit(solution)/shard_map/ppermute | solution.py:429
  20.3 1.1 %collective-permute-done.6.refs_2_ = f32[64,256]{1,0:T(8,128)S(1)} collective-permute-done((f32[64,256]{1,0:T(8,128)S(1)}, f32[64,256]{1,0:T(8,128)S(1)}, u32[]{:S(2)}, u32[]{:S(2)}) %collective-permute-start.6) | collective-permute-done | bytes 65568 | tf_op jit(solution)/shard_map/ppermute | solution.py:429
  21.4 1.7 %collective-permute-done.7.refs_3_ = f32[64,256]{1,0:T(8,128)S(1)} collective-permute-done((f32[64,256]{1,0:T(8,128)S(1)}, f32[64,256]{1,0:T(8,128)S(1)}, u32[]{:S(2)}, u32[]{:S(2)}) %collective-permute-start.7) | collective-permute-done | bytes 65568 | tf_op jit(solution)/shard_map/ppermute | solution.py:429
  23.7 1.6 %collective-permute-start.11 = (f32[256,256]{1,0:T(8,128)S(1)}, f32[256,256]{1,0:T(8,128)S(1)}, u32[]{:S(2)}, u32[]{:S(2)}) collective-permute-start(f32[256,256]{1,0:T(8,128)S(1)} %shard_map.182), channel_id=1, source_target_pairs={{0,2},{2,0},{1,3},{3,1},{6,4},{4,6},{7,5},{5,7},{12,14},{14,12},{1... | collective-permute-start | bytes 786440 | tf_op jit(solution)/shard_map/ppermute | solution.py:595
  25.6 2.4 %collective-permute-start.8 = (f32[256,256]{1,0:T(8,128)S(1)}, f32[256,256]{1,0:T(8,128)S(1)}, u32[]{:S(2)}, u32[]{:S(2)}) collective-permute-start(f32[256,256]{1,0:T(8,128)S(1)} %shard_map.179), channel_id=1, source_target_pairs={{2,6},{6,2},{3,7},{7,3},{4,12},{12,4},{5,13},{13,5},{14,10},{10,14... | collective-permute-start | bytes 786440 | tf_op jit(solution)/shard_map/ppermute | solution.py:593
  27.9 2.8 %collective-permute-done.11.behind = f32[256,256]{1,0:T(8,128)S(1)} collective-permute-done((f32[256,256]{1,0:T(8,128)S(1)}, f32[256,256]{1,0:T(8,128)S(1)}, u32[]{:S(2)}, u32[]{:S(2)}) %collective-permute-start.11) | collective-permute-done | bytes 262176 | tf_op jit(solution)/shard_map/ppermute | solution.py:595
  30.7 3.4 %collective-permute-done.8.ahead = f32[256,256]{1,0:T(8,128)S(1)} collective-permute-done((f32[256,256]{1,0:T(8,128)S(1)}, f32[256,256]{1,0:T(8,128)S(1)}, u32[]{:S(2)}, u32[]{:S(2)}) %collective-permute-start.8) | collective-permute-done | bytes 262176 | tf_op jit(solution)/shard_map/ppermute | solution.py:593
  34.8 0.6 collective-permute-start.15
  35.4 0.5 collective-permute-done.12.got
  35.8 0.7 %shard_map.184 = (f32[256,128]{1,0:T(8,128)S(1)}, f32[256,128]{1,0:T(8,128)S(1)}) custom-call(f32[256,128]{1,0:T(8,128)S(1)} %get-tuple-element.72.keep, f32[256,128]{1,0:T(8,128)S(1)} %collective-permute-done.12.got, f32[256,256]{1,0:T(8,128)S(1)} %get-tuple-element.57.mult, bf16[256,768]{1,0:T(8,128)(2,1)S(1)} %copy-done.3, ...), custom_call_target="tpu_custom_call" | custom-call | tf_op jit(solution)/shard_map/pallas_call | solution.py:541
  36.8 0.7 %shard_map.187 = (f32[256,128]{1,0:T(8,128)S(1)}, f32[256,128]{1,0:T(8,128)S(1)}) custom-call(f32[256,128]{1,0:T(8,128)S(1)} %get-tuple-element.76.keep, f32[256,128]{1,0:T(8,128)S(1)} %collective-permute-done.15.got, f32[256,256]{1,0:T(8,128)S(1)} %get-tuple-element.57.mult, bf16[256,768]{1,0:T(8,128)(2,1)S(1)} %copy-done.3, ...), custom_call_target="tpu_custom_call" | custom-call | tf_op jit(solution)/shard_map/pallas_call | solution.py:541
  37.6 0.4 collective-permute-start.16
  38.3 2.4 %collective-permute-start.14 = (f32[256,256]{1,0:T(8,128)S(1)}, f32[256,256]{1,0:T(8,128)S(1)}, u32[]{:S(2)}, u32[]{:S(2)}) collective-permute-start(f32[256,256]{1,0:T(8,128)S(1)} %shard_map.185), channel_id=1, source_target_pairs={{2,6},{6,2},{3,7},{7,3},{4,12},{12,4},{5,13},{13,5},{14,10},{10,14... | collective-permute-start | bytes 786440 | tf_op jit(solution)/shard_map/ppermute | solution.py:593
  41.0 1.3 %collective-permute-start.17 = (f32[256,256]{1,0:T(8,128)S(1)}, f32[256,256]{1,0:T(8,128)S(1)}, u32[]{:S(2)}, u32[]{:S(2)}) collective-permute-start(f32[256,256]{1,0:T(8,128)S(1)} %shard_map.188), channel_id=1, source_target_pairs={{0,2},{2,0},{1,3},{3,1},{6,4},{4,6},{7,5},{5,7},{12,14},{14,12},{1... | collective-permute-start | bytes 786440 | tf_op jit(solution)/shard_map/ppermute | solution.py:595
  42.4 6.2 %collective-permute-done.14.ahead = f32[256,256]{1,0:T(8,128)S(1)} collective-permute-done((f32[256,256]{1,0:T(8,128)S(1)}, f32[256,256]{1,0:T(8,128)S(1)}, u32[]{:S(2)}, u32[]{:S(2)}) %collective-permute-start.14) | collective-permute-done | bytes 262176 | tf_op jit(solution)/shard_map/ppermute | solution.py:593
  48.6 0.6 collective-permute-done.17.behind
  49.9 0.6 collective-permute-start.23
  50.5 0.5 collective-permute-done.18.got
  50.9 0.7 %shard_map.190 = (f32[256,128]{1,0:T(8,128)S(1)}, f32[256,128]{1,0:T(8,128)S(1)}) custom-call(f32[256,128]{1,0:T(8,128)S(1)} %get-tuple-element.80.keep, f32[256,128]{1,0:T(8,128)S(1)} %collective-permute-done.18.got, f32[256,256]{1,0:T(8,128)S(1)} %get-tuple-element.57.mult, bf16[256,768]{1,0:T(8,128)(2,1)S(1)} %copy-done.3, ...), custom_call_target="tpu_custom_call" | custom-call | tf_op jit(solution)/shard_map/pallas_call | solution.py:541
  51.9 0.7 %shard_map.193 = (f32[256,128]{1,0:T(8,128)S(1)}, f32[256,128]{1,0:T(8,128)S(1)}) custom-call(f32[256,128]{1,0:T(8,128)S(1)} %get-tuple-element.88.keep, f32[256,128]{1,0:T(8,128)S(1)} %collective-permute-done.23.got, f32[256,256]{1,0:T(8,128)S(1)} %get-tuple-element.57.mult, bf16[256,768]{1,0:T(8,128)(2,1)S(1)} %copy-done.3, ...), custom_call_target="tpu_custom_call" | custom-call | tf_op jit(solution)/shard_map/pallas_call | solution.py:541
  52.7 0.4 collective-permute-start.24
  53.1 0.3 shard_map.191
  53.4 1.3 %collective-permute-start.20 = (f32[64,256]{1,0:T(8,128)S(1)}, f32[64,256]{1,0:T(8,128)S(1)}, u32[]{:S(2)}, u32[]{:S(2)}) collective-permute-start(f32[64,256]{1,0:T(8,128)S(1)} %get-tuple-element.85), channel_id=1, source_target_pairs={{0,2},{1,3},{2,0},{3,1},{4,6},{5,7},{6,4},{7,5},{8,10},{9,11},{10,... | collective-permute-start | bytes 196616 | tf_op jit(solution)/shard_map/ppermute | solution.py:429
  54.8 0.9 %collective-permute-start.21 = (f32[64,256]{1,0:T(8,128)S(1)}, f32[64,256]{1,0:T(8,128)S(1)}, u32[]{:S(2)}, u32[]{:S(2)}) collective-permute-start(f32[64,256]{1,0:T(8,128)S(1)} %get-tuple-element.86), channel_id=1, source_target_pairs={{0,4},{1,5},{2,6},{3,7},{4,0},{5,1},{6,2},{7,3},{8,12},{9,13},{10,... | collective-permute-start | bytes 196616 | tf_op jit(solution)/shard_map/ppermute | solution.py:429
  55.7 1.3 %collective-permute-start.22 = (f32[64,256]{1,0:T(8,128)S(1)}, f32[64,256]{1,0:T(8,128)S(1)}, u32[]{:S(2)}, u32[]{:S(2)}) collective-permute-start(f32[64,256]{1,0:T(8,128)S(1)} %get-tuple-element.87), channel_id=1, source_target_pairs={{0,6},{1,7},{2,4},{3,5},{4,2},{5,3},{6,0},{7,1},{8,14},{9,15},{10,... | collective-permute-start | bytes 196616 | tf_op jit(solution)/shard_map/ppermute | solution.py:429
  57.0 0.3 shard_map.194
  57.4 1.3 %collective-permute-start.25 = (f32[64,256]{1,0:T(8,128)S(1)}, f32[64,256]{1,0:T(8,128)S(1)}, u32[]{:S(2)}, u32[]{:S(2)}) collective-permute-start(f32[64,256]{1,0:T(8,128)S(1)} %get-tuple-element.93), channel_id=1, source_target_pairs={{0,2},{1,3},{2,0},{3,1},{4,6},{5,7},{6,4},{7,5},{8,10},{9,11},{10,... | collective-permute-start | bytes 196616 | tf_op jit(solution)/shard_map/ppermute | solution.py:429
  58.7 0.9 %collective-permute-start.26 = (f32[64,256]{1,0:T(8,128)S(1)}, f32[64,256]{1,0:T(8,128)S(1)}, u32[]{:S(2)}, u32[]{:S(2)}) collective-permute-start(f32[64,256]{1,0:T(8,128)S(1)} %get-tuple-element.94), channel_id=1, source_target_pairs={{0,4},{1,5},{2,6},{3,7},{4,0},{5,1},{6,2},{7,3},{8,12},{9,13},{10,... | collective-permute-start | bytes 196616 | tf_op jit(solution)/shard_map/ppermute | solution.py:429
  59.6 1.3 %collective-permute-start.27 = (f32[64,256]{1,0:T(8,128)S(1)}, f32[64,256]{1,0:T(8,128)S(1)}, u32[]{:S(2)}, u32[]{:S(2)}) collective-permute-start(f32[64,256]{1,0:T(8,128)S(1)} %get-tuple-element.95), channel_id=1, source_target_pairs={{0,6},{1,7},{2,4},{3,5},{4,2},{5,3},{6,0},{7,1},{8,14},{9,15},{10,... | collective-permute-start | bytes 196616 | tf_op jit(solution)/shard_map/ppermute | solution.py:429
  61.3 1.4 %collective-permute-start.28 = (f32[64,256]{1,0:T(8,128)S(1)}, f32[64,256]{1,0:T(8,128)S(1)}, u32[]{:S(2)}, u32[]{:S(2)}) collective-permute-start(f32[64,256]{1,0:T(8,128)S(1)} %get-tuple-element.96), channel_id=1, source_target_pairs={{0,8},{8,0},{1,9},{9,1},{2,10},{10,2},{3,11},{11,3},{4,12},{12,4},... | collective-permute-start | bytes 196616 | tf_op jit(solution)/shard_map/ppermute | solution.py:620
  62.7 1.9 %collective-permute-start.29 = (f32[64,256]{1,0:T(8,128)S(1)}, f32[64,256]{1,0:T(8,128)S(1)}, u32[]{:S(2)}, u32[]{:S(2)}) collective-permute-start(f32[64,256]{1,0:T(8,128)S(1)} %get-tuple-element.97), channel_id=1, source_target_pairs={{8,16},{16,8},{9,17},{17,9},{10,18},{18,10},{11,19},{19,11},{12,20... | collective-permute-start | bytes 196616 | tf_op jit(solution)/shard_map/ppermute | solution.py:621
  64.8 0.9 %collective-permute-done.28.refs_8_ = f32[64,256]{1,0:T(8,128)S(1)} collective-permute-done((f32[64,256]{1,0:T(8,128)S(1)}, f32[64,256]{1,0:T(8,128)S(1)}, u32[]{:S(2)}, u32[]{:S(2)}) %collective-permute-start.28) | collective-permute-done | bytes 65568 | tf_op jit(solution)/shard_map/ppermute | solution.py:620
  65.6 3.2 %collective-permute-done.29.refs_9_ = f32[64,256]{1,0:T(8,128)S(1)} collective-permute-done((f32[64,256]{1,0:T(8,128)S(1)}, f32[64,256]{1,0:T(8,128)S(1)}, u32[]{:S(2)}, u32[]{:S(2)}) %collective-permute-start.29) | collective-permute-done | bytes 65568 | tf_op jit(solution)/shard_map/ppermute | solution.py:621
  68.8 1.0 %shard_map.196 = (f32[4,32,256]{2,1,0:T(8,128)}, f32[4,32,256]{2,1,0:T(8,128)}, f32[4,32,256]{2,1,0:T(8,128)}, f32[4,32,256]{2,1,0:T(8,128)}) custom-call(f32[64,256]{1,0:T(8,128)S(1)} %get-tuple-element.84.refs_0_, f32[64,256]{1,0:T(8,128)S(1)} %collective-permute-done.20.refs_1_, f32[64,256]{1,0:T(8,128)S(1)} %collective-permute-done.21.refs_2_, ...), custom_call_target="tpu_custom_call" | custom-call | tf_op jit(solution)/shard_map/pallas_call | solution.py:667
  (55 shorter events, 4.7 us)
Async XLA Ops:
  0.6 10.7 %copy-start.1 = (bf16[768,256]{1,0:T(8,128)(2,1)S(1)}, bf16[768,256]{1,0:T(8,128)(2,1)}, u32[]{:S(2)}) copy-start(bf16[768,256]{1,0:T(8,128)(2,1)} %constant.12.clone.refs_4_.table) | copy-start | bytes 1179652
  2.0 5.7 %collective-permute-start = (f32[128,256]{1,0:T(8,128)S(1)}, f32[128,256]{1,0:T(8,128)S(1)}, u32[]{:S(2)}, u32[]{:S(2)}) collective-permute-start(f32[128,256]{1,0:T(8,128)S(1)} %get-tuple-element.52), channel_id=1, source_target_pairs={{0,2},{1,3},{2,0},{3,1},{4,6},{5,7},{6,4},{7,5},{8,10},{9,11},{10,... | collective-permute-start | bytes 393224 | tf_op jit(solution)/shard_map/ppermute | solution.py:429
  3.6 7.8 %collective-permute-start.1 = (f32[128,256]{1,0:T(8,128)S(1)}, f32[128,256]{1,0:T(8,128)S(1)}, u32[]{:S(2)}, u32[]{:S(2)}) collective-permute-start(f32[128,256]{1,0:T(8,128)S(1)} %get-tuple-element.53), channel_id=1, source_target_pairs={{0,4},{1,5},{2,6},{3,7},{4,0},{5,1},{6,2},{7,3},{8,12},{9,13},{10,... | collective-permute-start | bytes 393224 | tf_op jit(solution)/shard_map/ppermute | solution.py:429
  5.1 6.3 %copy-start.6 = (f32[2,128]{1,0:T(2,128)S(1)}, f32[2,128]{1,0:T(2,128)}, u32[]{:S(2)}) copy-start(f32[2,128]{1,0:T(2,128)} %constant.16.clone.refs_5_.turn) | copy-start | bytes 3076
  5.1 6.3 %collective-permute-start.2 = (f32[128,256]{1,0:T(8,128)S(1)}, f32[128,256]{1,0:T(8,128)S(1)}, u32[]{:S(2)}, u32[]{:S(2)}) collective-permute-start(f32[128,256]{1,0:T(8,128)S(1)} %get-tuple-element.54), channel_id=1, source_target_pairs={{0,6},{1,7},{2,4},{3,5},{4,2},{5,3},{6,0},{7,1},{8,14},{9,15},{10,... | collective-permute-start | bytes 393224 | tf_op jit(solution)/shard_map/ppermute | solution.py:429
  11.7 2.0 %copy-start.2 = (bf16[256,768]{1,0:T(8,128)(2,1)S(1)}, bf16[256,768]{1,0:T(8,128)(2,1)}, u32[]{:S(2)}) copy-start(bf16[256,768]{1,0:T(8,128)(2,1)} %constant.15.clone.back) | copy-start | bytes 1179652
  11.7 2.0 %copy-start.3 = (bf16[256,768]{1,0:T(8,128)(2,1)S(1)}, bf16[256,768]{1,0:T(8,128)(2,1)}, u32[]{:S(2)}) copy-start(bf16[256,768]{1,0:T(8,128)(2,1)} %constant.14.clone.table) | copy-start | bytes 1179652
  11.7 2.0 %copy-start.4 = (f32[2,128,128]{2,1,0:T(8,128)S(1)}, f32[2,128,128]{2,1,0:T(8,128)}, u32[]{:S(2)}) copy-start(f32[2,128,128]{2,1,0:T(8,128)} %constant.17.clone.turn) | copy-start | bytes 393220
  11.7 1.9 %collective-permute-start.9 = (f32[256,128]{1,0:T(8,128)S(1)}, f32[256,128]{1,0:T(8,128)S(1)}, u32[]{:S(2)}, u32[]{:S(2)}) collective-permute-start(f32[256,128]{1,0:T(8,128)S(1)} %get-tuple-element.67), channel_id=1, source_target_pairs={{0,1},{1,0},{2,3},{3,2},{4,5},{5,4},{6,7},{7,6},{8,9},{9,8},{10,11... | collective-permute-start | bytes 393224 | tf_op jit(solution)/shard_map/ppermute | solution.py:581
  12.1 0.7 copy-start.9
  12.1 2.9 %collective-permute-start.3 = (f32[256,128]{1,0:T(8,128)S(1)}, f32[256,128]{1,0:T(8,128)S(1)}, u32[]{:S(2)}, u32[]{:S(2)}) collective-permute-start(f32[256,128]{1,0:T(8,128)S(1)} %get-tuple-element.56), channel_id=1, source_target_pairs={{0,1},{1,0},{2,3},{3,2},{4,5},{5,4},{6,7},{7,6},{8,9},{9,8},{10,11... | collective-permute-start | bytes 393224 | tf_op jit(solution)/shard_map/ppermute | solution.py:581
  14.4 8.9 %collective-permute-start.10 = (f32[256,128]{1,0:T(8,128)S(1)}, f32[256,128]{1,0:T(8,128)S(1)}, u32[]{:S(2)}, u32[]{:S(2)}) collective-permute-start(f32[256,128]{1,0:T(8,128)S(1)} %get-tuple-element.69), channel_id=1, source_target_pairs={{0,1},{1,0},{2,3},{3,2},{4,5},{5,4},{6,7},{7,6},{8,9},{9,8},{10,11... | collective-permute-start | bytes 393224 | tf_op jit(solution)/shard_map/ppermute | solution.py:581
  15.0 8.3 %copy-start = (bf16[768,256]{1,0:T(8,128)(2,1)S(1)}, bf16[768,256]{1,0:T(8,128)(2,1)}, u32[]{:S(2)}) copy-start(bf16[768,256]{1,0:T(8,128)(2,1)} %constant.13.clone.table) | copy-start | bytes 1179652
  15.8 9.5 %collective-permute-start.4 = (f32[256,128]{1,0:T(8,128)S(1)}, f32[256,128]{1,0:T(8,128)S(1)}, u32[]{:S(2)}, u32[]{:S(2)}) collective-permute-start(f32[256,128]{1,0:T(8,128)S(1)} %get-tuple-element.59), channel_id=1, source_target_pairs={{0,1},{1,0},{2,3},{3,2},{4,5},{5,4},{6,7},{7,6},{8,9},{9,8},{10,11... | collective-permute-start | bytes 393224 | tf_op jit(solution)/shard_map/ppermute | solution.py:581
  15.9 4.5 %collective-permute-start.5 = (f32[64,256]{1,0:T(8,128)S(1)}, f32[64,256]{1,0:T(8,128)S(1)}, u32[]{:S(2)}, u32[]{:S(2)}) collective-permute-start(f32[64,256]{1,0:T(8,128)S(1)} %get-tuple-element.61), channel_id=1, source_target_pairs={{0,2},{1,3},{2,0},{3,1},{4,6},{5,7},{6,4},{7,5},{8,10},{9,11},{10,... | collective-permute-start | bytes 196616 | tf_op jit(solution)/shard_map/ppermute | solution.py:429
  17.1 4.3 %collective-permute-start.6 = (f32[64,256]{1,0:T(8,128)S(1)}, f32[64,256]{1,0:T(8,128)S(1)}, u32[]{:S(2)}, u32[]{:S(2)}) collective-permute-start(f32[64,256]{1,0:T(8,128)S(1)} %get-tuple-element.62), channel_id=1, source_target_pairs={{0,4},{1,5},{2,6},{3,7},{4,0},{5,1},{6,2},{7,3},{8,12},{9,13},{10,... | collective-permute-start | bytes 196616 | tf_op jit(solution)/shard_map/ppermute | solution.py:429
  18.0 5.2 %collective-permute-start.7 = (f32[64,256]{1,0:T(8,128)S(1)}, f32[64,256]{1,0:T(8,128)S(1)}, u32[]{:S(2)}, u32[]{:S(2)}) collective-permute-start(f32[64,256]{1,0:T(8,128)S(1)} %get-tuple-element.63), channel_id=1, source_target_pairs={{0,6},{1,7},{2,4},{3,5},{4,2},{5,3},{6,0},{7,1},{8,14},{9,15},{10,... | collective-permute-start | bytes 196616 | tf_op jit(solution)/shard_map/ppermute | solution.py:429
  23.7 7.1 %collective-permute-start.11 = (f32[256,256]{1,0:T(8,128)S(1)}, f32[256,256]{1,0:T(8,128)S(1)}, u32[]{:S(2)}, u32[]{:S(2)}) collective-permute-start(f32[256,256]{1,0:T(8,128)S(1)} %shard_map.182), channel_id=1, source_target_pairs={{0,2},{2,0},{1,3},{3,1},{6,4},{4,6},{7,5},{5,7},{12,14},{14,12},{1... | collective-permute-start | bytes 786440 | tf_op jit(solution)/shard_map/ppermute | solution.py:595
  25.6 8.5 %collective-permute-start.8 = (f32[256,256]{1,0:T(8,128)S(1)}, f32[256,256]{1,0:T(8,128)S(1)}, u32[]{:S(2)}, u32[]{:S(2)}) collective-permute-start(f32[256,256]{1,0:T(8,128)S(1)} %shard_map.179), channel_id=1, source_target_pairs={{2,6},{6,2},{3,7},{7,3},{4,12},{12,4},{5,13},{13,5},{14,10},{10,14... | collective-permute-start | bytes 786440 | tf_op jit(solution)/shard_map/ppermute | solution.py:593
  34.4 1.4 %collective-permute-start.12 = (f32[256,128]{1,0:T(8,128)S(1)}, f32[256,128]{1,0:T(8,128)S(1)}, u32[]{:S(2)}, u32[]{:S(2)}) collective-permute-start(f32[256,128]{1,0:T(8,128)S(1)} %get-tuple-element.73), channel_id=1, source_target_pairs={{0,1},{1,0},{2,3},{3,2},{4,5},{5,4},{6,7},{7,6},{8,9},{9,8},{10,11... | collective-permute-start | bytes 393224 | tf_op jit(solution)/shard_map/ppermute | solution.py:581
  34.8 2.0 %collective-permute-start.15 = (f32[256,128]{1,0:T(8,128)S(1)}, f32[256,128]{1,0:T(8,128)S(1)}, u32[]{:S(2)}, u32[]{:S(2)}) collective-permute-start(f32[256,128]{1,0:T(8,128)S(1)} %get-tuple-element.77), channel_id=1, source_target_pairs={{0,1},{1,0},{2,3},{3,2},{4,5},{5,4},{6,7},{7,6},{8,9},{9,8},{10,11... | collective-permute-start | bytes 393224 | tf_op jit(solution)/shard_map/ppermute | solution.py:581
  36.6 1.4 %collective-permute-start.13 = (f32[256,128]{1,0:T(8,128)S(1)}, f32[256,128]{1,0:T(8,128)S(1)}, u32[]{:S(2)}, u32[]{:S(2)}) collective-permute-start(f32[256,128]{1,0:T(8,128)S(1)} %get-tuple-element.75), channel_id=1, source_target_pairs={{0,1},{1,0},{2,3},{3,2},{4,5},{5,4},{6,7},{7,6},{8,9},{9,8},{10,11... | collective-permute-start | bytes 393224 | tf_op jit(solution)/shard_map/ppermute | solution.py:581
  37.6 3.1 %collective-permute-start.16 = (f32[256,128]{1,0:T(8,128)S(1)}, f32[256,128]{1,0:T(8,128)S(1)}, u32[]{:S(2)}, u32[]{:S(2)}) collective-permute-start(f32[256,128]{1,0:T(8,128)S(1)} %get-tuple-element.79), channel_id=1, source_target_pairs={{0,1},{1,0},{2,3},{3,2},{4,5},{5,4},{6,7},{7,6},{8,9},{9,8},{10,11... | collective-permute-start | bytes 393224 | tf_op jit(solution)/shard_map/ppermute | solution.py:581
  38.3 10.3 %collective-permute-start.14 = (f32[256,256]{1,0:T(8,128)S(1)}, f32[256,256]{1,0:T(8,128)S(1)}, u32[]{:S(2)}, u32[]{:S(2)}) collective-permute-start(f32[256,256]{1,0:T(8,128)S(1)} %shard_map.185), channel_id=1, source_target_pairs={{2,6},{6,2},{3,7},{7,3},{4,12},{12,4},{5,13},{13,5},{14,10},{10,14... | collective-permute-start | bytes 786440 | tf_op jit(solution)/shard_map/ppermute | solution.py:593
  41.0 8.2 %collective-permute-start.17 = (f32[256,256]{1,0:T(8,128)S(1)}, f32[256,256]{1,0:T(8,128)S(1)}, u32[]{:S(2)}, u32[]{:S(2)}) collective-permute-start(f32[256,256]{1,0:T(8,128)S(1)} %shard_map.188), channel_id=1, source_target_pairs={{0,2},{2,0},{1,3},{3,1},{6,4},{4,6},{7,5},{5,7},{12,14},{14,12},{1... | collective-permute-start | bytes 786440 | tf_op jit(solution)/shard_map/ppermute | solution.py:595
  49.5 1.4 %collective-permute-start.18 = (f32[256,128]{1,0:T(8,128)S(1)}, f32[256,128]{1,0:T(8,128)S(1)}, u32[]{:S(2)}, u32[]{:S(2)}) collective-permute-start(f32[256,128]{1,0:T(8,128)S(1)} %get-tuple-element.81), channel_id=1, source_target_pairs={{0,1},{1,0},{2,3},{3,2},{4,5},{5,4},{6,7},{7,6},{8,9},{9,8},{10,11... | collective-permute-start | bytes 393224 | tf_op jit(solution)/shard_map/ppermute | solution.py:581
  49.9 2.0 %collective-permute-start.23 = (f32[256,128]{1,0:T(8,128)S(1)}, f32[256,128]{1,0:T(8,128)S(1)}, u32[]{:S(2)}, u32[]{:S(2)}) collective-permute-start(f32[256,128]{1,0:T(8,128)S(1)} %get-tuple-element.89), channel_id=1, source_target_pairs={{0,1},{1,0},{2,3},{3,2},{4,5},{5,4},{6,7},{7,6},{8,9},{9,8},{10,11... | collective-permute-start | bytes 393224 | tf_op jit(solution)/shard_map/ppermute | solution.py:581
  51.7 1.4 %collective-permute-start.19 = (f32[256,128]{1,0:T(8,128)S(1)}, f32[256,128]{1,0:T(8,128)S(1)}, u32[]{:S(2)}, u32[]{:S(2)}) collective-permute-start(f32[256,128]{1,0:T(8,128)S(1)} %get-tuple-element.83), channel_id=1, source_target_pairs={{0,1},{1,0},{2,3},{3,2},{4,5},{5,4},{6,7},{7,6},{8,9},{9,8},{10,11... | collective-permute-start | bytes 393224 | tf_op jit(solution)/shard_map/ppermute | solution.py:581
  52.7 4.3 %collective-permute-start.24 = (f32[256,128]{1,0:T(8,128)S(1)}, f32[256,128]{1,0:T(8,128)S(1)}, u32[]{:S(2)}, u32[]{:S(2)}) collective-permute-start(f32[256,128]{1,0:T(8,128)S(1)} %get-tuple-element.91), channel_id=1, source_target_pairs={{0,1},{1,0},{2,3},{3,2},{4,5},{5,4},{6,7},{7,6},{8,9},{9,8},{10,11... | collective-permute-start | bytes 393224 | tf_op jit(solution)/shard_map/ppermute | solution.py:581
  53.4 6.2 %collective-permute-start.20 = (f32[64,256]{1,0:T(8,128)S(1)}, f32[64,256]{1,0:T(8,128)S(1)}, u32[]{:S(2)}, u32[]{:S(2)}) collective-permute-start(f32[64,256]{1,0:T(8,128)S(1)} %get-tuple-element.85), channel_id=1, source_target_pairs={{0,2},{1,3},{2,0},{3,1},{4,6},{5,7},{6,4},{7,5},{8,10},{9,11},{10,... | collective-permute-start | bytes 196616 | tf_op jit(solution)/shard_map/ppermute | solution.py:429
  54.8 6.1 %collective-permute-start.21 = (f32[64,256]{1,0:T(8,128)S(1)}, f32[64,256]{1,0:T(8,128)S(1)}, u32[]{:S(2)}, u32[]{:S(2)}) collective-permute-start(f32[64,256]{1,0:T(8,128)S(1)} %get-tuple-element.86), channel_id=1, source_target_pairs={{0,4},{1,5},{2,6},{3,7},{4,0},{5,1},{6,2},{7,3},{8,12},{9,13},{10,... | collective-permute-start | bytes 196616 | tf_op jit(solution)/shard_map/ppermute | solution.py:429
  55.7 5.5 %collective-permute-start.22 = (f32[64,256]{1,0:T(8,128)S(1)}, f32[64,256]{1,0:T(8,128)S(1)}, u32[]{:S(2)}, u32[]{:S(2)}) collective-permute-start(f32[64,256]{1,0:T(8,128)S(1)} %get-tuple-element.87), channel_id=1, source_target_pairs={{0,6},{1,7},{2,4},{3,5},{4,2},{5,3},{6,0},{7,1},{8,14},{9,15},{10,... | collective-permute-start | bytes 196616 | tf_op jit(solution)/shard_map/ppermute | solution.py:429
  57.4 7.3 %collective-permute-start.25 = (f32[64,256]{1,0:T(8,128)S(1)}, f32[64,256]{1,0:T(8,128)S(1)}, u32[]{:S(2)}, u32[]{:S(2)}) collective-permute-start(f32[64,256]{1,0:T(8,128)S(1)} %get-tuple-element.93), channel_id=1, source_target_pairs={{0,2},{1,3},{2,0},{3,1},{4,6},{5,7},{6,4},{7,5},{8,10},{9,11},{10,... | collective-permute-start | bytes 196616 | tf_op jit(solution)/shard_map/ppermute | solution.py:429
  58.7 6.0 %collective-permute-start.26 = (f32[64,256]{1,0:T(8,128)S(1)}, f32[64,256]{1,0:T(8,128)S(1)}, u32[]{:S(2)}, u32[]{:S(2)}) collective-permute-start(f32[64,256]{1,0:T(8,128)S(1)} %get-tuple-element.94), channel_id=1, source_target_pairs={{0,4},{1,5},{2,6},{3,7},{4,0},{5,1},{6,2},{7,3},{8,12},{9,13},{10,... | collective-permute-start | bytes 196616 | tf_op jit(solution)/shard_map/ppermute | solution.py:429
  59.6 5.2 %collective-permute-start.27 = (f32[64,256]{1,0:T(8,128)S(1)}, f32[64,256]{1,0:T(8,128)S(1)}, u32[]{:S(2)}, u32[]{:S(2)}) collective-permute-start(f32[64,256]{1,0:T(8,128)S(1)} %get-tuple-element.95), channel_id=1, source_target_pairs={{0,6},{1,7},{2,4},{3,5},{4,2},{5,3},{6,0},{7,1},{8,14},{9,15},{10,... | collective-permute-start | bytes 196616 | tf_op jit(solution)/shard_map/ppermute | solution.py:429
  61.2 7.6 %copy-start.5 = (f32[4,32,256]{2,1,0:T(8,128)S(1)}, f32[4,32,256]{2,1,0:T(8,128)}, u32[]{:S(2)}) copy-start(f32[4,32,256]{2,1,0:T(8,128)} %refs_10_.1) | copy-start | bytes 393220
  61.2 7.6 %copy-start.7 = (f32[32,256]{1,0:T(8,128)S(1)}, f32[32,256]{1,0:T(8,128)}, u32[]{:S(2)}) copy-start(f32[32,256]{1,0:T(8,128)} %refs_11_.1) | copy-start | bytes 98308
  61.2 7.6 %copy-start.8 = (f32[32,256]{1,0:T(8,128)S(1)}, f32[32,256]{1,0:T(8,128)}, u32[]{:S(2)}) copy-start(f32[32,256]{1,0:T(8,128)} %refs_12_.1) | copy-start | bytes 98308
  61.3 4.3 %collective-permute-start.28 = (f32[64,256]{1,0:T(8,128)S(1)}, f32[64,256]{1,0:T(8,128)S(1)}, u32[]{:S(2)}, u32[]{:S(2)}) collective-permute-start(f32[64,256]{1,0:T(8,128)S(1)} %get-tuple-element.96), channel_id=1, source_target_pairs={{0,8},{8,0},{1,9},{9,1},{2,10},{10,2},{3,11},{11,3},{4,12},{12,4},... | collective-permute-start | bytes 196616 | tf_op jit(solution)/shard_map/ppermute | solution.py:620
  62.7 6.1 %collective-permute-start.29 = (f32[64,256]{1,0:T(8,128)S(1)}, f32[64,256]{1,0:T(8,128)S(1)}, u32[]{:S(2)}, u32[]{:S(2)}) collective-permute-start(f32[64,256]{1,0:T(8,128)S(1)} %get-tuple-element.97), channel_id=1, source_target_pairs={{8,16},{16,8},{9,17},{17,9},{10,18},{18,10},{11,19},{19,11},{12,20... | collective-permute-start | bytes 196616 | tf_op jit(solution)/shard_map/ppermute | solution.py:621
